TPU v7x, 32 devices: a whole 2x2x4 slice. The times are simulated.
32 devices in a mesh: rep: 4 (over x, core), dp: 2 (over y), ctx: 4 (over z).
Axes of the slice: x: 2, y: 2, z: 4, core: 2. Of those that a mesh axis runs over, the one named last changes fastest.
Arguments:
- hidden_in: bfloat16 [16, 1024, 1600], P(('rep', 'dp'), 'ctx'), may hold values from -6 to 6
- piece_starts: int32 [16, 2], P(('rep', 'dp')), may hold values from 0 to 768, as said below
- grad_out: bfloat16 [16, 1024, 1600], P(('rep', 'dp'), 'ctx'), may hold values from -6 to 6
- attn_gain: bfloat16 [1600], P(('dp', 'ctx')), may hold values from 0.099609375 to 1.8984375
- attn_shift: bfloat16 [1600], P(('dp', 'ctx')), may hold values from -2 to 2
- qkv_weight: bfloat16 [1600, 4800], P(('dp', 'ctx')), may hold values from -0.15625 to 0.15625
- qv_bias: bfloat16 [3200], P(('dp', 'ctx')), may hold values from -2 to 2
- out_weight: bfloat16 [1600, 1600], P(('dp', 'ctx')), may hold values from -0.625 to 0.625
- out_bias: bfloat16 [1600], P(('dp', 'ctx')), may hold values from -2 to 2
- mlp_gain: bfloat16 [1600], P(('dp', 'ctx')), may hold values from 0.099609375 to 1.8984375
- mlp_shift: bfloat16 [1600], P(('dp', 'ctx')), may hold values from -2 to 2
- fc_weight: bfloat16 [1600, 6400], P(('dp', 'ctx')), may hold values from -0.15625 to 0.15625
- fc_bias: bfloat16 [6400], P(('dp', 'ctx')), may hold values from -2 to 2
- proj_weight: bfloat16 [6400, 1600], P(('dp', 'ctx')), may hold values from -0.078125 to 0.078125
- proj_bias: bfloat16 [1600], P(('dp', 'ctx')), may hold values from -2 to 2
Outputs:
- block_out: bfloat16 [16, 1024, 1600], P(('rep', 'dp'), 'ctx')
- grad_input: float32 [16, 1024, 1600], P(('rep', 'dp'), 'ctx')
- grad_attn_gain: float32 [1600], P(('dp', 'ctx'))
- grad_attn_shift: float32 [1600], P(('dp', 'ctx'))
- grad_qkv_weight: float32 [1600, 4800], P(('dp', 'ctx'))
- grad_qv_bias: float32 [3200], P(('dp', 'ctx'))
- grad_out_weight: float32 [1600, 1600], P(('dp', 'ctx'))
- grad_out_bias: float32 [1600], P(('dp', 'ctx'))
- grad_mlp_gain: float32 [1600], P(('dp', 'ctx'))
- grad_mlp_shift: float32 [1600], P(('dp', 'ctx'))
- grad_fc_weight: float32 [1600, 6400], P(('dp', 'ctx'))
- grad_fc_bias: float32 [6400], P(('dp', 'ctx'))
- grad_proj_weight: float32 [6400, 1600], P(('dp', 'ctx'))
- grad_proj_bias: float32 [1600], P(('dp', 'ctx'))
Inputs may be any that keep to these rules, and one draw needn't show every extreme that they name: `piece_starts`: each entry is the first position of a bidirectional piece of its sequence, a multiple of 128; pieces of one sequence may intersect.
All inputs are finite; a program needn't handle non-finite values.
Results may differ from a plain program's by a relative error of at most 0.017.
Values may be sent and summed in bfloat16 or wider, within the bound.
No kernel may reach another device: no remote copies, remote signals or barrier semaphores. Data moves between devices by JAX's collectives and lax.ppermute only.
A program may use at most 576 MiB of HBM per device.

v0:
```python
import jax
import jax.numpy as jnp
from jax import lax
from jax.sharding import PartitionSpec as P

D = 1600
HEADS = 25
HD = 64
FF = 6400
SEQ = 1024
PIECE = 256


EPSILON = 1e-05
MASKED = -1000000000.0
gelu_coeff = 0.7978845608028654
gelu_cubic = 0.044715


def layer_norm(values, gain, shift):
    center = values - jnp.mean(values, axis=-1, keepdims=True)
    inv_std = lax.rsqrt(jnp.mean(center * center, axis=-1, keepdims=True) + EPSILON)
    normed = center * inv_std
    return (normed * gain + shift, normed, inv_std)


def norm_back(upstream, normed, inv_std, gain):
    scaled = upstream * gain
    inner = (
        scaled
        - jnp.mean(scaled, axis=-1, keepdims=True)
        - normed * jnp.mean(scaled * normed, axis=-1, keepdims=True)
    )
    return (inner * inv_std, jnp.sum(upstream * normed, axis=0), jnp.sum(upstream, axis=0))


def gelu_both(values):
    tanh_value = jnp.tanh(gelu_coeff * (values + gelu_cubic * values * values * values))
    result = 0.5 * values * (1.0 + tanh_value)
    slope = 0.5 * (1.0 + tanh_value) + 0.5 * values * (
        1.0 - tanh_value * tanh_value
    ) * gelu_coeff * (1.0 + 3.0 * gelu_cubic * values * values)
    return (result, slope)


def visible(starts, row_pos, key_pos):
    row_in = (
        (row_pos[:, None] >= starts[None, :]) & (row_pos[:, None] < starts[None, :] + PIECE)
    ).astype(jnp.float32)
    key_in = (
        (key_pos[:, None] >= starts[None, :]) & (key_pos[:, None] < starts[None, :] + PIECE)
    ).astype(jnp.float32)
    shared = jnp.dot(row_in, key_in.T, preferred_element_type=jnp.float32) > 0.5
    return (key_pos[None, :] <= row_pos[:, None]) | shared


def head_scores(query_heads, keys_heads, allowed):
    scores = jnp.einsum(
        "thd,shd->hts", query_heads, keys_heads, preferred_element_type=jnp.float32
    ) * HD ** (-0.5)
    return jnp.where(allowed[None], scores, MASKED)


def local(
    hidden_in,
    piece_starts,
    grad_out,
    attn_gain,
    attn_shift,
    qkv_weight,
    qv_bias,
    out_weight,
    out_bias,
    mlp_gain,
    mlp_shift,
    fc_weight,
    fc_bias,
    proj_weight,
    proj_bias,
):
    row_count = hidden_in.shape[1]
    shard_rows = attn_gain.shape[0]
    row_pos = lax.axis_index("ctx") * row_count + jnp.arange(row_count, dtype=jnp.int32)
    key_pos = jnp.arange(SEQ, dtype=jnp.int32)
    scale = HD ** (-0.5)
    attn_shards = (attn_gain, attn_shift, qkv_weight, qv_bias, out_weight, out_bias)
    mlp_shards = (mlp_gain, mlp_shift, fc_weight, fc_bias, proj_weight, proj_bias)
    outputs = []
    input_grads = []
    kept_rows = []
    norm_totals = [jnp.zeros((D,), jnp.float32) for index in range(4)]
    for micro_index in range(hidden_in.shape[0]):
        attn_full = (
            lax.all_gather(attn_shards[0], ("dp", "ctx"), axis=0, tiled=True),
            lax.all_gather(attn_shards[1], ("dp", "ctx"), axis=0, tiled=True),
            lax.all_gather(attn_shards[2], ("dp", "ctx"), axis=0, tiled=True),
            lax.all_gather(attn_shards[3], ("dp", "ctx"), axis=0, tiled=True),
            lax.all_gather(attn_shards[4], ("dp", "ctx"), axis=0, tiled=True),
            lax.all_gather(attn_shards[5], ("dp", "ctx"), axis=0, tiled=True),
        )
        mlp_full = (
            lax.all_gather(mlp_shards[0], ("dp", "ctx"), axis=0, tiled=True),
            lax.all_gather(mlp_shards[1], ("dp", "ctx"), axis=0, tiled=True),
            lax.all_gather(mlp_shards[2], ("dp", "ctx"), axis=0, tiled=True),
            lax.all_gather(mlp_shards[3], ("dp", "ctx"), axis=0, tiled=True),
            lax.all_gather(mlp_shards[4], ("dp", "ctx"), axis=0, tiled=True),
            lax.all_gather(mlp_shards[5], ("dp", "ctx"), axis=0, tiled=True),
        )
        gain_one, shift_one, qkv_full, qv_full, out_full, out_bias_full = attn_full
        gain_two, shift_two, fc_full, fc_bias_full, proj_full, proj_bias_full = mlp_full
        tokens = hidden_in[micro_index].astype(jnp.float32)
        starts = piece_starts[micro_index]
        allowed = visible(starts, row_pos, key_pos)
        normed_out, normed_one, inv_one = layer_norm(
            tokens, gain_one.astype(jnp.float32), shift_one.astype(jnp.float32)
        )
        h1_low = normed_out.astype(jnp.bfloat16)
        qv_float = qv_full.astype(jnp.float32)
        full_bias = jnp.concatenate([qv_float[:D], jnp.zeros((D,), jnp.float32), qv_float[D:]])
        qkv_low = (
            jnp.dot(h1_low, qkv_full, preferred_element_type=jnp.float32) + full_bias
        ).astype(jnp.bfloat16)
        query_low = qkv_low[:, :D]
        keys_all, values_all = (
            lax.all_gather(qkv_low[:, D : 2 * D], "ctx", axis=0, tiled=True),
            lax.all_gather(qkv_low[:, 2 * D :], "ctx", axis=0, tiled=True),
        )
        query_heads = query_low.reshape(row_count, HEADS, HD)
        keys_heads = keys_all.reshape(SEQ, HEADS, HD)
        values_heads = values_all.reshape(SEQ, HEADS, HD)
        scores = head_scores(query_heads, keys_heads, allowed)
        top_score = jnp.max(scores, axis=-1, keepdims=True)
        expo = jnp.exp(scores - top_score)
        expo_sum = jnp.sum(expo, axis=-1, keepdims=True)
        probs_low = (expo / expo_sum).astype(jnp.bfloat16)
        log_total = top_score + jnp.log(expo_sum)
        mixed = jnp.einsum(
            "hts,shd->thd", probs_low, values_heads, preferred_element_type=jnp.float32
        )
        attn_low = mixed.reshape(row_count, D).astype(jnp.bfloat16)
        after_attn = (
            tokens
            + jnp.dot(attn_low, out_full, preferred_element_type=jnp.float32)
            + out_bias_full.astype(jnp.float32)
        )
        normed_out_two, normed_two, inv_two = layer_norm(
            after_attn, gain_two.astype(jnp.float32), shift_two.astype(jnp.float32)
        )
        h2_low = normed_out_two.astype(jnp.bfloat16)
        hidden_pre = jnp.dot(
            h2_low, fc_full, preferred_element_type=jnp.float32
        ) + fc_bias_full.astype(jnp.float32)
        hidden_act, hidden_slope = gelu_both(hidden_pre)
        act_low = hidden_act.astype(jnp.bfloat16)
        block_value = (
            after_attn
            + jnp.dot(act_low, proj_full, preferred_element_type=jnp.float32)
            + proj_bias_full.astype(jnp.float32)
        )
        outputs.append(block_value.astype(jnp.bfloat16))
        gain_two_back, fc_back, proj_back = (
            lax.all_gather(mlp_gain, ("dp", "ctx"), axis=0, tiled=True),
            lax.all_gather(fc_weight, ("dp", "ctx"), axis=0, tiled=True),
            lax.all_gather(proj_weight, ("dp", "ctx"), axis=0, tiled=True),
        )
        gain_one_back, qkv_back, out_back = (
            lax.all_gather(attn_gain, ("dp", "ctx"), axis=0, tiled=True),
            lax.all_gather(qkv_weight, ("dp", "ctx"), axis=0, tiled=True),
            lax.all_gather(out_weight, ("dp", "ctx"), axis=0, tiled=True),
        )
        cot_low = grad_out[micro_index]
        grad_act = jnp.einsum("td,fd->tf", cot_low, proj_back, preferred_element_type=jnp.float32)
        grad_pre_low = (grad_act * hidden_slope).astype(jnp.bfloat16)
        grad_h2 = jnp.einsum("tf,df->td", grad_pre_low, fc_back, preferred_element_type=jnp.float32)
        grad_through, grad_gain_two, grad_shift_two = norm_back(
            grad_h2, normed_two, inv_two, gain_two_back.astype(jnp.float32)
        )
        grad_after = grad_through + cot_low.astype(jnp.float32)
        grad_after_low = grad_after.astype(jnp.bfloat16)
        grad_attn_low = jnp.einsum(
            "te,de->td", grad_after_low, out_back, preferred_element_type=jnp.float32
        ).astype(jnp.bfloat16)
        grad_attn_heads = grad_attn_low.reshape(row_count, HEADS, HD)
        again_scores = head_scores(query_heads, keys_heads, allowed)
        probs = jnp.exp(again_scores - log_total)
        probs_again = probs.astype(jnp.bfloat16)
        grad_probs = jnp.einsum(
            "thd,shd->hts", grad_attn_heads, values_heads, preferred_element_type=jnp.float32
        )
        grad_scores_low = (
            probs * (grad_probs - jnp.sum(probs * grad_probs, axis=-1, keepdims=True))
        ).astype(jnp.bfloat16)
        grad_query = (
            jnp.einsum(
                "hts,shd->thd", grad_scores_low, keys_heads, preferred_element_type=jnp.float32
            )
            * scale
        )

        def key_value_term(
            start,
            count,
            grad_scores_low=grad_scores_low,
            probs_again=probs_again,
            query_heads=query_heads,
            grad_attn_heads=grad_attn_heads,
        ):
            grad_k = (
                jnp.einsum(
                    "hts,thd->shd", grad_scores_low, query_heads, preferred_element_type=jnp.float32
                )
                * scale
            )
            grad_v = jnp.einsum(
                "hts,thd->shd", probs_again, grad_attn_heads, preferred_element_type=jnp.float32
            )
            return jnp.concatenate([grad_k.reshape(count, D), grad_v.reshape(count, D)], axis=1)

        kv_summed = lax.psum_scatter(
            key_value_term(jnp.int32(0), lax.axis_size("ctx") * row_count).astype(jnp.bfloat16),
            "ctx",
            scatter_dimension=0,
            tiled=True,
        ).astype(jnp.float32)
        grad_qkv_low = jnp.concatenate(
            [grad_query.reshape(row_count, D), kv_summed], axis=1
        ).astype(jnp.bfloat16)
        grad_h1 = jnp.einsum(
            "te,de->td", grad_qkv_low, qkv_back, preferred_element_type=jnp.float32
        )
        grad_into, grad_gain_one, grad_shift_one = norm_back(
            grad_h1, normed_one, inv_one, gain_one_back.astype(jnp.float32)
        )
        input_grads.append(grad_after + grad_into)
        kept_rows.append(
            (h1_low, grad_qkv_low, attn_low, grad_after_low, h2_low, grad_pre_low, act_low, cot_low)
        )
        norm_totals = [
            norm_totals[0] + grad_gain_one,
            norm_totals[1] + grad_shift_one,
            norm_totals[2] + grad_gain_two,
            norm_totals[3] + grad_shift_two,
        ]
    (
        h1_rows,
        grad_qkv_rows,
        attn_rows,
        grad_after_rows,
        h2_rows,
        grad_pre_rows,
        act_rows,
        cot_rows,
    ) = [jnp.concatenate([item[index] for item in kept_rows], axis=0) for index in range(8)]
    grad_qkv_w = jnp.einsum("td,te->de", h1_rows, grad_qkv_rows, preferred_element_type=jnp.float32)
    grad_out_w = jnp.einsum(
        "td,te->de", attn_rows, grad_after_rows, preferred_element_type=jnp.float32
    )
    attn_matrices = lax.psum_scatter(
        jnp.concatenate([grad_qkv_w, grad_out_w], axis=1),
        ("dp", "ctx"),
        scatter_dimension=0,
        tiled=True,
    )
    grad_fc_w = jnp.einsum("td,tf->df", h2_rows, grad_pre_rows, preferred_element_type=jnp.float32)
    grad_proj_w = jnp.einsum("tf,td->fd", act_rows, cot_rows, preferred_element_type=jnp.float32)
    mlp_matrices = lax.psum_scatter(
        jnp.concatenate(
            [grad_fc_w, grad_proj_w.reshape(lax.axis_size(("dp", "ctx")) * shard_rows, 4 * D)],
            axis=1,
        ),
        ("dp", "ctx"),
        scatter_dimension=0,
        tiled=True,
    )
    column_sums = jnp.sum(grad_qkv_rows, axis=0, dtype=jnp.float32)
    grad_qv_b = jnp.concatenate([column_sums[:D], column_sums[2 * D :]])
    grad_out_b = jnp.sum(grad_after_rows, axis=0, dtype=jnp.float32)
    grad_fc_b = jnp.sum(grad_pre_rows, axis=0, dtype=jnp.float32)
    grad_proj_b = jnp.sum(cot_rows, axis=0, dtype=jnp.float32)
    small_sums = (
        lax.psum_scatter(norm_totals[0], ("dp", "ctx"), scatter_dimension=0, tiled=True),
        lax.psum_scatter(norm_totals[1], ("dp", "ctx"), scatter_dimension=0, tiled=True),
        lax.psum_scatter(grad_qv_b, ("dp", "ctx"), scatter_dimension=0, tiled=True),
        lax.psum_scatter(grad_out_b, ("dp", "ctx"), scatter_dimension=0, tiled=True),
        lax.psum_scatter(norm_totals[2], ("dp", "ctx"), scatter_dimension=0, tiled=True),
        lax.psum_scatter(norm_totals[3], ("dp", "ctx"), scatter_dimension=0, tiled=True),
        lax.psum_scatter(grad_fc_b, ("dp", "ctx"), scatter_dimension=0, tiled=True),
        lax.psum_scatter(grad_proj_b, ("dp", "ctx"), scatter_dimension=0, tiled=True),
    )
    grad_qkv_shard = attn_matrices[:, : 3 * D]
    grad_out_shard = attn_matrices[:, 3 * D :]
    grad_fc_shard = mlp_matrices[:, :FF]
    grad_proj_shard = mlp_matrices[:, FF:].reshape(4 * shard_rows, D)
    summed = (
        lax.psum(small_sums[0].astype(jnp.bfloat16), "rep").astype(jnp.float32),
        lax.psum(small_sums[1].astype(jnp.bfloat16), "rep").astype(jnp.float32),
        lax.psum(grad_qkv_shard.astype(jnp.bfloat16), "rep").astype(jnp.float32),
        lax.psum(small_sums[2].astype(jnp.bfloat16), "rep").astype(jnp.float32),
        lax.psum(grad_out_shard.astype(jnp.bfloat16), "rep").astype(jnp.float32),
        lax.psum(small_sums[3].astype(jnp.bfloat16), "rep").astype(jnp.float32),
        lax.psum(small_sums[4].astype(jnp.bfloat16), "rep").astype(jnp.float32),
        lax.psum(small_sums[5].astype(jnp.bfloat16), "rep").astype(jnp.float32),
        lax.psum(grad_fc_shard.astype(jnp.bfloat16), "rep").astype(jnp.float32),
        lax.psum(small_sums[6].astype(jnp.bfloat16), "rep").astype(jnp.float32),
        lax.psum(grad_proj_shard.astype(jnp.bfloat16), "rep").astype(jnp.float32),
        lax.psum(small_sums[7].astype(jnp.bfloat16), "rep").astype(jnp.float32),
    )
    return (
        jnp.stack(outputs),
        jnp.stack(input_grads),
        summed[0],
        summed[1],
        summed[2],
        summed[3],
        summed[4],
        summed[5],
        summed[6],
        summed[7],
        summed[8],
        summed[9],
        summed[10],
        summed[11],
    )


def solution(mesh):
    placed = (
        P(("rep", "dp"), "ctx", None),
        P(("rep", "dp"), None),
        P(("rep", "dp"), "ctx", None),
        P(("dp", "ctx")),
        P(("dp", "ctx")),
        P(("dp", "ctx"), None),
        P(("dp", "ctx")),
        P(("dp", "ctx"), None),
        P(("dp", "ctx")),
        P(("dp", "ctx")),
        P(("dp", "ctx")),
        P(("dp", "ctx"), None),
        P(("dp", "ctx")),
        P(("dp", "ctx"), None),
        P(("dp", "ctx")),
    )
    return jax.shard_map(
        local,
        mesh=mesh,
        in_specs=placed,
        out_specs=(
            P(("rep", "dp"), "ctx", None),
            P(("rep", "dp"), "ctx", None),
            P(("dp", "ctx")),
            P(("dp", "ctx")),
            P(("dp", "ctx"), None),
            P(("dp", "ctx")),
            P(("dp", "ctx"), None),
            P(("dp", "ctx")),
            P(("dp", "ctx")),
            P(("dp", "ctx")),
            P(("dp", "ctx"), None),
            P(("dp", "ctx")),
            P(("dp", "ctx"), None),
            P(("dp", "ctx")),
        ),
        check_vma=False,
    )
```

profile of v0, /device:TPU:0, one launch (start us, length us, event | category | flops | bytes accessed | tf_op | source)
XLA Modules:
  0.0 4230.1 jit_solution(15753856021191116933)
XLA Ops:
  18.1 42.6 %all-reduce.19 = (bf16[1600]{0:T(1024)(128)(2,1)S(1)}, bf16[1600]{0:T(1024)(128)(2,1)S(1)}, bf16[3200]{0:T(1024)(128)(2,1)S(1)}, bf16[1600]{0:T(1024)(128)(2,1)S...) all-reduce(bf16[1600]{0:T(1024)(128)(2,1)S(1)} %dynamic-update-slic, ...), channel_id=1, replica_groups=mesh['rep'=4,'dp'=2,'ctx'=4] {'dp','ctx'}, use_global_device_ids=true, to_apply=%add.1 | all-reduce | flops 19200 | bytes 76800
  63.8 164.1 %all-gather.9.cloned.1.call-done = bf16[1600,4800]{1,0:T(8,128)(2,1)} async-done(((bf16[200,4800]{1,0:T(8,128)(2,1)}), bf16[1600,4800]{1,0:T(8,128)(2,1)}) %all-gather.9.cloned.1.call-update) | async-done | bytes 15360016 | tf_op jit(solution)/shard_map/all_gather | solution.py:96
  277.0 31.6 all-gather.13.cloned.1.call-done
  332.9 41.6 all-gather.11.cloned.1.call-done
  388.6 73.3 %all-gather.15.cloned.1.call-done = bf16[1600,1600]{1,0:T(8,128)(2,1)} async-done(((bf16[200,1600]{1,0:T(8,128)(2,1)}), bf16[1600,1600]{1,0:T(8,128)(2,1)}) %all-gather.15.cloned.1.call-update) | async-done | bytes 5120016 | tf_op jit(solution)/shard_map/all_gather | solution.py:98
  467.4 60.3 %all-gather.23.cloned.1.call-done = bf16[1024,1600]{0,1:T(8,128)(2,1)} async-done(((bf16[256,1600]{0,1:T(8,128)(2,1)}), bf16[1024,1600]{0,1:T(8,128)(2,1)}) %all-gather.23.cloned.1.call-update) | async-done | bytes 3276816 | tf_op jit(solution)/shard_map/all_gather | solution.py:125
  527.7 15.8 fusion.128
  554.5 39.0 all-gather.21.cloned.1.call-done
  615.0 370.8 %all-gather.17.cloned.1.call-done = bf16[1600,6400]{1,0:T(8,128)(2,1)} async-done(((bf16[200,6400]{1,0:T(8,128)(2,1)}), bf16[1600,6400]{1,0:T(8,128)(2,1)}) %all-gather.17.cloned.1.call-update) | async-done | bytes 20480016 | tf_op jit(solution)/shard_map/all_gather | solution.py:104
  985.8 17.5 multiply_convert_fusion.4
  1003.2 17.6 multiply_convert_fusion.5
  1020.9 375.6 %all-gather.19.cloned.1.call-done = bf16[6400,1600]{1,0:T(8,128)(2,1)} async-done(((bf16[800,1600]{1,0:T(8,128)(2,1)}), bf16[6400,1600]{1,0:T(8,128)(2,1)}) %all-gather.19.cloned.1.call-update) | async-done | bytes 20480016 | tf_op jit(solution)/shard_map/all_gather | solution.py:106
  1435.9 15.8 multiply_reduce_fusion.3
  1472.6 17.8 multiply_reduce_fusion
  1490.3 17.2 multiply_convert_fusion
  1521.2 19.0 multiply_reduce_fusion.1
  1540.2 17.5 multiply_convert_fusion.1
  1564.7 14.7 fusion.47
  1613.7 18.5 reduce-scatter.11.cloned.1.call-done
  1632.2 117.7 %reduce-scatter.9.cloned.1.call-done = bf16[256,3200]{0,1:T(8,128)(2,1)} async-done(((bf16[1024,3200]{0,1:T(8,128)(2,1)}), bf16[256,3200]{0,1:T(8,128)(2,1)}) %reduce-scatter.9.cloned.1.call-update) | async-done | bytes 1638416 | tf_op jit(solution)/shard_map/reduce_scatter | solution.py:219
  1749.9 16.3 fusion.85
  1766.2 29.0 pad_maximum_fusion.1
  1796.7 22.2 fusion.24
  1818.9 48.2 %reshape.217 = f32[1600,6400]{1,0:T(8,128)} reshape(f32[6400,1600]{1,0:T(8,128)} %fusion.24) | data formatting | bytes 81920000 | tf_op jit(solution)/shard_map/reshape | solution.py:268
  1867.1 20.1 fusion.30
  1887.2 56.2 %pad_maximum_fusion = f32[1600,12800]{1,0:T(8,128)} fusion(f32[1600,6400]{1,0:T(8,128)} %reshape.217, f32[1600,6400]{1,0:T(8,128)} %fusion.30), kind=kLoop, calls=%fused_computation | loop fusion | flops 20480000 | bytes 163840000 | tf_op jit(solution)/shard_map/concatenate | solution.py:267
  1948.5 15.6 fusion.38
  1995.4 555.8 %reduce-scatter.13.cloned.1.call-done = f32[200,6400]{1,0:T(8,128)} async-done(((f32[1600,6400]{1,0:T(8,128)}), f32[200,6400]{1,0:T(8,128)}) %reduce-scatter.13.cloned.1.call-update) | async-done | bytes 5120016
  2556.5 1487.1 %reduce-scatter.15.cloned.1.call-done = f32[200,12800]{1,0:T(8,128)} async-done(((f32[1600,12800]{1,0:T(8,128)}), f32[200,12800]{1,0:T(8,128)}) %reduce-scatter.15.cloned.1.call-update) | async-done | bytes 10240016
  4084.1 35.0 all-reduce.18
  4119.7 18.7 all-reduce.20
  4151.5 61.3 %all-reduce.24.cloned.1.call-done = (bf16[200,4800]{1,0:T(8,128)(2,1)}, bf16[200,1600]{1,0:T(8,128)(2,1)}, bf16[200,6400]{1,0:T(8,128)(2,1)}, bf16[800,1600]{1,0:T(8,128)(2,1)}) async-done(((bf16[200,4800]{1,0:T(8,128)(2,1)}, bf16[200,1600]{1,0:T(8,128)(2,1)}, bf16[200,6400]{1,0:T(8,128)(2,1)}, bf16[800,1600]{1,0:T(8,128)(2,1)}), (bf16[200,4800]{1,0:T(8,128)(2,1)}, bf16[200,1600]{1,0:T(8,128)(2,1)}, ...) | async-done | bytes 7680016 | tf_op jit(solution)/shard_map/psum | solution.py:297
  (327 shorter events, 357.4 us)
Async XLA Ops:
  7.2 220.7 %all-gather.9.cloned.1.call-start = ((), (), s32[]{:S(2)}) async-start(), calls=%async_computation.4 | async-start | bytes 17510400 | tf_op jit(solution)/shard_map/all_gather | solution.py:96
  7.9 300.6 %all-gather.13.cloned.1.call-start = ((), (), s32[]{:S(2)}) async-start(), calls=%async_computation.6 | async-start | bytes 4096000 | tf_op jit(solution)/shard_map/all_gather | solution.py:125
  63.8 164.1 %copy-start.40 = (bf16[256,1600]{0,1:T(8,128)(2,1)}, bf16[256,1600]{0,1:T(8,128)(2,1)S(1)}, u32[]{:S(2)}) copy-start(bf16[256,1600]{0,1:T(8,128)(2,1)S(1)} %get-tuple-element.72) | copy-start | bytes 2457604
  63.8 192.4 %copy-start.42 = (bf16[256,1600]{0,1:T(8,128)(2,1)}, bf16[256,1600]{0,1:T(8,128)(2,1)S(1)}, u32[]{:S(2)}) copy-start(bf16[256,1600]{0,1:T(8,128)(2,1)S(1)} %get-tuple-element.73) | copy-start | bytes 2457604
  244.6 129.8 %all-gather.11.cloned.1.call-start = ((), (), s32[]{:S(2)}) async-start(), calls=%async_computation.5 | async-start | bytes 4096000 | tf_op jit(solution)/shard_map/all_gather | solution.py:126
  245.4 216.6 %all-gather.15.cloned.1.call-start = ((), (), s32[]{:S(2)}) async-start(), calls=%async_computation.7 | async-start | bytes 5990400 | tf_op jit(solution)/shard_map/all_gather | solution.py:98
  245.9 281.8 %all-gather.23.cloned.1.call-start = ((), (), s32[]{:S(2)}) async-start(), calls=%async_computation.11 | async-start | bytes 4096000 | tf_op jit(solution)/shard_map/all_gather | solution.py:125
  273.1 320.3 %all-gather.21.cloned.1.call-start = ((), (), s32[]{:S(2)}) async-start(), calls=%async_computation.10 | async-start | bytes 4096000 | tf_op jit(solution)/shard_map/all_gather | solution.py:126
  273.7 712.1 %all-gather.17.cloned.1.call-start = ((), (), s32[]{:S(2)}) async-start(), calls=%async_computation.8 | async-start | bytes 23040000 | tf_op jit(solution)/shard_map/all_gather | solution.py:104
  274.5 1122.0 %all-gather.19.cloned.1.call-start = ((), (), s32[]{:S(2)}) async-start(), calls=%async_computation.9 | async-start | bytes 23961600 | tf_op jit(solution)/shard_map/all_gather | solution.py:106
  275.2 1357.0 %reduce-scatter.11.cloned.1.call-start = ((), (), s32[]{:S(2)}) async-start(), calls=%async_computation.13 | async-start | bytes 8192000 | tf_op jit(solution)/shard_map/reduce_scatter | solution.py:219
  275.3 1176.5 %copy-start.52 = (f32[1600]{0:T(1024)}, f32[1600]{0:T(1024)S(1)}, u32[]{:S(2)}) copy-start(f32[1600]{0:T(1024)S(1)} %convert_element_type.239) | copy-start | bytes 19204
  467.1 984.7 %copy-start.4 = (f32[256,1600]{0,1:T(8,128)}, f32[256,1600]{0,1:T(8,128)S(1)}, u32[]{:S(2)}) copy-start(f32[256,1600]{0,1:T(8,128)S(1)} %get-tuple-element.99) | copy-start | bytes 4915204
  467.1 984.7 %copy-start.58 = (f32[256]{0:T(256)}, f32[256]{0:T(256)S(1)}, u32[]{:S(2)}) copy-start(f32[256]{0:T(256)S(1)} %broadcast_multiply_fusion.10) | copy-start | bytes 3076
  612.0 839.8 %copy-start.60 = (f32[256]{0:T(256)}, f32[256]{0:T(256)S(1)}, u32[]{:S(2)}) copy-start(f32[256]{0:T(256)S(1)} %broadcast_multiply_fusion.8) | copy-start | bytes 3076
  612.3 839.6 %copy-start.66 = (f32[256]{0:T(256)}, f32[256]{0:T(256)S(1)}, u32[]{:S(2)}) copy-start(f32[256]{0:T(256)S(1)} %add_rsqrt_fusion.2) | copy-start | bytes 3076
  612.3 839.6 %copy-start.68 = (f32[256]{0:T(256)}, f32[256]{0:T(256)S(1)}, u32[]{:S(2)}) copy-start(f32[256]{0:T(256)S(1)} %add_rsqrt_fusion) | copy-start | bytes 3076
  615.0 388.3 %copy-start.47 = (bf16[256,1600]{0,1:T(8,128)(2,1)}, bf16[256,1600]{0,1:T(8,128)(2,1)S(1)}, u32[]{:S(2)}) copy-start(bf16[256,1600]{0,1:T(8,128)(2,1)S(1)} %get-tuple-element.81) | copy-start | bytes 2457604
  1003.2 393.2 %copy-start.9 = (bf16[2,256,1600]{1,2,0:T(8,128)(2,1)S(1)}, bf16[2,256,1600]{1,2,0:T(8,128)(2,1)}, u32[]{:S(2)}) copy-start(bf16[2,256,1600]{1,2,0:T(8,128)(2,1)} %param.17) | copy-start | bytes 4915204
  1515.9 234.1 %reduce-scatter.9.cloned.1.call-start = ((), (), s32[]{:S(2)}) async-start(), calls=%async_computation.12 | async-start | bytes 8192000 | tf_op jit(solution)/shard_map/reduce_scatter | solution.py:219
  1584.9 966.4 %reduce-scatter.13.cloned.1.call-start = ((), (), s32[]{:S(2)}) async-start(), calls=%async_computation.14 | async-start | bytes 46080000
  1604.6 145.3 %copy-start.28 = (bf16[25,64,256]{2,1,0:T(8,128)(2,1)S(1)}, bf16[25,64,256]{2,1,0:T(8,128)(2,1)}, u32[]{:S(2)}) copy-start(bf16[25,64,256]{2,1,0:T(8,128)(2,1)} %multiply_convert_fusion.6) | copy-start | bytes 2457604
  1604.6 145.3 %copy-start.41 = (bf16[256,1600]{0,1:T(8,128)(2,1)S(1)}, bf16[256,1600]{0,1:T(8,128)(2,1)}, u32[]{:S(2)}) copy-start(bf16[256,1600]{0,1:T(8,128)(2,1)} %copy-done.40) | copy-start | bytes 2457604
  1604.6 145.3 %copy-start.43 = (bf16[256,1600]{0,1:T(8,128)(2,1)S(1)}, bf16[256,1600]{0,1:T(8,128)(2,1)}, u32[]{:S(2)}) copy-start(bf16[256,1600]{0,1:T(8,128)(2,1)} %copy-done.42) | copy-start | bytes 2457604
  1613.7 152.5 %copy-start.31 = (bf16[25,64,256]{2,1,0:T(8,128)(2,1)}, bf16[25,64,256]{2,1,0:T(8,128)(2,1)S(1)}, u32[]{:S(2)}) copy-start(bf16[25,64,256]{2,1,0:T(8,128)(2,1)S(1)} %multiply_convert_fusion.7) | copy-start | bytes 2457604
  1795.2 2248.3 %reduce-scatter.15.cloned.1.call-start = ((), (), s32[]{:S(2)}) async-start(), calls=%async_computation.15 | async-start | bytes 92160000
  1943.5 2269.3 %all-reduce.24.cloned.1.call-start = ((), (), s32[]{:S(2)}) async-start(), calls=%async_computation.16 | async-start | bytes 15667200 | tf_op jit(solution)/shard_map/psum | solution.py:297
  4070.7 72.3 %copy-start.53 = (f32[1600]{0:T(1024)S(1)}, f32[1600]{0:T(1024)}, u32[]{:S(2)}) copy-start(f32[1600]{0:T(1024)} %copy-done.52) | copy-start | bytes 19204
  4070.7 72.3 %copy-start.61 = (f32[256]{0:T(256)S(1)}, f32[256]{0:T(256)}, u32[]{:S(2)}) copy-start(f32[256]{0:T(256)} %copy-done.60) | copy-start | bytes 3076
  4070.7 72.3 %copy-start.69 = (f32[256]{0:T(256)S(1)}, f32[256]{0:T(256)}, u32[]{:S(2)}) copy-start(f32[256]{0:T(256)} %copy-done.68) | copy-start | bytes 3076
  4070.7 72.3 %copy-start.79 = (f32[256]{0:T(256)S(1)}, f32[256]{0:T(256)}, u32[]{:S(2)}) copy-start(f32[256]{0:T(256)} %copy-done.78) | copy-start | bytes 3076
  4070.7 72.3 %copy-start.81 = (f32[256]{0:T(256)S(1)}, f32[256]{0:T(256)}, u32[]{:S(2)}) copy-start(f32[256]{0:T(256)} %copy-done.80) | copy-start | bytes 3076
  (70 other events, 732.1 us)
Sparse Core Ops, SparseCore 0:
  10.1 217.6 all-gather.8
  244.7 63.7 all-gather.12
  310.7 63.7 all-gather.10
  376.4 85.4 all-gather.14
  463.9 63.7 all-gather.22
  529.7 63.7 all-gather.20
  595.0 390.7 all-gather.16
  987.3 409.0 all-gather.18
  1516.0 116.2 reduce-scatter.10
  1634.4 115.5 reduce-scatter.8
  1795.3 755.9 reduce-scatter.12
  2554.7 1488.7 reduce-scatter.14
  4056.6 156.1 all-reduce.23
where the time goes:
time: 4240 us; the launch traced here: 4230 us
  waiting for transfers between devices  3400 us (80%)
  matrix products  406 us (10%)
  other arithmetic  206 us (5%)
  blocking collectives  96.3 us (2%)
  local copies, waits for them, and re-layouts  90.6 us (2%)
    unnamed x15, waiting for transfers between devices  2050 us
    all_gather x1, waiting for transfers between devices, local(): lax.all_gather(mlp_shards[4], ('dp', 'ctx'), axis=0, tiled=True)  376 us
    all_gather x1, waiting for transfers between devices, local(): lax.all_gather(mlp_shards[2], ('dp', 'ctx'), axis=0, tiled=True)  371 us
    all_gather x1, waiting for transfers between devices, local(): lax.all_gather(attn_shards[2], ('dp', 'ctx'), axis=0, tiled=True)  164 us
    reduce_scatter x2, waiting for transfers between devices, local(): lax.psum_scatter(key_value_term(jnp.int32(0), lax.axis_size('ctx') * row_...  136 us
    all_gather x2, waiting for transfers between devices, local(): lax.all_gather(qkv_low[:, D:2 * D], 'ctx', axis=0, tiled=True)  91.9 us
  transfers between devices with their start and end apart: 13, of which 13 were waited for; matrix products, arithmetic and copies ran while one was open for 11% of the time, Pallas kernels for 0%

commit v1 on v0

--- a/solution.py
+++ b/solution.py
@@ -1,6 +1,8 @@
 import jax
 import jax.numpy as jnp
 from jax import lax
+from jax.experimental import pallas as pl
+from jax.experimental.pallas import tpu as pltpu
 from jax.sharding import PartitionSpec as P
 
 D = 1600
@@ -61,7 +63,7 @@
     return jnp.where(allowed[None], scores, MASKED)
 
 
-def local(
+def general_local(
     hidden_in,
     piece_starts,
     grad_out,
@@ -323,6 +325,457 @@
     )
 
 
+LANES = 128
+
+
+def over_core(value):
+    return lax.ppermute(value, "rep", [(0, 1), (1, 0), (2, 3), (3, 2)])
+
+
+def over_x(value):
+    return lax.ppermute(value, "rep", [(0, 2), (2, 0), (1, 3), (3, 1)])
+
+
+def over_y(value):
+    return lax.ppermute(value, "dp", [(0, 1), (1, 0)])
+
+
+def ordered(first_is_mine, mine, other):
+    return jnp.stack(
+        [jnp.where(first_is_mine, mine, other), jnp.where(first_is_mine, other, mine)]
+    )
+
+
+def mxu(left, right, dims=((1,), (0,))):
+    return lax.dot_general(left, right, (dims, ((), ())), preferred_element_type=jnp.float32)
+
+
+def attend_forward_kernel(limit_ref, q_ref, k_ref, v_t_ref, o_ref, lse_ref):
+    pair = pl.program_id(0)
+    width = q_ref.shape[0] // 2
+    lane = lax.broadcasted_iota(jnp.int32, (1, LANES), 1)
+    valid = lane < D - pair * LANES
+    queries = jnp.where(valid, q_ref[...], 0) * jnp.asarray(HD ** (-0.5), q_ref.dtype)
+    keys = jnp.where(valid, k_ref[...], 0)
+    for part in range(2):
+        rows = slice(part * width, (part + 1) * width)
+        first, count = KEY_SPANS[part]
+        limit = limit_ref[:, rows]
+        mixed = []
+        for head in range(2):
+            own = (lane >= head * HD) & (lane < (head + 1) * HD)
+            scores = mxu(keys[:count], jnp.where(own, queries[rows], 0), ((1,), (1,)))
+            position = first + lax.broadcasted_iota(jnp.int32, (count - first, width), 0)
+            tail = jnp.where(position < limit, scores[first:], MASKED)
+            scores = tail if first == 0 else jnp.concatenate([scores[:first], tail], axis=0)
+            top = jnp.max(scores, axis=0, keepdims=True)
+            expo = jnp.exp(scores - top)
+            total = jnp.sum(expo, axis=0, keepdims=True)
+            values = v_t_ref[head * HD : (head + 1) * HD, :count]
+            mixed.append(mxu(values, expo.astype(jnp.bfloat16)) / total)
+            lse_ref[0, head : head + 1, rows] = top + jnp.log(total)
+        o_ref[rows, :] = jnp.concatenate(mixed, axis=0).T.astype(o_ref.dtype)
+
+
+def attend_backward_kernel(
+    limit_ref,
+    q_ref,
+    k_ref,
+    k_t_ref,
+    v_ref,
+    grad_ref,
+    lse_ref,
+    dq_ref,
+    dk_ref,
+    dv_ref,
+    dk_sum,
+    dv_sum,
+):
+    pair = pl.program_id(0)
+    width = q_ref.shape[0] // 2
+    lane = lax.broadcasted_iota(jnp.int32, (1, LANES), 1)
+    valid = lane < D - pair * LANES
+    queries = jnp.where(valid, q_ref[...], 0) * jnp.asarray(HD ** (-0.5), q_ref.dtype)
+    grads = jnp.where(valid, grad_ref[...], 0)
+    keys = jnp.where(valid, k_ref[...], 0)
+    values = jnp.where(valid, v_ref[...], 0)
+    dk_sum[...] = jnp.zeros_like(dk_sum)
+    dv_sum[...] = jnp.zeros_like(dv_sum)
+    for part in range(2):
+        rows = slice(part * width, (part + 1) * width)
+        first, count = KEY_SPANS[part]
+        limit = limit_ref[:, rows]
+        grad_q = []
+        for head in range(2):
+            own = (lane >= head * HD) & (lane < (head + 1) * HD)
+            queries_own = jnp.where(own, queries[rows], 0)
+            grads_own = jnp.where(own, grads[rows], 0)
+            scores = mxu(keys[:count], queries_own, ((1,), (1,)))
+            position = first + lax.broadcasted_iota(jnp.int32, (count - first, width), 0)
+            tail = jnp.where(position < limit, scores[first:], MASKED)
+            scores = tail if first == 0 else jnp.concatenate([scores[:first], tail], axis=0)
+            probs = jnp.exp(scores - lse_ref[0, head : head + 1, rows])
+            grad_probs = mxu(values[:count], grads_own, ((1,), (1,)))
+            inner = jnp.sum(probs * grad_probs, axis=0, keepdims=True)
+            grad_scores = (probs * (grad_probs - inner)).astype(jnp.bfloat16)
+            grad_q.append(mxu(k_t_ref[head * HD : (head + 1) * HD, :count], grad_scores))
+            dk_sum[:count, :] += mxu(grad_scores, queries_own)
+            dv_sum[:count, :] += mxu(probs.astype(jnp.bfloat16), grads_own)
+        grad_q = jnp.concatenate(grad_q, axis=0) * HD ** (-0.5)
+        dq_ref[rows, :] = grad_q.T.astype(dq_ref.dtype)
+    dk_ref[...] = dk_sum[...].astype(dk_ref.dtype)
+    dv_ref[...] = dv_sum[...].astype(dv_ref.dtype)
+
+
+PAIRS = -(-D // LANES)
+KEY_SPANS = ((0, 640), (512, 1024))
+
+
+def by_columns(rows):
+    return pl.BlockSpec((rows, LANES), lambda pair: (0, pair))
+
+
+def by_rows(columns):
+    return pl.BlockSpec((LANES, columns), lambda pair: (pair, 0))
+
+
+def attend_forward(limit, q, k, v_t):
+    rows, keys = q.shape[0], k.shape[0]
+    return pl.pallas_call(
+        attend_forward_kernel,
+        grid=(PAIRS,),
+        in_specs=[
+            pl.BlockSpec((1, rows), lambda pair: (0, 0)),
+            by_columns(rows),
+            by_columns(keys),
+            by_rows(keys),
+        ],
+        out_specs=[by_columns(rows), pl.BlockSpec((1, 2, rows), lambda pair: (pair, 0, 0))],
+        out_shape=[
+            jax.ShapeDtypeStruct((rows, D), jnp.bfloat16),
+            jax.ShapeDtypeStruct((PAIRS, 2, rows), jnp.float32),
+        ],
+        cost_estimate=pl.CostEstimate(
+            flops=4 * rows * keys * D, transcendentals=rows * keys * HEADS, bytes_accessed=8 * keys * D
+        ),
+        compiler_params=pltpu.CompilerParams(vmem_limit_bytes=48 << 20),
+        name="attend_forward",
+    )(limit, q, k, v_t)
+
+
+def attend_backward(limit, q, k, k_t, v, grad, lse):
+    rows, keys = q.shape[0], k.shape[0]
+    return pl.pallas_call(
+        attend_backward_kernel,
+        grid=(PAIRS,),
+        in_specs=[
+            pl.BlockSpec((1, rows), lambda pair: (0, 0)),
+            by_columns(rows),
+            by_columns(keys),
+            by_rows(keys),
+            by_columns(keys),
+            by_columns(rows),
+            pl.BlockSpec((1, 2, rows), lambda pair: (pair, 0, 0)),
+        ],
+        out_specs=[by_columns(rows), by_columns(keys), by_columns(keys)],
+        out_shape=[
+            jax.ShapeDtypeStruct((rows, D), jnp.bfloat16),
+            jax.ShapeDtypeStruct((keys, D), jnp.bfloat16),
+            jax.ShapeDtypeStruct((keys, D), jnp.bfloat16),
+        ],
+        scratch_shapes=[pltpu.VMEM((keys, LANES), jnp.float32), pltpu.VMEM((keys, LANES), jnp.float32)],
+        cost_estimate=pl.CostEstimate(
+            flops=10 * rows * keys * D, transcendentals=rows * keys * HEADS, bytes_accessed=16 * keys * D
+        ),
+        compiler_params=pltpu.CompilerParams(vmem_limit_bytes=48 << 20),
+        name="attend_backward",
+    )(limit, q, k, k_t, v, grad, lse)
+
+
+def sequence_local(
+    hidden_in,
+    piece_starts,
+    grad_out,
+    attn_gain,
+    attn_shift,
+    qkv_weight,
+    qv_bias,
+    out_weight,
+    out_bias,
+    mlp_gain,
+    mlp_shift,
+    fc_weight,
+    fc_bias,
+    proj_weight,
+    proj_bias,
+):
+    rep, dp, ctx = (lax.axis_index(name) for name in ("rep", "dp", "ctx"))
+    chip_x, core = rep // 2, rep % 2
+    chips, shards = lax.axis_size("ctx"), lax.axis_size(("dp", "ctx"))
+    seqs, block, _ = hidden_in.shape
+    half = block // 2
+    rows = chips * half
+    shard_rows = D // shards
+    f32, low = jnp.float32, jnp.bfloat16
+    core_low, x_low, y_low = core == 0, chip_x == 0, dp == 0
+    half_of = lambda index: (core + index) % 2
+
+    def to_sequence(value):
+        halves = value.reshape(seqs, 2, half, D)
+        mine = half_of(ctx)
+        kept = lax.dynamic_index_in_dim(halves, mine, 1, keepdims=False)
+        came = over_core(lax.dynamic_index_in_dim(halves, 1 - mine, 1, keepdims=False))
+        every = ordered(core_low, kept, came).reshape(chips, half, D)
+        return lax.all_to_all(every, "ctx", 0, 0, tiled=True).reshape(rows, D)
+
+    def from_sequence(value):
+        every = lax.all_to_all(value.reshape(chips, half, D), "ctx", 0, 0, tiled=True)
+        every = every.reshape(2, seqs, half, D)
+        kept = lax.dynamic_index_in_dim(every, core, 0, keepdims=False)
+        came = over_core(lax.dynamic_index_in_dim(every, 1 - core, 0, keepdims=False))
+        both = ordered(half_of(ctx) == 0, kept, came)
+        return both.transpose(1, 0, 2, 3).reshape(seqs, block, D)
+
+    def interleave(mine, other):
+        mine, other = mine.reshape(chips, half, D), other.reshape(chips, half, D)
+        first = (half_of(jnp.arange(chips)) == 0)[:, None, None]
+        return jnp.stack(
+            [jnp.where(first, mine, other), jnp.where(first, other, mine)], axis=1
+        ).reshape(2 * rows, D)
+
+    def split_rows(value):
+        value = value.reshape(chips, 2, half, D)
+        first = (half_of(jnp.arange(chips)) == 0)[:, None, None]
+        return (
+            jnp.where(first, value[:, 0], value[:, 1]).reshape(rows, D),
+            jnp.where(first, value[:, 1], value[:, 0]).reshape(rows, D),
+        )
+
+    def gather_shared(shard):
+        mine = lax.all_gather(shard, "ctx", axis=0, tiled=True)
+        count = mine.shape[0] // 2
+        near = over_y(lax.dynamic_slice_in_dim(mine, chip_x * count, count, 0))
+        far = over_x(near)
+        other = ordered(x_low, near, far).reshape(mine.shape)
+        return ordered(y_low, mine, other).reshape(2 * mine.shape[0], D)
+
+    def gather_own(shard):
+        mine = lax.all_gather(shard, "ctx", axis=0, tiled=True)
+        other = over_y(mine)
+        return ordered(y_low, mine, other).reshape(2 * mine.shape[0], D)
+
+    small = jnp.concatenate(
+        [attn_gain, attn_shift, qv_bias, out_bias, mlp_gain, mlp_shift, fc_bias, proj_bias]
+    )
+    small = lax.all_gather(small[None], ("dp", "ctx"), axis=0, tiled=True).astype(f32)
+    parts, at = [], 0
+    for item in (attn_gain, attn_shift, qv_bias, out_bias, mlp_gain, mlp_shift, fc_bias, proj_bias):
+        parts.append(small[:, at : at + item.shape[0]].reshape(-1))
+        at += item.shape[0]
+    gain_one, shift_one, qv_full, out_bias_full, gain_two, shift_two, fc_bias_full, proj_bias_full = parts
+    query_bias, value_bias = qv_full[:D], qv_full[D:]
+    fc_bias_mine = lax.dynamic_index_in_dim(
+        fc_bias_full.reshape(shards, 4, shard_rows), rep, 1, keepdims=False
+    ).reshape(D)
+
+    q_or_v = gather_shared(jnp.where(core_low, qkv_weight[:, :D], qkv_weight[:, 2 * D :]))
+    k_or_out = gather_shared(jnp.where(core_low, qkv_weight[:, D : 2 * D], out_weight))
+    v_or_q, out_or_k = over_core(q_or_v), over_core(k_or_out)
+    fc_mine = gather_own(
+        lax.dynamic_index_in_dim(
+            fc_weight.reshape(shard_rows, shards, 4, shard_rows), rep, 2, keepdims=False
+        ).reshape(shard_rows, D)
+    )
+    proj_mine = gather_own(
+        lax.dynamic_index_in_dim(proj_weight.reshape(4, shard_rows, D), rep, 0, keepdims=False)
+    )
+    key_weight = jnp.where(core_low, k_or_out, out_or_k)
+    out_full = jnp.where(core_low, out_or_k, k_or_out)
+
+    tokens_low = to_sequence(hidden_in)
+    cot_low = to_sequence(grad_out)
+    every_starts = ordered(core_low, piece_starts, over_core(piece_starts)).reshape(chips, -1)
+    starts = lax.dynamic_index_in_dim(every_starts, ctx, 0, keepdims=False)
+    block_index = jnp.arange(chips)
+    row_pos = (
+        (block_index * block + half_of(block_index) * half)[:, None] + jnp.arange(half)[None, :]
+    ).reshape(rows)
+    inside = (row_pos[:, None] >= starts[None, :]) & (row_pos[:, None] < starts[None, :] + PIECE)
+    limit = jnp.maximum(row_pos + 1, jnp.max(jnp.where(inside, starts[None, :] + PIECE, 0), axis=1))
+    limit = limit.astype(jnp.int32)[None, :]
+
+    tokens = tokens_low.astype(f32)
+    normed_out, normed_one, inv_one = layer_norm(tokens, gain_one, shift_one)
+    h1_low = normed_out.astype(low)
+    bias_a = jnp.where(core_low, query_bias, value_bias)
+    bias_b = jnp.where(core_low, value_bias, query_bias)
+    result_a = (mxu(h1_low, q_or_v) + bias_a).astype(low)
+    result_b = (mxu(h1_low, v_or_q) + bias_b).astype(low)
+    query_low = jnp.where(core_low, result_a, result_b)
+    value_low = jnp.where(core_low, result_b, result_a)
+    key_low = mxu(h1_low, key_weight).astype(low)
+    keys = interleave(key_low, over_core(key_low))
+    values = interleave(value_low, over_core(value_low))
+    attn_low, lse = attend_forward(limit, query_low, keys, values.T)
+    after_attn = tokens + mxu(attn_low, out_full) + out_bias_full
+    normed_out_two, normed_two, inv_two = layer_norm(after_attn, gain_two, shift_two)
+    h2_low = normed_out_two.astype(low)
+
+    def spread(value):
+        chip = jnp.concatenate([value, over_x(value)], axis=0)
+        return jnp.concatenate([chip, over_core(chip)], axis=0)
+
+    def collect(value):
+        terms = value.astype(low)
+        pair = terms[: 2 * rows].astype(f32) + over_core(terms[2 * rows :]).astype(f32)
+        return pair[:rows] + over_x(pair[rows:].astype(low)).astype(f32)
+
+    h2_all = spread(h2_low)
+    cot_all = spread(cot_low)
+    hidden_pre = mxu(h2_all, fc_mine) + fc_bias_mine
+    hidden_act, hidden_slope = gelu_both(hidden_pre)
+    act_low = hidden_act.astype(low)
+    block_value = (after_attn + collect(mxu(act_low, proj_mine)) + proj_bias_full).astype(low)
+
+    grad_act = mxu(cot_all, proj_mine, ((1,), (1,)))
+    grad_pre_low = (grad_act * hidden_slope).astype(low)
+    grad_proj_mine = mxu(act_low, cot_all, ((0,), (0,)))
+    grad_fc_mine = mxu(h2_all, grad_pre_low, ((0,), (0,)))
+    grad_h2 = collect(mxu(grad_pre_low, fc_mine, ((1,), (1,))))
+    grad_through, grad_gain_two, grad_shift_two = norm_back(grad_h2, normed_two, inv_two, gain_two)
+    grad_after = grad_through + cot_low.astype(f32)
+    grad_after_low = grad_after.astype(low)
+
+    grad_attn_low = mxu(grad_after_low, out_full, ((1,), (1,))).astype(low)
+    grad_query, grad_keys, grad_values = attend_backward(
+        limit, query_low, keys, keys.T, values, grad_attn_low, lse
+    )
+
+    def own_rows(value):
+        mine, other = split_rows(value)
+        return (mine.astype(f32) + over_core(other).astype(f32)).astype(low)
+
+    grad_key, grad_value = own_rows(grad_keys), own_rows(grad_values)
+    grad_a = jnp.where(core_low, grad_query, grad_value)
+    grad_b = jnp.where(core_low, grad_value, grad_query)
+    grad_h1 = (
+        mxu(grad_a, q_or_v, ((1,), (1,)))
+        + mxu(grad_b, v_or_q, ((1,), (1,)))
+        + mxu(grad_key, key_weight, ((1,), (1,)))
+    )
+    grad_into, grad_gain_one, grad_shift_one = norm_back(grad_h1, normed_one, inv_one, gain_one)
+    input_grad = from_sequence((grad_after + grad_into).astype(low)).astype(f32)
+    block_out = from_sequence(block_value)
+
+    h1_chip = jnp.concatenate([h1_low, over_core(h1_low)], axis=0)
+    attn_chip = jnp.concatenate([attn_low, over_core(attn_low)], axis=0)
+    right_a = jnp.concatenate([grad_a, over_core(grad_b)], axis=0)
+    right_b = jnp.concatenate(
+        [
+            jnp.where(core_low, grad_key, grad_after_low),
+            over_core(jnp.where(core_low, grad_after_low, grad_key)),
+        ],
+        axis=0,
+    )
+    left_b = jnp.where(core_low, h1_chip, attn_chip)
+    term_a = mxu(h1_chip, right_a, ((0,), (0,))).astype(low)
+    term_b = mxu(left_b, right_b, ((0,), (0,))).astype(low)
+
+    def finish(value):
+        return lax.psum_scatter(value, "ctx", scatter_dimension=0, tiled=True)
+
+    def sum_own(value):
+        both = value.astype(low).reshape(2, -1, D)
+        kept = lax.dynamic_index_in_dim(both, dp, 0, keepdims=False)
+        came = over_y(lax.dynamic_index_in_dim(both, 1 - dp, 0, keepdims=False))
+        return finish((kept.astype(f32) + came.astype(f32)).astype(low))
+
+    def sum_shared(first, second):
+        quarter = D // 4
+        both = jnp.stack([first, second]).reshape(2, 2, 2, quarter, D)
+        kept_x = lax.dynamic_index_in_dim(both[:, :, 0], chip_x, 0, keepdims=False)
+        came_x = over_x(lax.dynamic_index_in_dim(both[:, :, 0], 1 - chip_x, 0, keepdims=False))
+        kept_y = lax.dynamic_index_in_dim(both[:, :, 1], dp, 1, keepdims=False)
+        came_y = over_y(lax.dynamic_index_in_dim(both[:, :, 1], 1 - dp, 1, keepdims=False))
+        sum_x = (kept_x.astype(f32) + came_x.astype(f32)).astype(low)
+        sum_y = (kept_y.astype(f32) + came_y.astype(f32)).astype(low)
+        last_x = lax.dynamic_index_in_dim(sum_x, dp, 0, keepdims=False).astype(f32) + over_y(
+            lax.dynamic_index_in_dim(sum_x, 1 - dp, 0, keepdims=False)
+        ).astype(f32)
+        last_y = lax.dynamic_index_in_dim(sum_y, chip_x, 0, keepdims=False).astype(f32) + over_x(
+            lax.dynamic_index_in_dim(sum_y, 1 - chip_x, 0, keepdims=False)
+        ).astype(f32)
+        return finish(jnp.concatenate([last_x, last_y], axis=0).astype(low))
+
+    def share(value):
+        pair = ordered(x_low, value, over_x(value))
+        return ordered(core_low, pair, over_core(pair)).reshape((4,) + value.shape)
+
+    attn_quarters = share(sum_shared(term_a, term_b)).astype(f32)
+    grad_qkv_shard = jnp.concatenate([attn_quarters[0], attn_quarters[1], attn_quarters[2]], axis=1)
+    grad_out_shard = attn_quarters[3]
+    fc_quarters = share(sum_own(grad_fc_mine)).astype(f32)
+    grad_fc_shard = (
+        fc_quarters.reshape(2, 2, shard_rows, shards, shard_rows)
+        .transpose(2, 3, 1, 0, 4)
+        .reshape(shard_rows, FF)
+    )
+    proj_quarters = share(sum_own(grad_proj_mine)).astype(f32)
+    grad_proj_shard = (
+        proj_quarters.reshape(2, 2, shard_rows, D).transpose(1, 0, 2, 3).reshape(4 * shard_rows, D)
+    )
+
+    fc_bias_part = jnp.where(
+        jnp.arange(4)[None, :, None] == rep,
+        jnp.sum(grad_pre_low, axis=0, dtype=f32).reshape(shards, 1, shard_rows),
+        0.0,
+    )
+    sums = [
+        grad_gain_one,
+        grad_shift_one,
+        jnp.concatenate(
+            [jnp.sum(grad_query, axis=0, dtype=f32), jnp.sum(grad_value, axis=0, dtype=f32)]
+        ),
+        jnp.sum(grad_after_low, axis=0, dtype=f32),
+        grad_gain_two,
+        grad_shift_two,
+        fc_bias_part,
+        jnp.sum(cot_low, axis=0, dtype=f32),
+    ]
+    table = jnp.concatenate([item.reshape(shards, -1) for item in sums], axis=1)
+    table = lax.psum(table, ("rep", "dp", "ctx"))
+    mine = lax.dynamic_index_in_dim(table, dp * chips + ctx, 0, keepdims=False)
+    small_out, at = [], 0
+    for item in sums:
+        count = item.size // shards
+        small_out.append(mine[at : at + count])
+        at += count
+    return (
+        block_out,
+        input_grad,
+        small_out[0],
+        small_out[1],
+        grad_qkv_shard,
+        small_out[2],
+        grad_out_shard,
+        small_out[3],
+        small_out[4],
+        small_out[5],
+        grad_fc_shard,
+        small_out[6],
+        grad_proj_shard,
+        small_out[7],
+    )
+
+
+def local(hidden_in, *rest):
+    seqs, block, _ = hidden_in.shape
+    sizes = tuple(lax.axis_size(name) for name in ("rep", "dp", "ctx"))
+    if sizes[:2] == (4, 2) and 2 * seqs == sizes[2] and sizes[2] * block == SEQ and block == PIECE:
+        return sequence_local(hidden_in, *rest)
+    return general_local(hidden_in, *rest)
+
+
 def solution(mesh):
     placed = (
         P(("rep", "dp"), "ctx", None),

time: 4240 us -> 1340 us (0.32)
  waiting for transfers between devices: 3400 us -> 475 us
  matrix products: 406 us -> 202 us
  local copies, waits for them, and re-layouts: 90.6 us -> 294 us
  Pallas kernels: 0 us -> 83.2 us
  other arithmetic: 206 us -> 153 us
    unnamed x15 -> x11, waiting for transfers between devices: 2050 us -> 42.7 us
    all_gather x8 -> x4, waiting for transfers between devices: 1160 us -> 97.2 us  [the longest x2 97.2 us: gather_shared(): mine = lax.all_gather(shard, 'ctx', axis=0, tiled=True)]
    ppermute x0 -> x41, waiting for transfers between devices: none -> 255 us  [the longest x11 138 us: over_x(): return lax.ppermute(value, 'rep', [(0, 2), (2, 0), (1, 3), (3, 1)])]
    dot_general x34 -> x16, matrix products: 406 us -> 202 us  [mxu(): lax.dot_general(left, right, (dims, ((), ())), preferred_element_type=jnp...]
    reduce_scatter x2 -> x0, waiting for transfers between devices: 136 us -> none  [local(): lax.psum_scatter(key_value_term(jnp.int32(0), lax.axis_size('ctx') * row_...]
    concatenate x5 -> x4, other arithmetic: 94.2 us -> 9.07 us  [the longest x2 7.36 us: spread(): chip = jnp.concatenate([value, over_x(value)], axis=0)]
    pallas_call x0 -> x2, Pallas kernels: none -> 83.2 us  [the longest x1 47.9 us: attend_backward(): pl.pallas_call(attend_backward_kernel, grid=(PAIRS,), in_specs=[pl.BlockS...]
    ppermute x0 -> x12, local copies, waits for them, and re-layouts: none -> 46.8 us  [the longest x8 33.4 us: over_core(): return lax.ppermute(value, 'rep', [(0, 1), (1, 0), (2, 3), (3, 2)])]
  transfers between devices with their start and end apart: 13 -> 53, of which waited for: 13 -> 18; matrix products, arithmetic and copies ran while one was open for 11% -> 39% of each run, Pallas kernels for 0% -> 3%
where the time goes in v1:
time: 1340 us
  waiting for transfers between devices  475 us (35%)
  local copies, waits for them, and re-layouts  294 us (22%)
  matrix products  202 us (15%)
  other arithmetic  153 us (11%)
  Pallas kernels  83.2 us (6%)
  blocking collectives  61 us (5%)
  starting transfers between devices  51.7 us (4%)
  between operations  16.6 us (1%)
    dot_general x16, matrix products, mxu(): lax.dot_general(left, right, (dims, ((), ())), preferred_element_type=jnp...  202 us
    ppermute x11, waiting for transfers between devices, over_x(): return lax.ppermute(value, 'rep', [(0, 2), (2, 0), (1, 3), (3, 1)])  138 us
    ppermute x8, waiting for transfers between devices, over_y(): return lax.ppermute(value, 'dp', [(0, 1), (1, 0)])  117 us
    all_gather x2, waiting for transfers between devices, gather_shared(): mine = lax.all_gather(shard, 'ctx', axis=0, tiled=True)  97.2 us
    psum x1, waiting for transfers between devices, sequence_local(): table = lax.psum(table, ('rep', 'dp', 'ctx'))  79.5 us
    unnamed x1, blocking collectives  61 us
    pallas_call x1, Pallas kernels, attend_backward(): pl.pallas_call(attend_backward_kernel, grid=(PAIRS,), in_specs=[pl.BlockS...  47.9 us
    unnamed x11, waiting for transfers between devices  42.7 us
  transfers between devices with their start and end apart: 53, of which 18 were waited for; matrix products, arithmetic and copies ran while one was open for 39% of the time, Pallas kernels for 3%

profile of v1, /device:TPU:0, one launch (start us, length us, event | category | flops | bytes accessed | tf_op | source)
XLA Modules:
  0.0 1336.0 jit_solution(5507230208376352252)
XLA Ops:
  11.1 57.5 %all-gather.9.cloned.1.call-done = bf16[800,1600]{1,0:T(8,128)(2,1)} async-done(((bf16[200,1600]{1,0:T(8,128)(2,1)}), bf16[800,1600]{1,0:T(8,128)(2,1)}) %all-gather.9.cloned.1.call-update) | async-done | bytes 2560016 | tf_op jit(solution)/shard_map/all_gather | solution.py:555
  85.3 39.7 %all-gather.7.cloned.1.call-done = bf16[800,1600]{1,0:T(8,128)(2,1)} async-done(((bf16[200,1600]{1,0:T(8,128)(2,1)}), bf16[800,1600]{1,0:T(8,128)(2,1)}) %all-gather.7.cloned.1.call-update) | async-done | bytes 2560016 | tf_op jit(solution)/shard_map/all_gather | solution.py:555
  130.5 11.6 reshape.506
  170.5 22.6 %collective-permute-done.3 = bf16[400,1600]{1,0:T(8,128)(2,1)S(1)} collective-permute-done((bf16[400,1600]{1,0:T(8,128)(2,1)}, bf16[400,1600]{1,0:T(8,128)(2,1)S(1)}, u32[]{:S(2)}, u32[]{:S(2)}) %collective-permute-start.3) | collective-permute-done | bytes 1280032 | tf_op jit(solution)/shard_map/ppermute | solution.py:336
  204.8 61.0 %all-reduce = bf16[19200]{0:T(1024)(128)(2,1)S(1)} all-reduce(bf16[19200]{0:T(1024)(128)(2,1)S(1)} %dynamic-update-slice), channel_id=2, replica_groups=mesh['rep'=4,'dp'=2,'ctx'=4] {'dp','ctx'}, use_global_device_ids=true, to_apply=%add | all-reduce | flops 19200 | bytes 76800
  288.0 8.1 convolution_convert_fusion.7
  316.1 8.7 reduce-scatter.14.cloned.1.call-start
  347.7 35.3 %attend_forward.1 = (bf16[512,1600]{1,0:T(8,128)(2,1)S(1)}, f32[13,2,512]{2,1,0:T(2,128)S(1)}) custom-call(s32[1,512]{1,0:T(1,128)S(1)} %max.10.limit_ref, bf16[512,1600]{1,0:T(8,128)(2,1)S(1)} %copy-done.5, bf16[1024,1600]{1,0:T(8,128)(2,1)} %bitcast.301, bf16[1600,1024]{1,0:T(8,128)(2,1)} %copy.391.v_t_ref), custom_call_target="tpu_custom_call" | custom-call | flops 3355443200 | bytes 13107200 | tf_op jit(solution)/shard_map/attend_forward/pallas_call | solution.py:444
  403.8 29.8 %collective-permute-done.10 = bf16[512,1600]{0,1:T(8,128)(2,1)} collective-permute-done((bf16[512,1600]{0,1:T(8,128)(2,1)}, bf16[512,1600]{0,1:T(8,128)(2,1)}, u32[]{:S(2)}, u32[]{:S(2)}) %collective-permute-start.10) | collective-permute-done | bytes 1638432 | tf_op jit(solution)/shard_map/ppermute | solution.py:336
  448.5 19.3 %collective-permute-done.18 = bf16[512,1600]{0,1:T(8,128)(2,1)} collective-permute-done((bf16[512,1600]{0,1:T(8,128)(2,1)}, bf16[512,1600]{0,1:T(8,128)(2,1)}, u32[]{:S(2)}, u32[]{:S(2)}) %collective-permute-start.18) | collective-permute-done | bytes 1638432 | tf_op jit(solution)/shard_map/ppermute | solution.py:336
  483.5 29.0 %collective-permute-done.13 = bf16[800,1600]{1,0:T(8,128)(2,1)} collective-permute-done((bf16[800,1600]{1,0:T(8,128)(2,1)}, bf16[800,1600]{1,0:T(8,128)(2,1)}, u32[]{:S(2)}, u32[]{:S(2)}) %collective-permute-start.13) | collective-permute-done | bytes 2560032 | tf_op jit(solution)/shard_map/ppermute | solution.py:340
  519.3 17.4 %fusion.26 = f32[2048,1600]{0,1:T(8,128)} fusion(bf16[1600,1600]{1,0:T(8,128)(2,1)S(1)} %bitcast.325, bf16[1024,1600]{0,1:T(8,128)(2,1)} %collective-permute-done.11, bf16[512,1600]{0,1:T(8,128)(2,1)} %collective-permute-done.10, bf16[512,1600]{0,1:T(8,128)(2,1)} %copy.396), kind=kOutput, calls=%fused_computation.95 | convolution fusion | flops 10505420800 | bytes 24780800 | tf_op jit(solution)/shard_map/dot_general | solution.py:350
  536.7 28.8 %convert_reduce_fusion = (f32[1600]{0:T(1024)}, bf16[2048,1600]{0,1:T(8,128)(2,1)}) fusion(f32[2048,1600]{0,1:T(8,128)} %fusion.26, f32[1600]{0:T(1024)S(1)} %add.388, bf16[1600,1600]{1,0:T(8,128)(2,1)} %bitcast.323, bf16[1024,1600]{0,1:T(8,128)(2,1)} %collective-permute-done.19, bf16[512,1600]{0,1:T(8,128)(2,1)} %collective-permute-done.18, ...), kind=kOutput, calls=%fused_computation.9 | convolution fusion | flops 10577508352 | bytes 31347200 | tf_op jit(solution)/shard_map/dot_general | solution.py:350
  565.5 17.2 %convolution_convert_fusion.2 = bf16[2048,1600]{1,0:T(8,128)(2,1)S(1)} fusion(bf16[2048,1600]{0,1:T(8,128)(2,1)} %get-tuple-element.193, bf16[1600,1600]{1,0:T(8,128)(2,1)} %bitcast.326), kind=kOutput, calls=%fused_computation.15 | convolution fusion | flops 10489036800 | bytes 18227200 | tf_op jit(solution)/shard_map/dot_general | solution.py:350
  593.1 20.8 %convolution_convert_fusion.3 = bf16[2048,1600]{1,0:T(8,128)(2,1)S(1)} fusion(bf16[1600,1600]{1,0:T(8,128)(2,1)} %bitcast.324, f32[2048,1600]{0,1:T(8,128)} %fusion.26, f32[1600]{0:T(1024)S(1)} %add.388), kind=kOutput, calls=%fused_computation.16 | convolution fusion | flops 10521804800 | bytes 24787200 | tf_op jit(solution)/shard_map/dot_general | solution.py:350
  693.7 25.7 %collective-permute-done.15 = bf16[512,1600]{0,1:T(8,128)(2,1)} collective-permute-done((bf16[512,1600]{0,1:T(8,128)(2,1)}, bf16[512,1600]{0,1:T(8,128)(2,1)}, u32[]{:S(2)}, u32[]{:S(2)}) %collective-permute-start.15) | collective-permute-done | bytes 1638432 | tf_op jit(solution)/shard_map/ppermute | solution.py:336
  743.1 47.9 %attend_backward.1 = (bf16[512,1600]{1,0:T(8,128)(2,1)S(1)}, bf16[1024,1600]{1,0:T(8,128)(2,1)}, bf16[1024,1600]{1,0:T(8,128)(2,1)}) custom-call(s32[1,512]{1,0:T(1,128)S(1)} %copy-done.4, bf16[512,1600]{1,0:T(8,128)(2,1)S(1)} %copy-done.6, bf16[1024,1600]{1,0:T(8,128)(2,1)} %bitcast.303, bf16[1600,1024]{1,0:T(8,128)(2,1)} %bitcast.329, ...), custom_call_target="tpu_custom_call" | custom-call | flops 8388608000 | bytes 26214400 | tf_op jit(solution)/shard_map/attend_backward/pallas_call | solution.py:468
  800.7 24.2 %convolution_convert_fusion.4 = bf16[1600,1600]{1,0:T(8,128)(2,1)} fusion(bf16[1024,1600]{0,1:T(8,128)(2,1)} %collective-permute-done.19, bf16[512,1600]{0,1:T(8,128)(2,1)} %collective-permute-done.18, bf16[512,1600]{0,1:T(8,128)(2,1)} %copy.412, f32[2048,1600]{0,1:T(8,128)} %fusion.26, f32[1600]{0:T(1024)S(1)} %add.388), kind=kOutput, calls=%fused_computation.17 | convolution fusion | flops 10540748800 | bytes 24787200 | tf_op jit(solution)/shard_map/dot_general | solution.py:350
  847.4 17.9 %convolution_convert_fusion.5 = bf16[1600,1600]{1,0:T(8,128)(2,1)} fusion(bf16[2048,1600]{0,1:T(8,128)(2,1)} %get-tuple-element.193, bf16[1024,1600]{0,1:T(8,128)(2,1)} %collective-permute-done.11, bf16[512,1600]{0,1:T(8,128)(2,1)} %collective-permute-done.10, bf16[512,1600]{0,1:T(8,128)(2,1)} %copy.396), kind=kOutput, calls=%fused_computation.18 | convolution fusion | flops 10507980800 | bytes 18227200 | tf_op jit(solution)/shard_map/dot_general | solution.py:350
  870.4 18.6 %collective-permute-done.38 = bf16[800,1600]{1,0:T(8,128)(2,1)} collective-permute-done((bf16[800,1600]{1,0:T(8,128)(2,1)}, bf16[800,1600]{1,0:T(8,128)(2,1)}, u32[]{:S(2)}, u32[]{:S(2)}) %collective-permute-start.38) | collective-permute-done | bytes 2560032 | tf_op jit(solution)/shard_map/ppermute | solution.py:340
  916.0 12.1 convolution_convert_fusion
  932.0 8.8 convolution_convert_fusion.1
  945.6 25.4 %collective-permute-done.35 = bf16[800,1600]{1,0:T(8,128)(2,1)} collective-permute-done((bf16[800,1600]{1,0:T(8,128)(2,1)}, bf16[800,1600]{1,0:T(8,128)(2,1)}, u32[]{:S(2)}, u32[]{:S(2)}) %collective-permute-start.35) | collective-permute-done | bytes 2560032 | tf_op jit(solution)/shard_map/ppermute | solution.py:340
  1008.2 32.2 %collective-permute-done.31 = bf16[2,400,1600]{2,1,0:T(8,128)(2,1)} collective-permute-done((bf16[2,400,1600]{2,1,0:T(8,128)(2,1)}, bf16[2,400,1600]{2,1,0:T(8,128)(2,1)}, u32[]{:S(2)}, u32[]{:S(2)}) %collective-permute-start.31) | collective-permute-done | bytes 2560032 | tf_op jit(solution)/shard_map/ppermute | solution.py:340
  1045.8 8.6 multiply_reduce_fusion.1
  1055.5 12.2 collective-permute-done.30
  1094.3 17.4 %collective-permute-done.36 = bf16[200,1600]{1,0:T(8,128)(2,1)} collective-permute-done((bf16[200,1600]{1,0:T(8,128)(2,1)}, bf16[200,1600]{1,0:T(8,128)(2,1)}, u32[]{:S(2)}, u32[]{:S(2)}) %collective-permute-start.36) | collective-permute-done | bytes 640032 | tf_op jit(solution)/shard_map/ppermute | solution.py:336
  1122.8 79.5 %all-reduce.6.cloned.1.call-done = f32[8,2400]{1,0:T(8,128)} async-done(((f32[8,2400]{1,0:T(8,128)}), f32[8,2400]{1,0:T(8,128)}) %all-reduce.6.cloned.1.call-update) | async-done | bytes 76816 | tf_op jit(solution)/shard_map/psum | solution.py:746
  1217.7 41.9 %reduce-scatter.10.cloned.1.call-done = bf16[200,1600]{1,0:T(8,128)(2,1)} async-done(((bf16[800,1600]{1,0:T(8,128)(2,1)}), bf16[200,1600]{1,0:T(8,128)(2,1)}) %reduce-scatter.10.cloned.1.call-update) | async-done | bytes 640016
  1266.6 10.0 collective-permute-done.33
  1283.7 10.6 copy.443
  1294.3 10.7 reshape.542
  (492 shorter events, 508.6 us)
Async XLA Ops:
  7.2 61.4 %all-gather.9.cloned.1.call-start = ((), (), s32[]{:S(2)}) async-start(), calls=%async_computation.8 | async-start | bytes 3328000 | tf_op jit(solution)/shard_map/all_gather | solution.py:555
  10.3 114.8 %all-gather.7.cloned.1.call-start = ((), (), s32[]{:S(2)}) async-start(), calls=%async_computation.7 | async-start | bytes 3328000 | tf_op jit(solution)/shard_map/all_gather | solution.py:555
  11.0 384.7 %all-gather.11.cloned.1.call-start = ((), (), s32[]{:S(2)}) async-start(), calls=%async_computation.9 | async-start | bytes 3328000 | tf_op jit(solution)/shard_map/all_gather | solution.py:563
  71.1 57.9 %collective-permute-start.5 = (bf16[400,1600]{1,0:T(8,128)(2,1)}, bf16[400,1600]{1,0:T(8,128)(2,1)}, u32[]{:S(2)}, u32[]{:S(2)}) collective-permute-start(bf16[400,1600]{1,0:T(8,128)(2,1)} %constant_dynamic-slice_fusion.4), channel_id=1, source_target_pairs={{0,4},{4,0},{1,5},{5,1},{2,6},{6,2},{3,7},{7,3},{8,12},{12,8},{9,1... | collective-permute-start | bytes 3840008 | tf_op jit(solution)/shard_map/ppermute | solution.py:340
  85.3 69.6 %collective-permute-start = (bf16[2,128,1600]{1,2,0:T(8,128)(2,1)}, bf16[2,128,1600]{1,2,0:T(8,128)(2,1)}, u32[]{:S(2)}, u32[]{:S(2)}) collective-permute-start(bf16[2,128,1600]{1,2,0:T(8,128)(2,1)} %bitcast.333), channel_id=1, source_target_pairs={{0,8},{8,0},{16,24},{24,16},{1,9},{9,1},{17,25},{25,17},{2,10},{10... | collective-permute-start | bytes 2457608 | tf_op jit(solution)/shard_map/ppermute | solution.py:332
  157.8 110.5 %all-to-all-start = ((bf16[4,128,1600]{1,2,0:T(8,128)(2,1)}), bf16[4,128,1600]{1,2,0:T(8,128)(2,1)}, u32[]{:S(2)}, u32[]{:S(2)}) async-start(bf16[4,128,1600]{1,2,0:T(8,128)(2,1)} %bitcast.317), calls=%async_computation | async-start | bytes 3276800 | tf_op jit(solution)/shard_map/all_to_all | solution.py:529
  162.2 240.7 %all-gather.13.cloned.1.call-start = ((), (), s32[]{:S(2)}) async-start(), calls=%async_computation.11 | async-start | bytes 3328000 | tf_op jit(solution)/shard_map/all_gather | solution.py:563
  170.5 117.5 %collective-permute-start.7 = (bf16[1600,1600]{1,0:T(8,128)(2,1)}, bf16[1600,1600]{1,0:T(8,128)(2,1)}, u32[]{:S(2)}, u32[]{:S(2)}) collective-permute-start(bf16[1600,1600]{1,0:T(8,128)(2,1)} %bitcast.28), channel_id=1, source_target_pairs={{0,8},{8,0},{16,24},{24,16},{1,9},{9,1},{17,25},{25,17},{2,10},{10... | collective-permute-start | bytes 15360008 | tf_op jit(solution)/shard_map/ppermute | solution.py:332
  200.3 95.9 %collective-permute-start.4 = (bf16[1600,1600]{1,0:T(8,128)(2,1)}, bf16[1600,1600]{1,0:T(8,128)(2,1)}, u32[]{:S(2)}, u32[]{:S(2)}) collective-permute-start(bf16[1600,1600]{1,0:T(8,128)(2,1)} %bitcast.20), channel_id=1, source_target_pairs={{0,8},{8,0},{16,24},{24,16},{1,9},{9,1},{17,25},{25,17},{2,10},{10... | collective-permute-start | bytes 15360008 | tf_op jit(solution)/shard_map/ppermute | solution.py:332
  200.3 107.8 %collective-permute-start.1 = (s32[2,2]{1,0:T(2,128)}, s32[2,2]{1,0:T(2,128)}, u32[]{:S(2)}, u32[]{:S(2)}) collective-permute-start(s32[2,2]{1,0:T(2,128)} %param.16), channel_id=1, source_target_pairs={{0,8},{8,0},{16,24},{24,16},{1,9},{9,1},{17,25},{25,17},{2,10},{10... | collective-permute-start | bytes 56 | tf_op jit(solution)/shard_map/ppermute | solution.py:332
  202.1 107.1 %collective-permute-start.17 = (bf16[2,128,1600]{1,2,0:T(8,128)(2,1)}, bf16[2,128,1600]{1,2,0:T(8,128)(2,1)}, u32[]{:S(2)}, u32[]{:S(2)}) collective-permute-start(bf16[2,128,1600]{1,2,0:T(8,128)(2,1)} %bitcast.332), channel_id=1, source_target_pairs={{0,8},{8,0},{16,24},{24,16},{1,9},{9,1},{17,25},{25,17},{2,10},{10... | collective-permute-start | bytes 2457608 | tf_op jit(solution)/shard_map/ppermute | solution.py:332
  311.7 85.8 %all-to-all-start.2 = ((bf16[4,128,1600]{1,2,0:T(8,128)(2,1)}), bf16[4,128,1600]{1,2,0:T(8,128)(2,1)}, u32[]{:S(2)}, u32[]{:S(2)}) async-start(bf16[4,128,1600]{1,2,0:T(8,128)(2,1)} %bitcast.56), calls=%async_computation.2 | async-start | bytes 3276800 | tf_op jit(solution)/shard_map/all_to_all | solution.py:529
  316.1 763.4 %reduce-scatter.14.cloned.1.call-start = ((), (), s32[]{:S(2)}) async-start(), calls=%async_computation.14 | async-start | bytes 3328000
  395.7 84.6 %collective-permute-start.12 = (bf16[800,1600]{1,0:T(8,128)(2,1)}, bf16[800,1600]{1,0:T(8,128)(2,1)}, u32[]{:S(2)}, u32[]{:S(2)}) collective-permute-start(bf16[800,1600]{1,0:T(8,128)(2,1)} %all-gather.11.cloned.1.call-done), channel_id=1, source_target_pairs={{0,4},{4,0},{1,5},{5,1},{2,6},{6,2},{3,7},{7,3},{8,12},{12,8},{9,1... | collective-permute-start | bytes 7680008 | tf_op jit(solution)/shard_map/ppermute | solution.py:340
  402.6 65.1 %collective-permute-start.18 = (bf16[512,1600]{0,1:T(8,128)(2,1)}, bf16[512,1600]{0,1:T(8,128)(2,1)}, u32[]{:S(2)}, u32[]{:S(2)}) collective-permute-start(bf16[512,1600]{0,1:T(8,128)(2,1)} %copy.412), channel_id=1, source_target_pairs={{0,16},{16,0},{8,24},{24,8},{1,17},{17,1},{9,25},{25,9},{2,18},{18... | collective-permute-start | bytes 4915208 | tf_op jit(solution)/shard_map/ppermute | solution.py:336
  402.8 109.7 %collective-permute-start.13 = (bf16[800,1600]{1,0:T(8,128)(2,1)}, bf16[800,1600]{1,0:T(8,128)(2,1)}, u32[]{:S(2)}, u32[]{:S(2)}) collective-permute-start(bf16[800,1600]{1,0:T(8,128)(2,1)} %bitcast.330), channel_id=1, source_target_pairs={{0,4},{4,0},{1,5},{5,1},{2,6},{6,2},{3,7},{7,3},{8,12},{12,8},{9,1... | collective-permute-start | bytes 7680008 | tf_op jit(solution)/shard_map/ppermute | solution.py:340
  446.8 71.9 %collective-permute-start.11 = (bf16[1024,1600]{0,1:T(8,128)(2,1)}, bf16[1024,1600]{0,1:T(8,128)(2,1)}, u32[]{:S(2)}, u32[]{:S(2)}) collective-permute-start(bf16[1024,1600]{0,1:T(8,128)(2,1)} %copy.395), channel_id=1, source_target_pairs={{0,8},{8,0},{16,24},{24,16},{1,9},{9,1},{17,25},{25,17},{2,10},{10... | collective-permute-start | bytes 9830408 | tf_op jit(solution)/shard_map/ppermute | solution.py:332
  480.3 56.5 %collective-permute-start.19 = (bf16[1024,1600]{0,1:T(8,128)(2,1)}, bf16[1024,1600]{0,1:T(8,128)(2,1)}, u32[]{:S(2)}, u32[]{:S(2)}) collective-permute-start(bf16[1024,1600]{0,1:T(8,128)(2,1)} %copy.411), channel_id=1, source_target_pairs={{0,8},{8,0},{16,24},{24,16},{1,9},{9,1},{17,25},{25,17},{2,10},{10... | collective-permute-start | bytes 9830408 | tf_op jit(solution)/shard_map/ppermute | solution.py:332
  662.1 57.4 %collective-permute-start.15 = (bf16[512,1600]{0,1:T(8,128)(2,1)}, bf16[512,1600]{0,1:T(8,128)(2,1)}, u32[]{:S(2)}, u32[]{:S(2)}) collective-permute-start(bf16[512,1600]{0,1:T(8,128)(2,1)} %copy.401), channel_id=1, source_target_pairs={{0,16},{16,0},{8,24},{24,8},{1,17},{17,1},{9,25},{25,9},{2,18},{18... | collective-permute-start | bytes 4915208 | tf_op jit(solution)/shard_map/ppermute | solution.py:336
  828.5 60.5 %collective-permute-start.38 = (bf16[800,1600]{1,0:T(8,128)(2,1)}, bf16[800,1600]{1,0:T(8,128)(2,1)}, u32[]{:S(2)}, u32[]{:S(2)}) collective-permute-start(bf16[800,1600]{1,0:T(8,128)(2,1)} %dynamic-slice_bitcast_fusion), channel_id=1, source_target_pairs={{0,4},{4,0},{1,5},{5,1},{2,6},{6,2},{3,7},{7,3},{8,12},{12,8},{9,1... | collective-permute-start | bytes 7680008 | tf_op jit(solution)/shard_map/ppermute | solution.py:340
  846.7 47.1 %collective-permute-start.22 = (bf16[512,1600]{0,1:T(8,128)(2,1)}, bf16[512,1600]{0,1:T(8,128)(2,1)}, u32[]{:S(2)}, u32[]{:S(2)}) collective-permute-start(bf16[512,1600]{0,1:T(8,128)(2,1)} %copy.422), channel_id=1, source_target_pairs={{0,8},{8,0},{16,24},{24,16},{1,9},{9,1},{17,25},{25,17},{2,10},{10... | collective-permute-start | bytes 4915208 | tf_op jit(solution)/shard_map/ppermute | solution.py:332
  893.8 186.5 %reduce-scatter.12.cloned.1.call-start = ((), (), s32[]{:S(2)}) async-start(), calls=%async_computation.13 | async-start | bytes 3328000
  910.5 60.5 %collective-permute-start.35 = (bf16[800,1600]{1,0:T(8,128)(2,1)}, bf16[800,1600]{1,0:T(8,128)(2,1)}, u32[]{:S(2)}, u32[]{:S(2)}) collective-permute-start(bf16[800,1600]{1,0:T(8,128)(2,1)} %dynamic-slice_bitcast_fusion.1), channel_id=1, source_target_pairs={{0,4},{4,0},{1,5},{5,1},{2,6},{6,2},{3,7},{7,3},{8,12},{12,8},{9,1... | collective-permute-start | bytes 7680008 | tf_op jit(solution)/shard_map/ppermute | solution.py:340
  943.9 60.2 %collective-permute-start.29 = (bf16[2,400,1600]{2,1,0:T(8,128)(2,1)}, bf16[2,400,1600]{2,1,0:T(8,128)(2,1)}, u32[]{:S(2)}, u32[]{:S(2)}) collective-permute-start(bf16[2,400,1600]{2,1,0:T(8,128)(2,1)} %dynamic-slice_bitcast_fusion.2), channel_id=1, source_target_pairs={{0,16},{16,0},{8,24},{24,8},{1,17},{17,1},{9,25},{25,9},{2,18},{18... | collective-permute-start | bytes 7680008 | tf_op jit(solution)/shard_map/ppermute | solution.py:336
  979.5 61.0 %collective-permute-start.31 = (bf16[2,400,1600]{2,1,0:T(8,128)(2,1)}, bf16[2,400,1600]{2,1,0:T(8,128)(2,1)}, u32[]{:S(2)}, u32[]{:S(2)}) collective-permute-start(bf16[2,400,1600]{2,1,0:T(8,128)(2,1)} %fusion.28), channel_id=1, source_target_pairs={{0,4},{4,0},{1,5},{5,1},{2,6},{6,2},{3,7},{7,3},{8,12},{12,8},{9,1... | collective-permute-start | bytes 7680008 | tf_op jit(solution)/shard_map/ppermute | solution.py:340
  984.2 93.2 %all-to-all-start.1 = ((bf16[4,128,1600]{1,2,0:T(8,128)(2,1)}), bf16[4,128,1600]{1,2,0:T(8,128)(2,1)}, u32[]{:S(2)}, u32[]{:S(2)}) async-start(bf16[4,128,1600]{1,2,0:T(8,128)(2,1)} %copy.403), calls=%async_computation.1 | async-start | bytes 3276800 | tf_op jit(solution)/shard_map/all_to_all | solution.py:532
  988.6 213.7 %all-reduce.6.cloned.1.call-start = ((), (), s32[]{:S(2)}) async-start(), calls=%async_computation.10 | async-start | bytes 155648 | tf_op jit(solution)/shard_map/psum | solution.py:746
  1007.8 59.9 %collective-permute-start.30 = (bf16[400,1600]{1,0:T(8,128)(2,1)}, bf16[400,1600]{1,0:T(8,128)(2,1)}, u32[]{:S(2)}, u32[]{:S(2)}) collective-permute-start(bf16[400,1600]{1,0:T(8,128)(2,1)} %dynamic-slice_bitcast_fusion.4), channel_id=1, source_target_pairs={{0,4},{4,0},{1,5},{5,1},{2,6},{6,2},{3,7},{7,3},{8,12},{12,8},{9,1... | collective-permute-start | bytes 3840008 | tf_op jit(solution)/shard_map/ppermute | solution.py:340
  1055.4 204.2 %reduce-scatter.10.cloned.1.call-start = ((), (), s32[]{:S(2)}) async-start(), calls=%async_computation.12 | async-start | bytes 3328000
  1089.8 174.7 %all-to-all-start.3 = ((bf16[4,128,1600]{1,2,0:T(8,128)(2,1)}), bf16[4,128,1600]{1,2,0:T(8,128)(2,1)}, u32[]{:S(2)}, u32[]{:S(2)}) async-start(bf16[4,128,1600]{1,2,0:T(8,128)(2,1)} %copy.431), calls=%async_computation.3 | async-start | bytes 3276800 | tf_op jit(solution)/shard_map/all_to_all | solution.py:532
  1114.3 92.3 %collective-permute-start.37 = (bf16[2,200,1600]{2,1,0:T(8,128)(2,1)}, bf16[2,200,1600]{2,1,0:T(8,128)(2,1)}, u32[]{:S(2)}, u32[]{:S(2)}) collective-permute-start(bf16[2,200,1600]{2,1,0:T(8,128)(2,1)} %pad_maximum_fusion.24), channel_id=1, source_target_pairs={{0,8},{8,0},{16,24},{24,16},{1,9},{9,1},{17,25},{25,17},{2,10},{10... | collective-permute-start | bytes 3840008 | tf_op jit(solution)/shard_map/ppermute | solution.py:332
  1117.0 144.0 %collective-permute-start.40 = (bf16[2,200,1600]{2,1,0:T(8,128)(2,1)}, bf16[2,200,1600]{2,1,0:T(8,128)(2,1)}, u32[]{:S(2)}, u32[]{:S(2)}) collective-permute-start(bf16[2,200,1600]{2,1,0:T(8,128)(2,1)} %pad_maximum_fusion.25), channel_id=1, source_target_pairs={{0,8},{8,0},{16,24},{24,16},{1,9},{9,1},{17,25},{25,17},{2,10},{10... | collective-permute-start | bytes 3840008 | tf_op jit(solution)/shard_map/ppermute | solution.py:332
  (115 other events, 2292.6 us)
Sparse Core Ops, SparseCore 0:
  10.4 58.1 all-gather.8
  70.7 54.2 all-gather.6
  152.9 87.7 all-gather.10
  242.1 54.5 all-gather.12
  893.9 52.5 reduce-scatter.13
  975.9 82.2 reduce-scatter.11
  1063.8 138.4 all-reduce.5
  1205.2 54.3 reduce-scatter.9

commit v2 on v0

--- a/solution.py
+++ b/solution.py
@@ -1,6 +1,8 @@
 import jax
 import jax.numpy as jnp
 from jax import lax
+from jax.experimental import pallas as pl
+from jax.experimental.pallas import tpu as pltpu
 from jax.sharding import PartitionSpec as P
 
 D = 1600
@@ -61,7 +63,7 @@
     return jnp.where(allowed[None], scores, MASKED)
 
 
-def local(
+def general_local(
     hidden_in,
     piece_starts,
     grad_out,
@@ -323,6 +325,1087 @@
     )
 
 
+LANES = 128
+SUBLANES = 8
+GRANT = 58 << 20
+NO_COST = pl.CostEstimate(flops=1, transcendentals=0, bytes_accessed=1)
+
+
+def permuted(value, axis, pairs):
+    if value.ndim < 2 or value.shape[-2] % SUBLANES:
+        return lax.ppermute(value, axis, pairs)
+    rows = value.reshape(-1, SUBLANES, value.shape[-1])
+    return lax.ppermute(rows, axis, pairs).reshape(value.shape)
+
+
+def over_core(value):
+    return permuted(value, "rep", [(0, 1), (1, 0), (2, 3), (3, 2)])
+
+
+def over_x(value):
+    return permuted(value, "rep", [(0, 2), (2, 0), (1, 3), (3, 1)])
+
+
+def over_y(value):
+    return permuted(value, "dp", [(0, 1), (1, 0)])
+
+
+def ordered(first_is_mine, mine, other):
+    return jnp.stack(
+        [jnp.where(first_is_mine, mine, other), jnp.where(first_is_mine, other, mine)]
+    )
+
+
+def mxu(left, right, dims=((1,), (0,))):
+    return lax.dot_general(left, right, (dims, ((), ())), preferred_element_type=jnp.float32)
+
+
+def after(value, *others):
+    return lax.optimization_barrier((value, *others))[0]
+
+
+def half_rows(index, core, half):
+    mine = (core + index) % 2
+    start = 2 * half * index
+    return (
+        pl.ds(pl.multiple_of(start + half * mine, half), half),
+        pl.ds(pl.multiple_of(start + half * (1 - mine), half), half),
+    )
+
+
+def in_sequence(core, valid, mine_ref, other_ref, whole):
+    half = mine_ref.shape[0] // CHUNKS
+    for index in range(CHUNKS):
+        mine, other = half_rows(index, core, half)
+        rows = slice(index * half, (index + 1) * half)
+        whole[mine, :] = jnp.where(valid, mine_ref[rows, :], 0)
+        whole[other, :] = jnp.where(valid, other_ref[rows, :], 0)
+
+
+def masked_scores(keys, queries, first, count, limit):
+    scores = mxu(keys[:count], queries, ((1,), (1,)))
+    position = first + lax.broadcasted_iota(jnp.int32, (count - first, queries.shape[0]), 0)
+    tail = jnp.where(position < limit, scores[first:], MASKED)
+    return tail if first == 0 else jnp.concatenate([scores[:first], tail], axis=0)
+
+
+def attend_forward_kernel(
+    core_ref, limit_ref, q_ref, k_ref, k_other_ref, v_ref, v_other_ref, o_ref, lse_ref, k_all, v_all
+):
+    pair = pl.program_id(0)
+    width = q_ref.shape[0] // 2
+    lane = lax.broadcasted_iota(jnp.int32, (1, LANES), 1)
+    valid = lane < D - pair * LANES
+    queries = jnp.where(valid, q_ref[...], 0) * jnp.asarray(HD ** (-0.5), q_ref.dtype)
+    in_sequence(core_ref[0], valid, k_ref, k_other_ref, k_all)
+    in_sequence(core_ref[0], valid, v_ref, v_other_ref, v_all)
+    keys = k_all[...]
+    values_t = v_all[...].T
+    for part in range(2):
+        rows = slice(part * width, (part + 1) * width)
+        first, count = KEY_SPANS[part]
+        mixed = []
+        for head in range(2):
+            own = (lane >= head * HD) & (lane < (head + 1) * HD)
+            scores = masked_scores(
+                keys, jnp.where(own, queries[rows], 0), first, count, limit_ref[:, rows]
+            )
+            top = jnp.max(scores, axis=0, keepdims=True)
+            expo = jnp.exp(scores - top)
+            total = jnp.sum(expo, axis=0, keepdims=True)
+            values = values_t[head * HD : (head + 1) * HD, :count]
+            mixed.append(mxu(values, expo.astype(jnp.bfloat16)) / total)
+            lse_ref[0, head : head + 1, rows] = top + jnp.log(total)
+        o_ref[rows, :] = jnp.concatenate(mixed, axis=0).T.astype(o_ref.dtype)
+
+
+def attend_backward_kernel(
+    start,
+    core_ref,
+    limit_ref,
+    q_ref,
+    k_ref,
+    k_other_ref,
+    v_ref,
+    v_other_ref,
+    grad_ref,
+    after_ref,
+    lse_ref,
+    dq_ref,
+    dk_ref,
+    dk_other_ref,
+    dv_ref,
+    dv_other_ref,
+    send_a_ref,
+    send_b_ref,
+    k_all,
+    v_all,
+    dk_sum,
+    dv_sum,
+):
+    pair = pl.program_id(0) + start
+    width = q_ref.shape[0] // 2
+    lane = lax.broadcasted_iota(jnp.int32, (1, LANES), 1)
+    valid = lane < D - pair * LANES
+    queries = jnp.where(valid, q_ref[...], 0) * jnp.asarray(HD ** (-0.5), q_ref.dtype)
+    grads = jnp.where(valid, grad_ref[...], 0)
+    core = core_ref[0]
+    in_sequence(core, valid, k_ref, k_other_ref, k_all)
+    in_sequence(core, valid, v_ref, v_other_ref, v_all)
+    keys = k_all[...]
+    keys_t = keys.T
+    values = v_all[...]
+    for part in (1, 0):
+        rows = slice(part * width, (part + 1) * width)
+        first, count = KEY_SPANS[part]
+        grad_q, grad_k, grad_v = [], 0.0, 0.0
+        for head in range(2):
+            own = (lane >= head * HD) & (lane < (head + 1) * HD)
+            queries_own = jnp.where(own, queries[rows], 0)
+            grads_own = jnp.where(own, grads[rows], 0)
+            scores = masked_scores(keys, queries_own, first, count, limit_ref[:, rows])
+            probs = jnp.exp(scores - lse_ref[0, head : head + 1, rows])
+            grad_probs = mxu(values[:count], grads_own, ((1,), (1,)))
+            inner = jnp.sum(probs * grad_probs, axis=0, keepdims=True)
+            grad_scores = (probs * (grad_probs - inner)).astype(jnp.bfloat16)
+            grad_q.append(mxu(keys_t[head * HD : (head + 1) * HD, :count], grad_scores))
+            grad_k += mxu(grad_scores, queries_own)
+            grad_v += mxu(probs.astype(jnp.bfloat16), grads_own)
+        grad_q = jnp.concatenate(grad_q, axis=0) * HD ** (-0.5)
+        dq_ref[rows, :] = grad_q.T.astype(dq_ref.dtype)
+        if part == 1:
+            dk_sum[...] = grad_k
+            dv_sum[...] = grad_v
+        else:
+            dk_sum[:count, :] += grad_k
+            dv_sum[:count, :] += grad_v
+    half = dk_ref.shape[0] // CHUNKS
+    for index in range(CHUNKS):
+        mine, other = half_rows(index, core, half)
+        at = slice(index * half, (index + 1) * half)
+        dk_ref[at, :] = dk_sum[mine, :].astype(dk_ref.dtype)
+        dk_other_ref[at, :] = dk_sum[other, :].astype(dk_ref.dtype)
+        dv_ref[at, :] = dv_sum[mine, :].astype(dv_ref.dtype)
+        dv_other_ref[at, :] = dv_sum[other, :].astype(dv_ref.dtype)
+
+    @pl.when(core == 0)
+    def _():
+        send_a_ref[...] = dv_ref[...]
+        send_b_ref[...] = after_ref[...]
+
+    @pl.when(core == 1)
+    def _():
+        send_a_ref[...] = dq_ref[...]
+        send_b_ref[...] = dk_ref[...]
+
+
+CHUNKS = SEQ // PIECE
+PAIRS = -(-D // LANES)
+GROUPS = ((0, 7), (7, PAIRS))
+KEY_SPANS = ((0, 640), (512, 1024))
+
+
+def by_columns(rows, start=0):
+    return pl.BlockSpec((rows, LANES), lambda pair: (0, pair + start))
+
+
+def attend_forward(core, limit, q, k, k_other, v, v_other):
+    rows = q.shape[0]
+    return pl.pallas_call(
+        attend_forward_kernel,
+        grid=(PAIRS,),
+        in_specs=[
+            pl.BlockSpec(memory_space=pltpu.SMEM),
+            pl.BlockSpec((1, rows), lambda pair: (0, 0)),
+        ]
+        + [by_columns(rows)] * 5,
+        out_specs=[by_columns(rows), pl.BlockSpec((1, 2, rows), lambda pair: (pair, 0, 0))],
+        out_shape=[
+            jax.ShapeDtypeStruct((rows, D), jnp.bfloat16),
+            jax.ShapeDtypeStruct((PAIRS, 2, rows), jnp.float32),
+        ],
+        scratch_shapes=[pltpu.VMEM((2 * rows, LANES), jnp.bfloat16)] * 2,
+        cost_estimate=NO_COST,
+        compiler_params=pltpu.CompilerParams(vmem_limit_bytes=GRANT),
+        name="attend_forward",
+    )(core, limit, q, k, k_other, v, v_other)
+
+
+def attend_backward(group, core, limit, q, k, k_other, v, v_other, grad, grad_after, lse):
+    rows = q.shape[0]
+    start, stop = group
+    columns = min(D, stop * LANES) - start * LANES
+    return pl.pallas_call(
+        lambda *refs: attend_backward_kernel(start, *refs),
+        grid=(stop - start,),
+        in_specs=[
+            pl.BlockSpec(memory_space=pltpu.SMEM),
+            pl.BlockSpec((1, rows), lambda pair: (0, 0)),
+        ]
+        + [by_columns(rows, start)] * 7
+        + [pl.BlockSpec((1, 2, rows), lambda pair: (pair + start, 0, 0))],
+        out_specs=[by_columns(rows)] * 7,
+        out_shape=[jax.ShapeDtypeStruct((rows, columns), jnp.bfloat16)] * 7,
+        scratch_shapes=[pltpu.VMEM((2 * rows, LANES), jnp.bfloat16)] * 2
+        + [pltpu.VMEM((2 * rows, LANES), jnp.float32)] * 2,
+        cost_estimate=NO_COST,
+        compiler_params=pltpu.CompilerParams(vmem_limit_bytes=GRANT),
+        name="attend_backward",
+    )(core, limit, q, k, k_other, v, v_other, grad, grad_after, lse)
+
+
+def weight_gradient_kernel(count, place_ref, *refs):
+    lefts, rights = list(refs[:count]), list(refs[count:-3])
+    send_ref, keep_ref, whole = refs[-3:]
+    block = lefts[0].shape[1]
+    total, left_at, right_at = 0.0, 0, 0
+    while lefts:
+        rows = min(lefts[0].shape[0] - left_at, rights[0].shape[0] - right_at)
+        left = lefts[0][left_at : left_at + rows, :]
+        total += mxu(left, rights[0][right_at : right_at + rows, :], ((0,), (0,)))
+        left_at, right_at = left_at + rows, right_at + rows
+        if left_at == lefts[0].shape[0]:
+            lefts, left_at = lefts[1:], 0
+        if right_at == rights[0].shape[0]:
+            rights, right_at = rights[1:], 0
+    step = pl.program_id(0)
+    whole[pl.ds(pl.multiple_of(step * block, block), block), :] = total.astype(whole.dtype)
+
+    @pl.when(step == pl.num_programs(0) - 1)
+    def _():
+        rows, dp = send_ref.shape[0], place_ref[1]
+        send_ref[...] = whole[pl.ds(pl.multiple_of((1 - dp) * rows, rows), rows), :]
+        keep_ref[...] = whole[pl.ds(pl.multiple_of(dp * rows, rows), rows), :]
+
+
+def weight_gradient(place, lefts, rights, block=256):
+    inner, outer = lefts[0].shape[1], rights[0].shape[1]
+    steps = pl.cdiv(inner, block)
+    return pl.pallas_call(
+        lambda *refs: weight_gradient_kernel(len(lefts), *refs),
+        grid=(steps,),
+        in_specs=[pl.BlockSpec(memory_space=pltpu.SMEM)]
+        + [pl.BlockSpec((left.shape[0], block), lambda i: (0, i)) for left in lefts]
+        + [
+            pl.BlockSpec(right.shape, lambda i: (0, 0), pipeline_mode=pl.Buffered(1))
+            for right in rights
+        ],
+        out_specs=[pl.BlockSpec((inner // 2, outer), lambda i: (0, 0))] * 2,
+        out_shape=[jax.ShapeDtypeStruct((inner // 2, outer), jnp.bfloat16)] * 2,
+        scratch_shapes=[pltpu.VMEM((steps * block, outer), jnp.bfloat16)],
+        cost_estimate=NO_COST,
+        compiler_params=pltpu.CompilerParams(vmem_limit_bytes=GRANT),
+        name="weight_gradient",
+    )(place, *lefts, *rights)
+
+
+def pair_sum_kernel(first_ref, second_ref, out_ref):
+    total = first_ref[...].astype(jnp.float32) + second_ref[...].astype(jnp.float32)
+    out_ref[...] = total.astype(out_ref.dtype)
+
+
+def pair_sum(first, second, block=200):
+    spec = pl.BlockSpec((block, first.shape[1]), lambda i: (i, 0))
+    return pl.pallas_call(
+        pair_sum_kernel,
+        grid=(first.shape[0] // block,),
+        in_specs=[spec, spec],
+        out_specs=spec,
+        out_shape=jax.ShapeDtypeStruct(first.shape, first.dtype),
+        cost_estimate=NO_COST,
+        compiler_params=pltpu.CompilerParams(vmem_limit_bytes=GRANT),
+        name="pair_sum",
+    )(first, second)
+
+
+def second_terms_kernel(place_ref, *refs):
+    came_x, came_y, kept_x, kept_y, send_x, send_y, stay_x, stay_y = refs
+    dp, chip_x = place_ref[1], place_ref[0] // 2
+    f32 = jnp.float32
+    for kept, came, own, send, stay in (
+        (kept_x, came_x, dp, send_x, stay_x),
+        (kept_y, came_y, chip_x, send_y, stay_y),
+    ):
+        send[...] = (kept[1 - own].astype(f32) + came[1 - own].astype(f32)).astype(send.dtype)
+        stay[...] = (kept[own].astype(f32) + came[own].astype(f32)).astype(send.dtype)
+
+
+def second_terms(place, came_x, came_y, kept_x, kept_y):
+    shape = jax.ShapeDtypeStruct(came_x.shape[1:], came_x.dtype)
+    return pl.pallas_call(
+        second_terms_kernel,
+        in_specs=[pl.BlockSpec(memory_space=pltpu.SMEM)]
+        + [pl.BlockSpec(memory_space=pltpu.VMEM)] * 4,
+        out_specs=[pl.BlockSpec(memory_space=pltpu.VMEM)] * 4,
+        out_shape=[shape] * 4,
+        cost_estimate=NO_COST,
+        compiler_params=pltpu.CompilerParams(vmem_limit_bytes=GRANT),
+        name="second_terms",
+    )(place, came_x, came_y, kept_x, kept_y)
+
+
+def summed_kernel(came_x, came_y, stay_x, stay_y, out_ref):
+    rows = stay_x.shape[0]
+    f32 = jnp.float32
+    out_ref[:rows, :] = (stay_x[...].astype(f32) + came_x[...].astype(f32)).astype(out_ref.dtype)
+    out_ref[rows:, :] = (stay_y[...].astype(f32) + came_y[...].astype(f32)).astype(out_ref.dtype)
+
+
+def summed(came_x, came_y, stay_x, stay_y):
+    rows, width = stay_x.shape
+    return pl.pallas_call(
+        summed_kernel,
+        in_specs=[pl.BlockSpec(memory_space=pltpu.VMEM)] * 4,
+        out_specs=pl.BlockSpec(memory_space=pltpu.VMEM),
+        out_shape=jax.ShapeDtypeStruct((2 * rows, width), stay_x.dtype),
+        cost_estimate=NO_COST,
+        compiler_params=pltpu.CompilerParams(vmem_limit_bytes=GRANT),
+        name="summed",
+    )(came_x, came_y, stay_x, stay_y)
+
+
+def block_value_kernel(after_ref, own_ref, core_ref, far_ref, bias_ref, out_ref):
+    f32 = jnp.float32
+    value = after_ref[...] + own_ref[...].astype(f32) + core_ref[...].astype(f32)
+    out_ref[...] = (value + far_ref[...].astype(f32) + bias_ref[...]).astype(out_ref.dtype)
+
+
+def block_value_of(after_attn, own, core, far, bias, block=128):
+    spec = pl.BlockSpec((block, D), lambda i: (i, 0))
+    return pl.pallas_call(
+        block_value_kernel,
+        grid=(own.shape[0] // block,),
+        in_specs=[spec] * 4 + [pl.BlockSpec((1, D), lambda i: (0, 0))],
+        out_specs=spec,
+        out_shape=jax.ShapeDtypeStruct(own.shape, jnp.bfloat16),
+        cost_estimate=NO_COST,
+        compiler_params=pltpu.CompilerParams(vmem_limit_bytes=GRANT),
+        name="block_value",
+    )(after_attn, own, core, far, bias)
+
+
+def attention_weights_kernel(
+    place_ref,
+    hidden_ref,
+    hidden_other_ref,
+    left_ref,
+    left_other_ref,
+    dq_ref,
+    dk_ref,
+    dk_other_ref,
+    dv_ref,
+    dv_other_ref,
+    after_ref,
+    key_came_ref,
+    value_came_ref,
+    came_a_ref,
+    came_b_ref,
+    send_x_ref,
+    keep_x_ref,
+    send_y_ref,
+    keep_y_ref,
+    right,
+    terms,
+):
+    rep, dp = place_ref[0], place_ref[1]
+    chip_x, core = rep // 2, rep % 2
+    rows, width = dq_ref.shape
+    low, f32 = jnp.bfloat16, jnp.float32
+    own, other = slice(0, rows), slice(rows, 2 * rows)
+    add = lambda first, second: (first[...].astype(f32) + second[...].astype(f32)).astype(low)
+
+    @pl.when(core == 0)
+    def _():
+        right[0, own, :] = dq_ref[...]
+        right[0, other, :] = came_a_ref[...]
+        right[1, own, :] = add(dk_ref, key_came_ref)
+        right[1, other, :] = add(dk_other_ref, came_b_ref)
+
+    @pl.when(core == 1)
+    def _():
+        right[0, own, :] = add(dv_ref, value_came_ref)
+        right[0, other, :] = add(dv_other_ref, came_a_ref)
+        right[1, own, :] = after_ref[:, :width]
+        right[1, other, :] = came_b_ref[...]
+
+    for index, lefts in enumerate(((hidden_ref, hidden_other_ref), (left_ref, left_other_ref))):
+        for at in range(0, D, 256):
+            columns = slice(at, min(D, at + 256))
+            term = mxu(lefts[0][:, columns], right[index, own, :], ((0,), (0,)))
+            term += mxu(lefts[1][:, columns], right[index, other, :], ((0,), (0,)))
+            terms[index, columns, :] = term.astype(low)
+    quarter = D // 4
+    for side in range(2):
+        part = pl.ds(2 * side * quarter, quarter)
+        send_x_ref[side] = terms[1 - chip_x, part, :]
+        keep_x_ref[side] = terms[chip_x, part, :]
+    for index in range(2):
+        start = lambda at: pl.ds(pl.multiple_of((2 * at + 1) * quarter, quarter), quarter)
+        send_y_ref[index] = terms[index, start(1 - dp), :]
+        keep_y_ref[index] = terms[index, start(dp), :]
+
+
+def attention_weights(place, hidden, hidden_other, left, left_other, grads, came):
+    rows, width = grads[0].shape
+    shape = jax.ShapeDtypeStruct((2, D // 4, width), jnp.bfloat16)
+    arrays = [hidden, hidden_other, left, left_other, *grads, *came]
+    return pl.pallas_call(
+        attention_weights_kernel,
+        in_specs=[pl.BlockSpec(memory_space=pltpu.SMEM)]
+        + [pl.BlockSpec(memory_space=pltpu.VMEM)] * len(arrays),
+        out_specs=[pl.BlockSpec(memory_space=pltpu.VMEM)] * 4,
+        out_shape=[shape] * 4,
+        scratch_shapes=[
+            pltpu.VMEM((2, 2 * rows, width), jnp.bfloat16),
+            pltpu.VMEM((2, D, width), jnp.bfloat16),
+        ],
+        cost_estimate=NO_COST,
+        compiler_params=pltpu.CompilerParams(vmem_limit_bytes=GRANT),
+        name="attention_weights",
+    )(place, *arrays)
+
+
+QUERY, VALUE, KEY, OUT = range(4)
+
+
+def matrix_copies(place_ref, role, pieces, whole, sems):
+    rep, dp = place_ref[0], place_ref[1]
+    count = pieces[0].shape[0]
+    copies = []
+    for t in range(4):
+        copies.append([])
+        for side in range(2):
+            start = pl.multiple_of((dp if side == 0 else 1 - dp) * count, count)
+            copies[t].append(
+                pltpu.make_async_copy(
+                    pieces[2 * t + side], whole.at[pl.ds(start, count), :], sems.at[side]
+                )
+            )
+
+    def start():
+        for t in range(4):
+
+            @pl.when((rep ^ t) == role)
+            def _():
+                copies[t][0].start()
+                copies[t][1].start()
+
+    def wait():
+        copies[0][0].wait()
+        copies[0][1].wait()
+
+    return start, wait
+
+
+def row_norm(values):
+    center = values - jnp.mean(values, axis=-1, keepdims=True)
+    inv_std = lax.rsqrt(jnp.mean(center * center, axis=-1, keepdims=True) + EPSILON)
+    return center * inv_std, inv_std
+
+
+def row_norm_back(upstream, normed, inv_std, gain):
+    scaled = upstream * gain
+    inner = (
+        scaled
+        - jnp.mean(scaled, axis=-1, keepdims=True)
+        - normed * jnp.mean(scaled * normed, axis=-1, keepdims=True)
+    )
+    return inner * inv_std
+
+
+def column_sum(values):
+    return jnp.sum(values, axis=0, keepdims=True)
+
+
+STRIP = 128
+
+
+def strips(ref):
+    return [slice(at, at + STRIP) for at in range(0, ref.shape[0], STRIP)]
+
+
+def project_kernel(place_ref, tokens_ref, gain_ref, shift_ref, bias_ref, *refs):
+    pieces, (h_ref, q_ref, k_ref, v_ref, weights, sems) = refs[:8], refs[8:]
+    loads = [
+        matrix_copies(place_ref, role, pieces, weights.at[slot], sems.at[slot])
+        for slot, role in enumerate((QUERY, VALUE, KEY))
+    ]
+    for start, _ in loads:
+        start()
+    for rows in strips(tokens_ref):
+        normed, _ = row_norm(tokens_ref[rows, :].astype(jnp.float32))
+        h_ref[rows, :] = (normed * gain_ref[...] + shift_ref[...]).astype(h_ref.dtype)
+    hidden = h_ref[...]
+    loads[0][1]()
+    q_ref[...] = (mxu(hidden, weights[0]) + bias_ref[:, :D]).astype(q_ref.dtype)
+    loads[1][1]()
+    v_ref[...] = (mxu(hidden, weights[1]) + bias_ref[:, D:]).astype(v_ref.dtype)
+    loads[2][1]()
+    k_ref[...] = mxu(hidden, weights[2]).astype(k_ref.dtype)
+
+
+def out_kernel(place_ref, attn_ref, hidden_ref, tokens_ref, bias_ref, gain_ref, shift_ref, *refs):
+    pieces, (x_ref, h_ref, left_ref, send_ref, weight, sems) = refs[:8], refs[8:]
+    start, wait = matrix_copies(place_ref, OUT, pieces, weight, sems)
+    start()
+    low_core = place_ref[0] % 2 == 0
+    left_ref[...] = jnp.where(low_core, hidden_ref[...], attn_ref[...])
+    send_ref[...] = jnp.where(low_core, attn_ref[...], hidden_ref[...])
+    wait()
+    x_ref[...] = mxu(attn_ref[...], weight[...])
+    for rows in strips(x_ref):
+        value = tokens_ref[rows, :].astype(jnp.float32) + x_ref[rows, :] + bias_ref[...]
+        x_ref[rows, :] = value
+        normed, _ = row_norm(value)
+        h_ref[rows, :] = (normed * gain_ref[...] + shift_ref[...]).astype(h_ref.dtype)
+
+
+def out_back_kernel(place_ref, own_ref, core_ref, far_ref, x_ref, cot_ref, gain_ref, *refs):
+    pieces, (after_ref, low_ref, grad_ref, sum_ref, weight, sems) = refs[:8], refs[8:]
+    start, wait = matrix_copies(place_ref, OUT, pieces, weight, sems)
+    start()
+    f32 = jnp.float32
+    totals = [0.0] * 4
+    for rows in strips(x_ref):
+        grad_h = own_ref[rows, :].astype(f32) + core_ref[rows, :].astype(f32)
+        grad_h += far_ref[rows, :].astype(f32)
+        normed, inv_std = row_norm(x_ref[rows, :])
+        value = row_norm_back(grad_h, normed, inv_std, gain_ref[...]) + cot_ref[rows, :].astype(f32)
+        after_ref[rows, :] = value
+        value_low = value.astype(low_ref.dtype)
+        low_ref[rows, :] = value_low
+        terms = (grad_h * normed, grad_h, value_low.astype(f32), cot_ref[rows, :].astype(f32))
+        totals = [total + column_sum(term) for total, term in zip(totals, terms)]
+    for index, total in enumerate(totals):
+        sum_ref[index : index + 1, :] = total
+    wait()
+    grad_ref[...] = mxu(low_ref[...], weight[...], ((1,), (1,))).astype(grad_ref.dtype)
+
+
+def project_back_kernel(groups, place_ref, tokens_ref, after_ref, gain_ref, *refs):
+    count = 5 * len(groups)
+    grads, pieces = refs[:count], refs[count : count + 8]
+    out_ref, sum_ref, weights, grad_h, sems = refs[count + 8 :]
+    f32 = jnp.float32
+    loads = [
+        matrix_copies(place_ref, role, pieces, weights.at[slot], sems.at[slot])
+        for slot, role in enumerate((QUERY, VALUE, KEY))
+    ]
+    for start, _ in loads:
+        start()
+    for slot in range(3):
+        loads[slot][1]()
+        for index, columns in enumerate(groups):
+            query, value, value_came, key, key_came = grads[5 * index : 5 * index + 5]
+            if slot == 0:
+                grad = query[...]
+            else:
+                near, came = (value, value_came) if slot == 1 else (key, key_came)
+                grad = (near[...].astype(f32) + came[...].astype(f32)).astype(query.dtype)
+            term = mxu(grad, weights[slot, :, columns], ((1,), (1,)))
+            if slot == 0 and index == 0:
+                grad_h[...] = term
+            else:
+                grad_h[...] += term
+            if slot < 2:
+                sum_ref[2 + slot : 3 + slot, columns] = column_sum(grad.astype(f32))
+    totals = [0.0, 0.0]
+    for rows in strips(tokens_ref):
+        upstream = grad_h[rows, :]
+        normed, inv_std = row_norm(tokens_ref[rows, :].astype(f32))
+        value = row_norm_back(upstream, normed, inv_std, gain_ref[...]) + after_ref[rows, :]
+        out_ref[rows, :] = value.astype(out_ref.dtype)
+        terms = (upstream * normed, upstream)
+        totals = [total + column_sum(term) for total, term in zip(totals, terms)]
+    for index, total in enumerate(totals):
+        sum_ref[index : index + 1, :] = total
+
+
+def on_chip(body, name, place, arrays, pieces, outs, scratch):
+    return pl.pallas_call(
+        body,
+        in_specs=[pl.BlockSpec(memory_space=pltpu.SMEM)]
+        + [pl.BlockSpec(memory_space=pltpu.VMEM)] * len(arrays)
+        + [pl.BlockSpec(memory_space=pl.ANY)] * len(pieces),
+        out_specs=[pl.BlockSpec(memory_space=pltpu.VMEM)] * len(outs),
+        out_shape=[jax.ShapeDtypeStruct(*out) for out in outs],
+        scratch_shapes=scratch,
+        cost_estimate=NO_COST,
+        compiler_params=pltpu.CompilerParams(vmem_limit_bytes=GRANT),
+        name=name,
+    )(place, *arrays, *pieces)
+
+
+def feed_forward_kernel(place_ref, *refs):
+    h_ref, h_core_ref, cot_ref, cot_core_ref, bias_ref, *refs = refs
+    pieces, refs = refs[:4], refs[4:]
+    act_ref, pre_ref, out_ref, out_core_ref, back_ref, back_core_ref, sum_ref, fc, proj, sems = refs
+    step = pl.program_id(0)
+    dp = place_ref[1]
+
+    @pl.when(step == 0)
+    def _():
+        copies = []
+        for index, piece in enumerate(pieces):
+            whole = fc if index < 2 else proj
+            count = piece.shape[0]
+            start = pl.multiple_of((dp if index % 2 == 0 else 1 - dp) * count, count)
+            copies.append(
+                pltpu.make_async_copy(piece, whole.at[pl.ds(start, count), :], sems.at[index])
+            )
+        for copy in copies:
+            copy.start()
+        for copy in copies:
+            copy.wait()
+        sum_ref[...] = jnp.zeros_like(sum_ref)
+
+    own = step < pl.num_programs(0) // 2
+    hidden = jnp.where(own, h_ref[...], h_core_ref[...])
+    cotangent = jnp.where(own, cot_ref[...], cot_core_ref[...])
+    hidden_act, hidden_slope = gelu_both(mxu(hidden, fc[...]) + bias_ref[...])
+    act_low = hidden_act.astype(jnp.bfloat16)
+    act_ref[...] = act_low
+    out = mxu(act_low, proj[...]).astype(out_ref.dtype)
+    grad_act = mxu(cotangent, proj[...], ((1,), (1,)))
+    pre_low = (grad_act * hidden_slope).astype(jnp.bfloat16)
+    pre_ref[...] = pre_low
+    back = mxu(pre_low, fc[...], ((1,), (1,))).astype(back_ref.dtype)
+    sum_ref[...] += column_sum(pre_low.astype(jnp.float32))
+
+    @pl.when(own)
+    def _():
+        out_ref[...] = out
+        back_ref[...] = back
+
+    @pl.when(jnp.logical_not(own))
+    def _():
+        out_core_ref[...] = out
+        back_core_ref[...] = back
+
+
+def feed_forward(place, hidden, hidden_core, cot, cot_core, bias, pieces, block_rows=256):
+    rows, units = hidden.shape[0], D
+    steps = rows // block_rows
+    first = pl.BlockSpec((block_rows, D), lambda i: (jnp.minimum(i, steps - 1), 0))
+    second = pl.BlockSpec((block_rows, D), lambda i: (jnp.maximum(i - steps, 0), 0))
+    by_block = pl.BlockSpec((block_rows, D), lambda i: (i, 0))
+    return pl.pallas_call(
+        feed_forward_kernel,
+        grid=(2 * steps,),
+        in_specs=[pl.BlockSpec(memory_space=pltpu.SMEM), first, second, first, second]
+        + [pl.BlockSpec((1, units), lambda i: (0, 0))]
+        + [pl.BlockSpec(memory_space=pl.ANY)] * 4,
+        out_specs=[by_block, by_block, first, second, first, second]
+        + [pl.BlockSpec((1, units), lambda i: (0, 0))],
+        out_shape=[jax.ShapeDtypeStruct((2 * rows, D), jnp.bfloat16)] * 2
+        + [jax.ShapeDtypeStruct((rows, D), jnp.bfloat16)] * 4
+        + [jax.ShapeDtypeStruct((1, units), jnp.float32)],
+        scratch_shapes=[pltpu.VMEM((D, D), jnp.bfloat16)] * 2 + [pltpu.SemaphoreType.DMA((4,))],
+        cost_estimate=NO_COST,
+        compiler_params=pltpu.CompilerParams(vmem_limit_bytes=GRANT),
+        name="feed_forward",
+    )(place, hidden, hidden_core, cot, cot_core, bias, *pieces)
+
+
+def unpack_kernel(widths, rep_ref, small_ref, *out_refs):
+    chips, count, _ = small_ref.shape
+    shards = chips * count
+    at = 0
+    for width, out_ref in zip(widths, out_refs):
+        pieces = [
+            small_ref[shard % chips, shard // chips : shard // chips + 1, at : at + width]
+            for shard in range(shards)
+        ]
+        at += width
+        if width * shards == out_ref.shape[1]:
+            out_ref[...] = jnp.concatenate(pieces, axis=1).astype(jnp.float32)
+            continue
+        part = width // 4
+        for rep in range(4):
+
+            @pl.when(rep_ref[0] == rep)
+            def _():
+                own = [piece[:, rep * part : (rep + 1) * part] for piece in pieces]
+                out_ref[...] = jnp.concatenate(own, axis=1).astype(jnp.float32)
+
+
+def unpack(rep, small, widths, picked):
+    shards = small.shape[0] * small.shape[1]
+    return pl.pallas_call(
+        lambda *refs: unpack_kernel(widths, *refs),
+        in_specs=[
+            pl.BlockSpec(memory_space=pltpu.SMEM),
+            pl.BlockSpec(memory_space=pltpu.VMEM),
+        ],
+        out_specs=[pl.BlockSpec(memory_space=pltpu.VMEM)] * len(widths),
+        out_shape=[
+            jax.ShapeDtypeStruct((1, width * shards // (4 if index == picked else 1)), jnp.float32)
+            for index, width in enumerate(widths)
+        ],
+        cost_estimate=NO_COST,
+        compiler_params=pltpu.CompilerParams(vmem_limit_bytes=GRANT),
+        name="unpack",
+    )(rep.astype(jnp.int32)[None], small)
+
+
+def pick_kernel(rep_ref, whole_ref, part_ref):
+    count = part_ref.shape[0]
+    for rep in range(4):
+
+        @pl.when(rep_ref[0] == rep)
+        def _():
+            pieces = [
+                whole_ref[:, at : at + count] for at in range(rep * count, whole_ref.shape[1], 4 * count)
+            ]
+            part_ref[...] = jnp.concatenate(pieces, axis=1)
+
+
+def pick_units(rep, whole):
+    return pl.pallas_call(
+        pick_kernel,
+        in_specs=[
+            pl.BlockSpec(memory_space=pltpu.SMEM),
+            pl.BlockSpec(memory_space=pltpu.VMEM),
+        ],
+        out_specs=pl.BlockSpec(memory_space=pltpu.VMEM),
+        out_shape=jax.ShapeDtypeStruct((whole.shape[0], whole.shape[1] // 4), whole.dtype),
+        compiler_params=pltpu.CompilerParams(vmem_limit_bytes=GRANT),
+        name="pick_units",
+    )(rep.astype(jnp.int32)[None], whole)
+
+
+def merge_kernel(parts_ref, whole_ref):
+    count = parts_ref.shape[1]
+    for at in range(0, parts_ref.shape[2], count):
+        pieces = [parts_ref[core * 2 + x, :, at : at + count] for x in range(2) for core in range(2)]
+        whole_ref[:, 4 * at : 4 * (at + count)] = jnp.concatenate(pieces, axis=1).astype(whole_ref.dtype)
+
+
+def merge_units(parts):
+    return pl.pallas_call(
+        merge_kernel,
+        in_specs=[pl.BlockSpec(memory_space=pltpu.VMEM)],
+        out_specs=pl.BlockSpec(memory_space=pltpu.VMEM),
+        out_shape=jax.ShapeDtypeStruct((parts.shape[1], 4 * parts.shape[2]), jnp.float32),
+        compiler_params=pltpu.CompilerParams(vmem_limit_bytes=GRANT),
+        name="merge_units",
+    )(parts)
+
+
+def sequence_local(
+    hidden_in,
+    piece_starts,
+    grad_out,
+    attn_gain,
+    attn_shift,
+    qkv_weight,
+    qv_bias,
+    out_weight,
+    out_bias,
+    mlp_gain,
+    mlp_shift,
+    fc_weight,
+    fc_bias,
+    proj_weight,
+    proj_bias,
+):
+    rep, dp, ctx = (lax.axis_index(name) for name in ("rep", "dp", "ctx"))
+    chip_x, core = rep // 2, rep % 2
+    chips, shards = lax.axis_size("ctx"), lax.axis_size(("dp", "ctx"))
+    seqs, block, _ = hidden_in.shape
+    half = block // 2
+    rows = chips * half
+    shard_rows = D // shards
+    f32, low = jnp.float32, jnp.bfloat16
+    core_low, x_low, y_low = core == 0, chip_x == 0, dp == 0
+    half_of = lambda index: (core + index) % 2
+
+    def exchange(tiles):
+        return lax.all_to_all(tiles, "ctx", 0, 0, tiled=True)
+
+    def tiled(value):
+        return value.reshape(chips, half // SUBLANES, SUBLANES, D)
+
+    def by_sequence(value):
+        halves = value.reshape(seqs, 2, half // SUBLANES, SUBLANES, D)
+        mine = half_of(ctx)
+        kept = lax.dynamic_index_in_dim(halves, mine, 1, keepdims=False)
+        came = over_core(lax.dynamic_index_in_dim(halves, 1 - mine, 1, keepdims=False))
+        return tiled(ordered(core_low, kept, came))
+
+    def from_sequence(every):
+        every = every.reshape(2, seqs, half // SUBLANES, SUBLANES, D)
+        kept = lax.dynamic_index_in_dim(every, core, 0, keepdims=False)
+        came = over_core(lax.dynamic_index_in_dim(every, 1 - core, 0, keepdims=False))
+        both = ordered(half_of(ctx) == 0, kept, came)
+        return both.transpose(1, 0, 2, 3, 4).reshape(seqs, block, D)
+
+    def along_ctx(shard):
+        return lax.all_gather(shard, "ctx", axis=0, tiled=True)
+
+    items = (attn_gain, attn_shift, qv_bias, out_bias, mlp_gain, mlp_shift, fc_bias, proj_bias)
+    small = jnp.concatenate(items)[None]
+    small = ordered(y_low, small, over_y(small)).reshape(1, 2, -1)
+    small = lax.all_to_all(
+        jnp.broadcast_to(small, (chips,) + small.shape[1:]), "ctx", 0, 0, tiled=True
+    )
+
+    shard_attn = jnp.where(
+        x_low,
+        jnp.where(core_low, qkv_weight[:, :D], qkv_weight[:, 2 * D :]),
+        jnp.where(core_low, qkv_weight[:, D : 2 * D], out_weight),
+    )
+    shard_fc = pick_units(rep, fc_weight)
+    shard_proj = lax.dynamic_index_in_dim(
+        proj_weight.reshape(4, shard_rows, D), rep, 0, keepdims=False
+    )
+    mine = along_ctx(shard_attn)
+    tokens_sent = by_sequence(after(hidden_in, shard_attn))
+    cot_sent = by_sequence(after(grad_out, tokens_sent))
+    tokens_low = exchange(tokens_sent).reshape(rows, D)
+    mine_fc = along_ctx(shard_fc)
+    mine_proj = along_ctx(shard_proj)
+
+    every_starts = ordered(core_low, piece_starts, over_core(piece_starts)).reshape(chips, -1)
+    starts = lax.dynamic_index_in_dim(every_starts, ctx, 0, keepdims=False)
+    block_index = jnp.arange(chips)
+    row_pos = (
+        (block_index * block + half_of(block_index) * half)[:, None] + jnp.arange(half)[None, :]
+    ).reshape(rows)
+    inside = (row_pos[:, None] >= starts[None, :]) & (row_pos[:, None] < starts[None, :] + PIECE)
+    limit = jnp.maximum(row_pos + 1, jnp.max(jnp.where(inside, starts[None, :] + PIECE, 0), axis=1))
+    limit = limit.astype(jnp.int32)[None, :]
+    core_id = core.astype(jnp.int32)[None]
+
+    place = jnp.stack([rep, dp]).astype(jnp.int32)
+
+    vectors = unpack(rep, small, [item.shape[0] for item in items], 6)
+    mine, vectors = lax.optimization_barrier(
+        (mine, vectors, shard_fc, shard_proj, tokens_low, cot_sent, limit)
+    )[:2]
+    gain_one, shift_one, qv_full, out_bias_full, gain_two, shift_two, fc_bias_mine, proj_bias_full = vectors
+    other, mine_x = lax.optimization_barrier((over_y(mine), over_x(mine)))
+    cot_low = exchange(after(cot_sent, mine_fc)).reshape(rows, D)
+    other_x, cot_low, fc_other = lax.optimization_barrier((over_x(other), cot_low, over_y(mine_fc)))
+    pieces = []
+    for pair in ((mine, other), (mine_x, other_x)):
+        pieces += [pair[0], pair[1], over_core(pair[0]), over_core(pair[1])]
+
+    h1_low, query_low, key_low, value_low = on_chip(
+        project_kernel,
+        "project",
+        place,
+        [tokens_low] + [gain_one, shift_one, qv_full],
+        pieces,
+        [((rows, D), low)] * 4,
+        [pltpu.VMEM((3, D, D), low), pltpu.SemaphoreType.DMA((3, 2))],
+    )
+    key_other, value_other = over_core(key_low), over_core(value_low)
+    proj_other = over_y(mine_proj)
+    query_low = after(query_low, mine_proj)
+    attn_low, lse = attend_forward(
+        core_id, limit, query_low, key_low, key_other, value_low, value_other
+    )
+    cot_x, cot_core = over_x(cot_low), over_core(cot_low)
+    after_attn, h2_low, left_b, send_b = on_chip(
+        out_kernel,
+        "attention_out",
+        place,
+        [after(attn_low, cot_x, proj_other), h1_low, tokens_low, out_bias_full, gain_two, shift_two],
+        pieces,
+        [((rows, D), f32)] + [((rows, D), low)] * 3,
+        [pltpu.VMEM((D, D), low), pltpu.SemaphoreType.DMA((2,))],
+    )
+
+    h2_x, h2_core = over_x(h2_low), over_core(h2_low)
+    proj_other = after(proj_other, h2_core)
+    pieces_fc = [mine_fc, fc_other, mine_proj, proj_other]
+    act_near, pre_near, out_near, out_core, back_near, back_core, sum_near = feed_forward(
+        place, h2_low, h2_core, cot_low, cot_core, fc_bias_mine, pieces_fc
+    )
+    cot_x = after(cot_x, back_near)
+    h2_x = after(h2_x, cot_x)
+    cot_xc, h2_xc = over_core(cot_x), over_core(h2_x)
+    act_far, pre_far, out_x, out_xc, back_x, back_xc, sum_far = feed_forward(
+        place, h2_x, h2_xc, cot_x, cot_xc, fc_bias_mine, pieces_fc
+    )
+
+    def far_sum(own, core):
+        return pair_sum(own, over_core(core), 128)
+
+    back_x = far_sum(back_x, back_xc)
+    back_came = over_x(back_x)
+    back_core = over_core(back_core)
+    out_x = far_sum(out_x, out_xc)
+    act_near, pre_near = after((act_near, pre_near), back_x, out_x, back_core)
+    proj_send, proj_kept = weight_gradient(
+        place, [act_near, act_far], [cot_low, cot_core, cot_x, cot_xc])
+    back_came = after(back_came, proj_send)
+    out_came, out_core = over_x(after(out_x, back_came)), over_core(out_core)
+    grad_after, grad_after_low, grad_attn_low, sums_two = on_chip(
+        out_back_kernel,
+        "attention_out_back",
+        place,
+        [back_near, back_core, back_came, after_attn, cot_low, gain_two],
+        pieces,
+        [((rows, D), f32), ((rows, D), low), ((rows, D), low), ((4, D), f32)],
+        [pltpu.VMEM((D, D), low), pltpu.SemaphoreType.DMA((2,))],
+    )
+
+    proj_came = over_y(after(proj_send, back_came))
+
+    def finish(value):
+        return lax.psum_scatter(value, "ctx", scatter_dimension=0, tiled=True)
+
+    def share(value):
+        pair = ordered(x_low, value, over_x(value))
+        return ordered(core_low, pair, over_core(pair)).reshape((4,) + value.shape)
+
+    h1_other, left_b_other = over_core(h1_low), over_core(send_b)
+
+    grads, terms = [], []
+    held, spans = (), []
+    for group in GROUPS:
+        columns = slice(group[0] * LANES, min(D, group[1] * LANES))
+        spans.append(columns)
+        dq, dk, dk_other, dv, dv_other, send_one, send_two = attend_backward(
+            group,
+            core_id,
+            limit,
+            query_low,
+            key_low,
+            key_other,
+            value_low,
+            value_other,
+            after(grad_attn_low, *held),
+            grad_after_low,
+            lse,
+        )
+        crossing = (dk_other, dv_other, send_one, send_two)
+        came = [over_core(item) for item in crossing]
+        if not group[0]:
+            pre_near = after(pre_near, dq, out_came)
+            fc_send, fc_kept = weight_gradient(
+                place, [h2_low, h2_core, h2_x, h2_xc], [pre_near, pre_far]
+            )
+            fc_came = over_y(fc_send)
+            proj_total = pair_sum(proj_kept, after(proj_came, fc_send))
+            proj_sum = finish(proj_total)
+            h1_low = after(h1_low, proj_total)
+        else:
+            fc_total = pair_sum(fc_kept, after(fc_came, dq))
+            fc_sum = finish(fc_total)
+            h1_low = after(h1_low, fc_total)
+        send_x, keep_x, send_y, keep_y = attention_weights(
+            place,
+            h1_low,
+            h1_other,
+            left_b,
+            left_b_other,
+            [dq, dk, dk_other, dv, dv_other, grad_after_low[:, columns]],
+            came,
+        )
+        terms.append((over_x(send_x), over_y(send_y), keep_x, keep_y))
+        held = (keep_x,)
+        grads.append((dq, dv, came[1], dk, came[0]))
+        if not group[0]:
+            out_came = after(out_came, keep_x)
+            block_tiles = tiled(block_value_of(after_attn, out_near, out_core, out_came, proj_bias_full))
+            block_sent = exchange(block_tiles)
+    came = after(terms[0][:2], *held)
+    second_0 = second_terms(place, *came, *terms[0][2:])
+    grad_input_low, sums_one = on_chip(
+        lambda *refs: project_back_kernel(spans, *refs),
+        "project_back",
+        place,
+        [tokens_low, after(grad_after, *held, block_tiles, *second_0), gain_one] + [item for group in grads for item in group],
+        pieces,
+        [((rows, D), low), ((4, D), f32)],
+        [
+            pltpu.VMEM((3, D, D), low),
+            pltpu.VMEM((rows, D), f32),
+            pltpu.SemaphoreType.DMA((3, 2)),
+        ],
+    )
+    came = after((over_y(second_0[0]), over_x(second_0[1])), grad_input_low, block_sent)
+    total_0 = summed(*came, *second_0[2:])
+    sum_0 = finish(total_0)
+    input_sent = exchange(tiled(after(grad_input_low, total_0)))
+    came = after(terms[1][:2], total_0)
+    second_1 = second_terms(place, *came, *terms[1][2:])
+    proj_quarters = share(after(proj_sum, *second_1))
+    came = after((over_y(second_1[0]), over_x(second_1[1])), proj_quarters)
+    total_1 = summed(*came, *second_1[2:])
+    sum_1 = finish(total_1)
+    block_out = from_sequence(after(block_sent, total_1))
+    fc_quarters = share(after(fc_sum, block_out))
+    grad_fc_shard = merge_units(fc_quarters)
+    grad_proj_shard = (
+        proj_quarters.reshape(2, 2, shard_rows, D)
+        .transpose(1, 0, 2, 3)
+        .reshape(4 * shard_rows, D)
+        .astype(f32)
+    )
+    share_0 = share(after(sum_0, fc_quarters))
+    input_grad = from_sequence(after(input_sent, share_0)).astype(f32)
+    sum_1 = after(sum_1, input_grad, grad_fc_shard, grad_proj_shard)
+    share_1 = share(sum_1)
+    quarters = [share_0.astype(f32), share_1.astype(f32)]
+    grad_qkv_shard = jnp.concatenate([part[index] for index in range(3) for part in quarters], axis=1)
+    grad_out_shard = jnp.concatenate([part[3] for part in quarters], axis=1)
+
+    fc_bias_part = jnp.where(
+        jnp.arange(4)[None, :, None] == rep, (sum_near + sum_far).reshape(shards, 1, shard_rows), 0.0
+    )
+    sums = [
+        sums_one[0],
+        sums_one[1],
+        sums_one[2:],
+        sums_two[2],
+        sums_two[0],
+        sums_two[1],
+        fc_bias_part,
+        sums_two[3],
+    ]
+    table = jnp.concatenate([item.reshape(shards, -1) for item in sums], axis=1)
+    table = after(table, total_1)
+    table = table + over_core(table)
+    table = (table + over_x(table)).reshape(2, chips, -1)
+    table = lax.dynamic_index_in_dim(table, dp, 0, keepdims=False) + over_y(
+        lax.dynamic_index_in_dim(table, 1 - dp, 0, keepdims=False)
+    )
+    mine = jnp.sum(lax.all_to_all(table[:, None], "ctx", 0, 0, tiled=True), axis=(0, 1))
+    small_out, at = [], 0
+    for item in sums:
+        count = item.size // shards
+        small_out.append(mine[at : at + count])
+        at += count
+    return (
+        block_out,
+        input_grad,
+        small_out[0],
+        small_out[1],
+        grad_qkv_shard,
+        small_out[2],
+        grad_out_shard,
+        small_out[3],
+        small_out[4],
+        small_out[5],
+        grad_fc_shard,
+        small_out[6],
+        grad_proj_shard,
+        small_out[7],
+    )
+
+
+def local(hidden_in, *rest):
+    seqs, block, _ = hidden_in.shape
+    sizes = tuple(lax.axis_size(name) for name in ("rep", "dp", "ctx"))
+    if sizes[:2] == (4, 2) and 2 * seqs == sizes[2] and sizes[2] * block == SEQ and block == PIECE:
+        return sequence_local(hidden_in, *rest)
+    return general_local(hidden_in, *rest)
+
+
 def solution(mesh):
     placed = (
         P(("rep", "dp"), "ctx", None),

time: 4240 us -> 871 us (0.21)
  waiting for transfers between devices: 3400 us -> 349 us
  matrix products: 406 us -> 0 us
  Pallas kernels: 0 us -> 349 us
  other arithmetic: 206 us -> 30.8 us
  blocking collectives: 96.3 us -> 8.29 us
  starting transfers between devices: 11.1 us -> 56.2 us
    unnamed x15 -> x7, waiting for transfers between devices: 2050 us -> 0.11 us
    all_gather x8 -> x3, waiting for transfers between devices: 1160 us -> 60.9 us  [along_ctx(): return lax.all_gather(shard, 'ctx', axis=0, tiled=True)]
    dot_general x34 -> x0, matrix products: 406 us -> none  [the longest x2 36.8 us: local(): jnp.einsum('thd,shd->hts', grad_attn_heads, values_heads, preferred_eleme...]
    pallas_call x0 -> x25, Pallas kernels: none -> 349 us  [the longest x2 76.1 us: feed_forward(): pl.pallas_call(feed_forward_kernel, grid=(2 * steps,), in_specs=[pl.Block...]
    all_to_all x0 -> x5, waiting for transfers between devices: none -> 177 us  [the longest x4 174 us: exchange(): return lax.all_to_all(tiles, 'ctx', 0, 0, tiled=True)]
    reduce_scatter x2 -> x1, waiting for transfers between devices: 136 us -> 0.01 us  [finish(): return lax.psum_scatter(value, 'ctx', scatter_dimension=0, tiled=True)]
    ppermute x0 -> x60, waiting for transfers between devices: none -> 111 us  [the longest x57 111 us: permuted(): return lax.ppermute(rows, axis, pairs).reshape(value.shape)]
    concatenate x5 -> x1, other arithmetic: 94.2 us -> 1.15 us  [sequence_local(): grad_out_shard = jnp.concatenate([part[3] for part in quarters], axis=1)]
  transfers between devices with their start and end apart: 13 -> 72, of which waited for: 13 -> 32; matrix products, arithmetic and copies ran while one was open for 11% -> 7% of each run, Pallas kernels for 0% -> 34%
where the time goes in v2:
time: 871 us; the launch traced here: 865 us
  waiting for transfers between devices  349 us (40%)
  Pallas kernels  349 us (40%)
  local copies, waits for them, and re-layouts  56.8 us (7%)
  starting transfers between devices  56.2 us (6%)
  other arithmetic  30.8 us (4%)
  between operations  15.3 us (2%)
    all_to_all x4, waiting for transfers between devices, exchange(): return lax.all_to_all(tiles, 'ctx', 0, 0, tiled=True)  174 us
    ppermute x57, waiting for transfers between devices, permuted(): return lax.ppermute(rows, axis, pairs).reshape(value.shape)  111 us
    pallas_call x2, Pallas kernels, feed_forward(): pl.pallas_call(feed_forward_kernel, grid=(2 * steps,), in_specs=[pl.Block...  76.1 us
    pallas_call x4, Pallas kernels, on_chip(): pl.pallas_call(body, in_specs=[pl.BlockSpec(memory_space=pltpu.SMEM)] + [...  63.1 us
    all_gather x3, waiting for transfers between devices, along_ctx(): return lax.all_gather(shard, 'ctx', axis=0, tiled=True)  60.9 us
    pallas_call x2, Pallas kernels, attend_backward(): pl.pallas_call(lambda *refs: attend_backward_kernel(start, *refs), grid=(...  50.6 us
    pallas_call x2, Pallas kernels, weight_gradient(): pl.pallas_call(lambda *refs: weight_gradient_kernel(len(lefts), *refs), g...  43.4 us
    pallas_call x1, Pallas kernels, attend_forward(): pl.pallas_call(attend_forward_kernel, grid=(PAIRS,), in_specs=[pl.BlockSp...  36.8 us
  transfers between devices with their start and end apart: 72, of which 32 were waited for; matrix products, arithmetic and copies ran while one was open for 7% of the time, Pallas kernels for 34%

profile of v2, /device:TPU:0, one launch (start us, length us, event | category | flops | bytes accessed | tf_op | source)
XLA Modules:
  0.0 865.1 jit_solution(1644257437237435792)
XLA Ops:
  19.0 4.9 all-to-all-start.1
  49.5 55.7 %all-to-all-done = bf16[4,16,8,1600]{3,2,1,0:T(8,128)(2,1)} async-done(((bf16[4,16,8,1600]{3,2,1,0:T(8,128)(2,1)}), bf16[4,16,8,1600]{3,2,1,0:T(8,128)(2,1)}, u32[]{:S(2)}, u32[]{:S(2)}) %all-to-all-start) | async-done | bytes 1638432 | tf_op jit(solution)/shard_map/all_to_all | solution.py:1124
  108.2 51.3 %all-gather.7.cloned.1.call-done.refs_5_ = bf16[800,1600]{1,0:T(8,128)(2,1)} async-done(((bf16[200,1600]{1,0:T(8,128)(2,1)}), bf16[800,1600]{1,0:T(8,128)(2,1)}) %all-gather.7.cloned.1.call-update) | async-done | bytes 2560016 | tf_op jit(solution)/shard_map/all_gather | solution.py:1144
  160.9 5.2 collective-permute-done.4
  174.2 70.5 %all-to-all-done.2 = bf16[4,16,8,1600]{3,2,1,0:T(8,128)(2,1)} async-done(((bf16[4,16,8,1600]{3,2,1,0:T(8,128)(2,1)}), bf16[4,16,8,1600]{3,2,1,0:T(8,128)(2,1)}, u32[]{:S(2)}, u32[]{:S(2)}) %all-to-all-start.2) | async-done | bytes 1638432 | tf_op jit(solution)/shard_map/all_to_all | solution.py:1124
  244.7 9.6 %all-gather.9.cloned.1.call-done = bf16[1,800,1600]{2,1,0:T(8,128)(2,1)} async-done(((bf16[1,200,1600]{2,1,0:T(8,128)(2,1)}), bf16[1,800,1600]{2,1,0:T(8,128)(2,1)}) %all-gather.9.cloned.1.call-update) | async-done | bytes 2560016 | tf_op jit(solution)/shard_map/all_gather | solution.py:1144
  256.9 16.4 %project.1 = (bf16[512,1600]{1,0:T(8,128)(2,1)}, bf16[512,1600]{1,0:T(8,128)(2,1)}, bf16[512,1600]{1,0:T(8,128)(2,1)}, bf16[512,1600]{1,0:T(8,128)(2,1)}) custom-call(s32[2]{0:T(128)} %pad_add_fusion.1.place_ref.refs_0_, bf16[512,1600]{1,0:T(8,128)(2,1)} %bitcast.14.tokens_ref.refs_1_, f32[1,1600]{1,0:T(1,128)} %get-tuple-element.147.gain_ref.refs_3_, ...), custom_call_target="tpu_custom_call" | custom-call | flops 1 | bytes 1 | tf_op jit(solution)/shard_map/project/pallas_call | solution.py:925
  280.8 36.8 %attend_forward.1 = (bf16[512,1600]{1,0:T(8,128)(2,1)}, f32[13,2,512]{2,1,0:T(2,128)}) custom-call(s32[1]{0:T(128)} %bitcast.2.core_ref.refs_0_, s32[1,512]{1,0:T(1,128)} %max.10.limit_ref.refs_1_, bf16[512,1600]{1,0:T(8,128)(2,1)} %get-tuple-element.156.q_ref.refs_2_, bf16[512,1600]{1,0:T(8,128)(2,1)} %get-tuple-element.157.k_ref.refs_3_, ...), custom_call_target="tpu_custom_call" | custom-call | flops 1 | bytes 1 | tf_op jit(solution)/shard_map/attend_forward/pallas_call | solution.py:514
  317.7 12.8 %attention_out.1 = (f32[512,1600]{1,0:T(8,128)}, bf16[512,1600]{1,0:T(8,128)(2,1)}, bf16[512,1600]{1,0:T(8,128)(2,1)}, bf16[512,1600]{1,0:T(8,128)(2,1)}) custom-call(s32[2]{0:T(128)} %pad_add_fusion.1.place_ref.refs_0_, bf16[512,1600]{1,0:T(8,128)(2,1)} %get-tuple-element.161.attn_ref, bf16[512,1600]{1,0:T(8,128)(2,1)} %get-tuple-element.215.hidden_ref, ...), custom_call_target="tpu_custom_call" | custom-call | flops 1 | bytes 1 | tf_op jit(solution)/shard_map/attention_out/pallas_call | solution.py:925
  337.0 37.9 %feed_forward.2 = (bf16[1024,1600]{1,0:T(8,128)(2,1)}, bf16[1024,1600]{1,0:T(8,128)(2,1)}, bf16[512,1600]{1,0:T(8,128)(2,1)}, bf16[512,1600]{1,0:T(8,128)(2,1)},...) custom-call(s32[2]{0:T(128)} %pad_add_fusion.1.place_ref.refs_0_, ...), custom_call_target="tpu_custom_call" | custom-call | flops 1 | bytes 1 | tf_op jit(solution)/shard_map/feed_forward/pallas_call | solution.py:992
  382.2 38.2 %feed_forward.3 = (bf16[1024,1600]{1,0:T(8,128)(2,1)}, bf16[1024,1600]{1,0:T(8,128)(2,1)}, bf16[512,1600]{1,0:T(8,128)(2,1)}, bf16[512,1600]{1,0:T(8,128)(2,1)},...) custom-call(s32[2]{0:T(128)} %pad_add_fusion.1.place_ref.refs_0_, ...), custom_call_target="tpu_custom_call" | custom-call | flops 1 | bytes 1 | tf_op jit(solution)/shard_map/feed_forward/pallas_call | solution.py:992
  435.5 21.7 %weight_gradient.2 = (bf16[800,1600]{1,0:T(8,128)(2,1)}, bf16[800,1600]{1,0:T(8,128)(2,1)}) custom-call(s32[2]{0:T(128)} %pad_add_fusion.1.place_ref.refs_0_, bf16[1024,1600]{1,0:T(8,128)(2,1)} %get-tuple-element.183.refs_1_, bf16[1024,1600]{1,0:T(8,128)(2,1)} %get-tuple-element.184.refs_2_, bf16[512,1600]{1,0:T(8,128)(2,1)} %bitcast.30.refs_2_.refs_3_.cot_ref, ...), custom_call_target="tpu_custom_call" | custom-call | flops 1 | bytes 1 | tf_op jit(solution)/shard_map/weight_gradient/pallas_call | solution.py:584
  457.2 11.9 %collective-permute-done.24 = bf16[64,8,1600]{2,1,0:T(8,128)(2,1)} collective-permute-done((bf16[64,8,1600]{2,1,0:T(8,128)(2,1)}, bf16[64,8,1600]{2,1,0:T(8,128)(2,1)}, u32[]{:S(2)}, u32[]{:S(2)}) %collective-permute-start.24) | collective-permute-done | bytes 1638432 | tf_op jit(solution)/shard_map/ppermute | solution.py:338
  471.1 12.5 %attention_out_back.1 = (f32[512,1600]{1,0:T(8,128)}, bf16[512,1600]{1,0:T(8,128)(2,1)}, bf16[512,1600]{1,0:T(8,128)(2,1)}, f32[4,1600]{1,0:T(4,128)}) custom-call(s32[2]{0:T(128)} %pad_add_fusion.1.place_ref.refs_0_, bf16[512,1600]{1,0:T(8,128)(2,1)} %get-tuple-element.173.own_ref, bf16[512,1600]{1,0:T(8,128)(2,1)} %bitcast.326, ...), custom_call_target="tpu_custom_call" | custom-call | flops 1 | bytes 1 | tf_op jit(solution)/shard_map/attention_out_back/pallas_call | solution.py:925
  483.6 27.1 %attend_backward.2 = (bf16[512,896]{1,0:T(8,128)(2,1)}, bf16[512,896]{1,0:T(8,128)(2,1)}, bf16[512,896]{1,0:T(8,128)(2,1)}, bf16[512,896]{1,0:T(8,128)(2,1)}, bf...) custom-call(s32[1]{0:T(128)} %bitcast.2.core_ref.refs_0_, ...), custom_call_target="tpu_custom_call" | custom-call | flops 1 | bytes 1 | tf_op jit(solution)/shard_map/attend_backward/pallas_call | solution.py:538
  510.7 21.7 %weight_gradient.3 = (bf16[800,1600]{1,0:T(8,128)(2,1)}, bf16[800,1600]{1,0:T(8,128)(2,1)}) custom-call(s32[2]{0:T(128)} %pad_add_fusion.1.place_ref.refs_0_, bf16[512,1600]{1,0:T(8,128)(2,1)} %get-tuple-element.167.refs_0_.refs_1_, bf16[512,1600]{1,0:T(8,128)(2,1)} %bitcast.302, bf16[512,1600]{1,0:T(8,128)(2,1)} %bitcast.304, bf16[512,1600]{1,0:T(8,128)(2,1)} %bitcast.308, ...), custom_call_target="tpu_custom_call" | custom-call | flops 1 | bytes 1 | tf_op jit(solution)/shard_map/weight_gradient/pallas_call | solution.py:584
  543.3 4.7 collective-permute-done.29
  551.0 16.6 %attention_weights.2 = (bf16[2,400,896]{2,1,0:T(8,128)(2,1)}, bf16[2,400,896]{2,1,0:T(8,128)(2,1)}, bf16[2,400,896]{2,1,0:T(8,128)(2,1)}, bf16[2,400,896]{2,1,0:T(8,128)(2,1)}) custom-call(s32[2]{0:T(128)} %pad_add_fusion.1.place_ref.refs_0_, bf16[512,1600]{1,0:T(8,128)(2,1)} %get-tuple-element.215.hidden_ref, bf16[512,1600]{1,0:T(8,128)(2,1)} %bitcast.285, ...), custom_call_target="tpu_custom_call" | custom-call | flops 1 | bytes 1 | tf_op jit(solution)/shard_map/attention_weights/pallas_call | solution.py:752
  567.6 23.6 %attend_backward.3 = (bf16[512,704]{1,0:T(8,128)(2,1)}, bf16[512,704]{1,0:T(8,128)(2,1)}, bf16[512,704]{1,0:T(8,128)(2,1)}, bf16[512,704]{1,0:T(8,128)(2,1)}, bf...) custom-call(s32[1]{0:T(128)} %bitcast.2.core_ref.refs_0_, ...), custom_call_target="tpu_custom_call" | custom-call | flops 1 | bytes 1 | tf_op jit(solution)/shard_map/attend_backward/pallas_call | solution.py:538
  591.2 6.3 collective-permute-done.34
  607.3 5.3 block_value.1
  624.3 13.8 %attention_weights.3 = (bf16[2,400,704]{2,1,0:T(8,128)(2,1)}, bf16[2,400,704]{2,1,0:T(8,128)(2,1)}, bf16[2,400,704]{2,1,0:T(8,128)(2,1)}, bf16[2,400,704]{2,1,0:T(8,128)(2,1)}) custom-call(s32[2]{0:T(128)} %pad_add_fusion.1.place_ref.refs_0_, bf16[512,1600]{1,0:T(8,128)(2,1)} %get-tuple-element.215.hidden_ref, bf16[512,1600]{1,0:T(8,128)(2,1)} %bitcast.286, ...), custom_call_target="tpu_custom_call" | custom-call | flops 1 | bytes 1 | tf_op jit(solution)/shard_map/attention_weights/pallas_call | solution.py:752
  639.8 11.0 %collective-permute-done.41 = bf16[100,8,896]{2,1,0:T(8,128)(2,1)S(1)} collective-permute-done((bf16[100,8,896]{2,1,0:T(8,128)(2,1)}, bf16[100,8,896]{2,1,0:T(8,128)(2,1)S(1)}, u32[]{:S(2)}, u32[]{:S(2)}) %collective-permute-start.41) | collective-permute-done | bytes 1433632 | tf_op jit(solution)/shard_map/ppermute | solution.py:338
  658.6 21.4 %project_back.1 = (bf16[512,1600]{1,0:T(8,128)(2,1)}, f32[4,1600]{1,0:T(4,128)}) custom-call(s32[2]{0:T(128)} %pad_add_fusion.1.place_ref.refs_0_, bf16[512,1600]{1,0:T(8,128)(2,1)} %bitcast.14.tokens_ref.refs_1_, f32[512,1600]{1,0:T(8,128)} %get-tuple-element.235.refs_2_, f32[1,1600]{1,0:T(1,128)} %get-tuple-element.147.gain_ref.refs_3_, ...), custom_call_target="tpu_custom_call" | custom-call | flops 1 | bytes 1 | tf_op jit(solution)/shard_map/project_back/pallas_call | solution.py:925
  680.0 13.0 %collective-permute-done.43 = bf16[50,8,896]{2,1,0:T(8,128)(2,1)S(1)} collective-permute-done((bf16[50,8,896]{2,1,0:T(8,128)(2,1)}, bf16[50,8,896]{2,1,0:T(8,128)(2,1)S(1)}, u32[]{:S(2)}, u32[]{:S(2)}) %collective-permute-start.43) | collective-permute-done | bytes 716832 | tf_op jit(solution)/shard_map/ppermute | solution.py:338
  702.6 13.7 %collective-permute-done.45 = bf16[50,8,704]{2,1,0:T(8,128)(2,1)S(1)} collective-permute-done((bf16[50,8,704]{2,1,0:T(8,128)(2,1)}, bf16[50,8,704]{2,1,0:T(8,128)(2,1)S(1)}, u32[]{:S(2)}, u32[]{:S(2)}) %collective-permute-start.45) | collective-permute-done | bytes 563232 | tf_op jit(solution)/shard_map/ppermute | solution.py:338
  735.1 48.1 %all-to-all-done.4 = bf16[4,16,8,1600]{3,2,1,0:T(8,128)(2,1)} async-done(((bf16[4,16,8,1600]{3,2,1,0:T(8,128)(2,1)}), bf16[4,16,8,1600]{3,2,1,0:T(8,128)(2,1)}, u32[]{:S(2)}, u32[]{:S(2)}) %all-to-all-start.4) | async-done | bytes 1638432 | tf_op jit(solution)/shard_map/all_to_all | solution.py:1124
  789.7 13.2 %collective-permute-done.48 = bf16[25,8,1600]{2,1,0:T(8,128)(2,1)S(1)} collective-permute-done((bf16[25,8,1600]{2,1,0:T(8,128)(2,1)}, bf16[25,8,1600]{2,1,0:T(8,128)(2,1)S(1)}, u32[]{:S(2)}, u32[]{:S(2)}) %collective-permute-start.48) | collective-permute-done | bytes 640032 | tf_op jit(solution)/shard_map/ppermute | solution.py:338
  819.2 5.8 merge_units.1
  825.7 8.3 all_to_all.30
  841.6 4.7 copy.55
  852.0 5.9 concatenate.70
  (330 shorter events, 200.1 us)
Async XLA Ops:
  7.2 98.0 %all-gather.5.cloned.1.call-start = ((), (), s32[]{:S(2)}) async-start(), calls=%async_computation.10 | async-start | bytes 3328000 | tf_op jit(solution)/shard_map/all_gather | solution.py:1144
  30.4 74.9 %all-to-all-start = ((bf16[4,16,8,1600]{3,2,1,0:T(8,128)(2,1)}), bf16[4,16,8,1600]{3,2,1,0:T(8,128)(2,1)}, u32[]{:S(2)}, u32[]{:S(2)}) async-start(bf16[4,16,8,1600]{3,2,1,0:T(8,128)(2,1)} %bitcast.297), calls=%async_computation | async-start | bytes 3407872 | tf_op jit(solution)/shard_map/all_to_all | solution.py:1124
  34.8 124.7 %all-gather.7.cloned.1.call-start = ((), (), s32[]{:S(2)}) async-start(), calls=%async_computation.11 | async-start | bytes 3328000 | tf_op jit(solution)/shard_map/all_gather | solution.py:1144
  105.2 60.9 %collective-permute-start.4 = (bf16[100,8,1600]{2,1,0:T(8,128)(2,1)}, bf16[100,8,1600]{2,1,0:T(8,128)(2,1)}, u32[]{:S(2)}, u32[]{:S(2)}) collective-permute-start(bf16[100,8,1600]{2,1,0:T(8,128)(2,1)} %bitcast.263), channel_id=1, source_target_pairs={{0,4},{4,0},{1,5},{5,1},{2,6},{6,2},{3,7},{7,3},{8,12},{12,8},{9,1... | collective-permute-start | bytes 7680008 | tf_op jit(solution)/shard_map/ppermute | solution.py:338
  106.7 59.7 %collective-permute-start.5 = (bf16[100,8,1600]{2,1,0:T(8,128)(2,1)}, bf16[100,8,1600]{2,1,0:T(8,128)(2,1)}, u32[]{:S(2)}, u32[]{:S(2)}) collective-permute-start(bf16[100,8,1600]{2,1,0:T(8,128)(2,1)} %bitcast.264), channel_id=1, source_target_pairs={{0,16},{16,0},{8,24},{24,8},{1,17},{17,1},{9,25},{25,9},{2,18},{18... | collective-permute-start | bytes 7680008 | tf_op jit(solution)/shard_map/ppermute | solution.py:338
  159.5 85.2 %collective-permute-start.9 = (bf16[100,8,1600]{2,1,0:T(8,128)(2,1)}, bf16[100,8,1600]{2,1,0:T(8,128)(2,1)}, u32[]{:S(2)}, u32[]{:S(2)}) collective-permute-start(bf16[100,8,1600]{2,1,0:T(8,128)(2,1)} %bitcast.281), channel_id=1, source_target_pairs={{0,4},{4,0},{1,5},{5,1},{2,6},{6,2},{3,7},{7,3},{8,12},{12,8},{9,1... | collective-permute-start | bytes 7680008 | tf_op jit(solution)/shard_map/ppermute | solution.py:338
  166.5 78.2 %collective-permute-start.8 = (bf16[100,8,1600]{2,1,0:T(8,128)(2,1)}, bf16[100,8,1600]{2,1,0:T(8,128)(2,1)}, u32[]{:S(2)}, u32[]{:S(2)}) collective-permute-start(bf16[100,8,1600]{2,1,0:T(8,128)(2,1)} %bitcast.27), channel_id=1, source_target_pairs={{0,16},{16,0},{8,24},{24,8},{1,17},{17,1},{9,25},{25,9},{2,18},{18... | collective-permute-start | bytes 7680008 | tf_op jit(solution)/shard_map/ppermute | solution.py:338
  167.9 76.7 %all-to-all-start.2 = ((bf16[4,16,8,1600]{3,2,1,0:T(8,128)(2,1)}), bf16[4,16,8,1600]{3,2,1,0:T(8,128)(2,1)}, u32[]{:S(2)}, u32[]{:S(2)}) async-start(bf16[4,16,8,1600]{3,2,1,0:T(8,128)(2,1)} %bitcast.298), calls=%async_computation.2 | async-start | bytes 3407872 | tf_op jit(solution)/shard_map/all_to_all | solution.py:1124
  172.3 81.9 %all-gather.9.cloned.1.call-start = ((), (), s32[]{:S(2)}) async-start(), calls=%async_computation.13 | async-start | bytes 3328000 | tf_op jit(solution)/shard_map/all_gather | solution.py:1144
  173.3 559.8 %reduce-scatter.17.cloned.1.call-start = ((), (), s32[]{:S(2)}) async-start(), calls=%async_computation.16 | async-start | bytes 3328000
  173.5 81.9 %collective-permute-start.6 = (bf16[100,8,1600]{2,1,0:T(8,128)(2,1)}, bf16[100,8,1600]{2,1,0:T(8,128)(2,1)S(1)}, u32[]{:S(2)}, u32[]{:S(2)}) collective-permute-start(bf16[100,8,1600]{2,1,0:T(8,128)(2,1)} %bitcast.265), channel_id=1, source_target_pairs={{0,8},{8,0},{16,24},{24,16},{1,9},{9,1},{17,25},{25,17},{2,10},{10... | collective-permute-start | bytes 7680008 | tf_op jit(solution)/shard_map/ppermute | solution.py:338
  173.6 81.8 %collective-permute-start.7 = (bf16[100,8,1600]{2,1,0:T(8,128)(2,1)}, bf16[100,8,1600]{2,1,0:T(8,128)(2,1)}, u32[]{:S(2)}, u32[]{:S(2)}) collective-permute-start(bf16[100,8,1600]{2,1,0:T(8,128)(2,1)} %bitcast.27), channel_id=1, source_target_pairs={{0,8},{8,0},{16,24},{24,16},{1,9},{9,1},{17,25},{25,17},{2,10},{10... | collective-permute-start | bytes 7680008 | tf_op jit(solution)/shard_map/ppermute | solution.py:338
  174.1 81.4 %collective-permute-start.10 = (bf16[100,8,1600]{2,1,0:T(8,128)(2,1)}, bf16[100,8,1600]{2,1,0:T(8,128)(2,1)}, u32[]{:S(2)}, u32[]{:S(2)}) collective-permute-start(bf16[100,8,1600]{2,1,0:T(8,128)(2,1)} %bitcast.33), channel_id=1, source_target_pairs={{0,8},{8,0},{16,24},{24,16},{1,9},{9,1},{17,25},{25,17},{2,10},{10... | collective-permute-start | bytes 7680008 | tf_op jit(solution)/shard_map/ppermute | solution.py:338
  254.3 63.4 %collective-permute-start.15 = (bf16[100,8,1600]{2,1,0:T(8,128)(2,1)}, bf16[100,8,1600]{2,1,0:T(8,128)(2,1)}, u32[]{:S(2)}, u32[]{:S(2)}) collective-permute-start(bf16[100,8,1600]{2,1,0:T(8,128)(2,1)} %bitcast.282), channel_id=1, source_target_pairs={{0,4},{4,0},{1,5},{5,1},{2,6},{6,2},{3,7},{7,3},{8,12},{12,8},{9,1... | collective-permute-start | bytes 7680008 | tf_op jit(solution)/shard_map/ppermute | solution.py:338
  273.9 43.7 %collective-permute-start.14 = (bf16[64,8,1600]{2,1,0:T(8,128)(2,1)}, bf16[64,8,1600]{2,1,0:T(8,128)(2,1)S(1)}, u32[]{:S(2)}, u32[]{:S(2)}) collective-permute-start(bf16[64,8,1600]{2,1,0:T(8,128)(2,1)} %bitcast.43), channel_id=1, source_target_pairs={{0,16},{16,0},{8,24},{24,8},{1,17},{17,1},{9,25},{25,9},{2,18},{18... | collective-permute-start | bytes 4915208 | tf_op jit(solution)/shard_map/ppermute | solution.py:338
  331.1 43.7 %collective-permute-start.19 = (bf16[64,8,1600]{2,1,0:T(8,128)(2,1)}, bf16[64,8,1600]{2,1,0:T(8,128)(2,1)S(1)}, u32[]{:S(2)}, u32[]{:S(2)}) collective-permute-start(bf16[64,8,1600]{2,1,0:T(8,128)(2,1)} %bitcast.300), channel_id=1, source_target_pairs={{0,16},{16,0},{8,24},{24,8},{1,17},{17,1},{9,25},{25,9},{2,18},{18... | collective-permute-start | bytes 4915208 | tf_op jit(solution)/shard_map/ppermute | solution.py:338
  429.6 39.6 %collective-permute-start.24 = (bf16[64,8,1600]{2,1,0:T(8,128)(2,1)}, bf16[64,8,1600]{2,1,0:T(8,128)(2,1)}, u32[]{:S(2)}, u32[]{:S(2)}) collective-permute-start(bf16[64,8,1600]{2,1,0:T(8,128)(2,1)} %bitcast.320), channel_id=1, source_target_pairs={{0,16},{16,0},{8,24},{24,8},{1,17},{17,1},{9,25},{25,9},{2,18},{18... | collective-permute-start | bytes 4915208 | tf_op jit(solution)/shard_map/ppermute | solution.py:338
  469.1 63.3 %collective-permute-start.27 = (bf16[100,8,1600]{2,1,0:T(8,128)(2,1)}, bf16[100,8,1600]{2,1,0:T(8,128)(2,1)S(1)}, u32[]{:S(2)}, u32[]{:S(2)}) collective-permute-start(bf16[100,8,1600]{2,1,0:T(8,128)(2,1)} %bitcast.354), channel_id=1, source_target_pairs={{0,4},{4,0},{1,5},{5,1},{2,6},{6,2},{3,7},{7,3},{8,12},{12,8},{9,1... | collective-permute-start | bytes 7680008 | tf_op jit(solution)/shard_map/ppermute | solution.py:338
  470.6 40.1 %collective-permute-start.26 = (bf16[64,8,1600]{2,1,0:T(8,128)(2,1)S(1)}, bf16[64,8,1600]{2,1,0:T(8,128)(2,1)S(1)}, u32[]{:S(2)}, u32[]{:S(2)}) collective-permute-start(bf16[64,8,1600]{2,1,0:T(8,128)(2,1)S(1)} %bitcast.319), channel_id=1, source_target_pairs={{0,16},{16,0},{8,24},{24,8},{1,17},{17,1},{9,25},{25,9},{2,18},{18... | collective-permute-start | bytes 4915208 | tf_op jit(solution)/shard_map/ppermute | solution.py:338
  538.7 246.6 %reduce-scatter.15.cloned.1.call-start = ((), (), s32[]{:S(2)}) async-start(), calls=%async_computation.15 | async-start | bytes 3328000
  538.7 58.7 %collective-permute-start.34 = (bf16[100,8,1600]{2,1,0:T(8,128)(2,1)}, bf16[100,8,1600]{2,1,0:T(8,128)(2,1)}, u32[]{:S(2)}, u32[]{:S(2)}) collective-permute-start(bf16[100,8,1600]{2,1,0:T(8,128)(2,1)} %bitcast.353), channel_id=1, source_target_pairs={{0,4},{4,0},{1,5},{5,1},{2,6},{6,2},{3,7},{7,3},{8,12},{12,8},{9,1... | collective-permute-start | bytes 7680008 | tf_op jit(solution)/shard_map/ppermute | solution.py:338
  612.6 80.4 %all-to-all-start.3 = ((bf16[4,16,8,1600]{3,2,1,0:T(8,128)(2,1)}), bf16[4,16,8,1600]{3,2,1,0:T(8,128)(2,1)S(1)}, u32[]{:S(2)}, u32[]{:S(2)}) async-start(bf16[4,16,8,1600]{3,2,1,0:T(8,128)(2,1)} %bitcast.296), calls=%async_computation.3 | async-start | bytes 3407872 | tf_op jit(solution)/shard_map/all_to_all | solution.py:1124
  616.2 208.9 %reduce-scatter.11.cloned.1.call-start = ((), (), s32[]{:S(2)}) async-start(), calls=%async_computation.12 | async-start | bytes 1536000 | tf_op jit(solution)/shard_map/reduce_scatter | solution.py:1258
  617.9 34.6 %collective-permute-start.42 = (bf16[100,8,896]{2,1,0:T(8,128)(2,1)}, bf16[100,8,896]{2,1,0:T(8,128)(2,1)}, u32[]{:S(2)}, u32[]{:S(2)}) collective-permute-start(bf16[100,8,896]{2,1,0:T(8,128)(2,1)} %bitcast.360), channel_id=1, source_target_pairs={{0,4},{4,0},{1,5},{5,1},{2,6},{6,2},{3,7},{7,3},{8,12},{12,8},{9,1... | collective-permute-start | bytes 4300808 | tf_op jit(solution)/shard_map/ppermute | solution.py:338
  638.0 59.2 %collective-permute-start.39 = (bf16[100,8,704]{2,1,0:T(8,128)(2,1)}, bf16[100,8,704]{2,1,0:T(8,128)(2,1)}, u32[]{:S(2)}, u32[]{:S(2)}) collective-permute-start(bf16[100,8,704]{2,1,0:T(8,128)(2,1)} %bitcast.363), channel_id=1, source_target_pairs={{0,16},{16,0},{8,24},{24,8},{1,17},{17,1},{9,25},{25,9},{2,18},{18... | collective-permute-start | bytes 3379208 | tf_op jit(solution)/shard_map/ppermute | solution.py:338
  638.6 58.7 %collective-permute-start.40 = (bf16[100,8,704]{2,1,0:T(8,128)(2,1)}, bf16[100,8,704]{2,1,0:T(8,128)(2,1)}, u32[]{:S(2)}, u32[]{:S(2)}) collective-permute-start(bf16[100,8,704]{2,1,0:T(8,128)(2,1)} %bitcast.362), channel_id=1, source_target_pairs={{0,4},{4,0},{1,5},{5,1},{2,6},{6,2},{3,7},{7,3},{8,12},{12,8},{9,1... | collective-permute-start | bytes 3379208 | tf_op jit(solution)/shard_map/ppermute | solution.py:338
  657.0 35.9 %collective-permute-start.43 = (bf16[50,8,896]{2,1,0:T(8,128)(2,1)}, bf16[50,8,896]{2,1,0:T(8,128)(2,1)S(1)}, u32[]{:S(2)}, u32[]{:S(2)}) collective-permute-start(bf16[50,8,896]{2,1,0:T(8,128)(2,1)} %bitcast.369), channel_id=1, source_target_pairs={{0,4},{4,0},{1,5},{5,1},{2,6},{6,2},{3,7},{7,3},{8,12},{12,8},{9,1... | collective-permute-start | bytes 2150408 | tf_op jit(solution)/shard_map/ppermute | solution.py:338
  657.7 35.3 %collective-permute-start.44 = (bf16[50,8,896]{2,1,0:T(8,128)(2,1)}, bf16[50,8,896]{2,1,0:T(8,128)(2,1)S(1)}, u32[]{:S(2)}, u32[]{:S(2)}) collective-permute-start(bf16[50,8,896]{2,1,0:T(8,128)(2,1)} %bitcast.368), channel_id=1, source_target_pairs={{0,16},{16,0},{8,24},{24,8},{1,17},{17,1},{9,25},{25,9},{2,18},{18... | collective-permute-start | bytes 2150408 | tf_op jit(solution)/shard_map/ppermute | solution.py:338
  720.6 62.6 %all-to-all-start.4 = ((bf16[4,16,8,1600]{3,2,1,0:T(8,128)(2,1)}), bf16[4,16,8,1600]{3,2,1,0:T(8,128)(2,1)}, u32[]{:S(2)}, u32[]{:S(2)}) async-start(bf16[4,16,8,1600]{3,2,1,0:T(8,128)(2,1)} %bitcast.323), calls=%async_computation.4 | async-start | bytes 3407872 | tf_op jit(solution)/shard_map/all_to_all | solution.py:1124
  725.2 110.1 %reduce-scatter.13.cloned.1.call-start = ((), (), s32[]{:S(2)}) async-start(), calls=%async_computation.14 | async-start | bytes 1792000
  732.6 72.9 %collective-permute-start.54 = (f32[1,8,2400]{2,1,0:T(8,128)}, f32[1,8,2400]{2,1,0:T(8,128)}, u32[]{:S(2)}, u32[]{:S(2)}) collective-permute-start(f32[1,8,2400]{2,1,0:T(8,128)} %fusion.16), channel_id=1, source_target_pairs={{0,16},{16,0},{8,24},{24,8},{1,17},{17,1},{9,25},{25,9},{2,18},{18... | collective-permute-start | bytes 230408 | tf_op jit(solution)/shard_map/ppermute | solution.py:338
  733.1 52.8 %collective-permute-start.56 = (bf16[25,8,1600]{2,1,0:T(8,128)(2,1)}, bf16[25,8,1600]{2,1,0:T(8,128)(2,1)}, u32[]{:S(2)}, u32[]{:S(2)}) collective-permute-start(bf16[25,8,1600]{2,1,0:T(8,128)(2,1)} %bitcast.342), channel_id=1, source_target_pairs={{0,16},{16,0},{8,24},{24,8},{1,17},{17,1},{9,25},{25,9},{2,18},{18... | collective-permute-start | bytes 1920008 | tf_op jit(solution)/shard_map/ppermute | solution.py:338
  (88 other events, 810.5 us)
Sparse Core Ops, SparseCore 0:
  10.3 92.6 all-gather.4
  105.1 54.3 all-gather.6
  175.3 78.9 all-gather.8
  538.8 50.5 reduce-scatter.16
  602.3 76.5 reduce-scatter.14
  720.7 48.6 reduce-scatter.10
  772.4 40.1 reduce-scatter.12

commit v3 on v2

--- a/solution.py
+++ b/solution.py
@@ -1331,13 +1331,14 @@
     total_0 = summed(*came, *second_0[2:])
     sum_0 = finish(total_0)
     input_sent = exchange(tiled(after(grad_input_low, total_0)))
-    came = after(terms[1][:2], total_0)
+    came = after(terms[1][:2], total_0, proj_sum, fc_sum)
     second_1 = second_terms(place, *came, *terms[1][2:])
-    proj_quarters = share(after(proj_sum, *second_1))
-    came = after((over_y(second_1[0]), over_x(second_1[1])), proj_quarters)
-    total_1 = summed(*came, *second_1[2:])
+    came = (over_y(second_1[0]), over_x(second_1[1]))
+    total_1 = summed(*after(came, sum_0), *second_1[2:])
     sum_1 = finish(total_1)
-    block_out = from_sequence(after(block_sent, total_1))
+    input_sent = after(input_sent, total_1)
+    proj_quarters = share(after(proj_sum, input_sent))
+    block_out = from_sequence(after(block_sent, input_sent))
     fc_quarters = share(after(fc_sum, block_out))
     grad_fc_shard = merge_units(fc_quarters)
     grad_proj_shard = (
@@ -1347,7 +1348,7 @@
         .astype(f32)
     )
     share_0 = share(after(sum_0, fc_quarters))
-    input_grad = from_sequence(after(input_sent, share_0)).astype(f32)
+    input_grad = from_sequence(input_sent).astype(f32)
     sum_1 = after(sum_1, input_grad, grad_fc_shard, grad_proj_shard)
     share_1 = share(sum_1)
     quarters = [share_0.astype(f32), share_1.astype(f32)]

time: 871 us -> 865 us (level)
    all_to_all x4, waiting for transfers between devices: 174 us -> 136 us  [exchange(): return lax.all_to_all(tiles, 'ctx', 0, 0, tiled=True)]
    optimization_barrier x3, waiting for transfers between devices: 0.01 us -> 20.9 us  [after(): return lax.optimization_barrier((value, *others))[0]]
    ppermute x57, waiting for transfers between devices: 111 us -> 122 us  [permuted(): return lax.ppermute(rows, axis, pairs).reshape(value.shape)]
    unnamed x99 -> x103, local copies, waits for them, and re-layouts: 21 us -> 20.1 us
  transfers between devices with their start and end apart: 72 -> 72, of which waited for: 32 -> 33; matrix products, arithmetic and copies ran while one was open for 7% -> 7% of each run, Pallas kernels for 34% -> 34%
where the time goes in v3:
time: 865 us; the launch traced here: 859 us
  Pallas kernels  349 us (40%)
  waiting for transfers between devices  343 us (40%)
  starting transfers between devices  59.4 us (7%)
  local copies, waits for them, and re-layouts  53.4 us (6%)
  other arithmetic  27.9 us (3%)
  between operations  15.3 us (2%)
  blocking collectives  11.4 us (1%)
    all_to_all x4, waiting for transfers between devices, exchange(): return lax.all_to_all(tiles, 'ctx', 0, 0, tiled=True)  136 us
    ppermute x57, waiting for transfers between devices, permuted(): return lax.ppermute(rows, axis, pairs).reshape(value.shape)  122 us
    pallas_call x2, Pallas kernels, feed_forward(): pl.pallas_call(feed_forward_kernel, grid=(2 * steps,), in_specs=[pl.Block...  76 us
    pallas_call x4, Pallas kernels, on_chip(): pl.pallas_call(body, in_specs=[pl.BlockSpec(memory_space=pltpu.SMEM)] + [...  63.1 us
    all_gather x3, waiting for transfers between devices, along_ctx(): return lax.all_gather(shard, 'ctx', axis=0, tiled=True)  60.9 us
    pallas_call x2, Pallas kernels, attend_backward(): pl.pallas_call(lambda *refs: attend_backward_kernel(start, *refs), grid=(...  50.6 us
    pallas_call x2, Pallas kernels, weight_gradient(): pl.pallas_call(lambda *refs: weight_gradient_kernel(len(lefts), *refs), g...  43.4 us
    pallas_call x1, Pallas kernels, attend_forward(): pl.pallas_call(attend_forward_kernel, grid=(PAIRS,), in_specs=[pl.BlockSp...  36.8 us
  transfers between devices with their start and end apart: 72, of which 33 were waited for; matrix products, arithmetic and copies ran while one was open for 7% of the time, Pallas kernels for 34%

profile of v3, /device:TPU:0, one launch (start us, length us, event | category | flops | bytes accessed | tf_op | source)
XLA Modules:
  0.0 858.8 jit_solution(13686378930177719447)
XLA Ops:
  19.0 4.9 all-to-all-start.1
  49.5 55.7 %all-to-all-done = bf16[4,16,8,1600]{3,2,1,0:T(8,128)(2,1)} async-done(((bf16[4,16,8,1600]{3,2,1,0:T(8,128)(2,1)}), bf16[4,16,8,1600]{3,2,1,0:T(8,128)(2,1)}, u32[]{:S(2)}, u32[]{:S(2)}) %all-to-all-start) | async-done | bytes 1638432 | tf_op jit(solution)/shard_map/all_to_all | solution.py:1124
  108.2 51.3 %all-gather.7.cloned.1.call-done.refs_5_ = bf16[800,1600]{1,0:T(8,128)(2,1)} async-done(((bf16[200,1600]{1,0:T(8,128)(2,1)}), bf16[800,1600]{1,0:T(8,128)(2,1)}) %all-gather.7.cloned.1.call-update) | async-done | bytes 2560016 | tf_op jit(solution)/shard_map/all_gather | solution.py:1144
  160.9 5.2 collective-permute-done.4
  174.2 70.5 %all-to-all-done.2 = bf16[4,16,8,1600]{3,2,1,0:T(8,128)(2,1)} async-done(((bf16[4,16,8,1600]{3,2,1,0:T(8,128)(2,1)}), bf16[4,16,8,1600]{3,2,1,0:T(8,128)(2,1)}, u32[]{:S(2)}, u32[]{:S(2)}) %all-to-all-start.2) | async-done | bytes 1638432 | tf_op jit(solution)/shard_map/all_to_all | solution.py:1124
  244.7 9.6 %all-gather.9.cloned.1.call-done = bf16[1,800,1600]{2,1,0:T(8,128)(2,1)} async-done(((bf16[1,200,1600]{2,1,0:T(8,128)(2,1)}), bf16[1,800,1600]{2,1,0:T(8,128)(2,1)}) %all-gather.9.cloned.1.call-update) | async-done | bytes 2560016 | tf_op jit(solution)/shard_map/all_gather | solution.py:1144
  256.9 16.4 %project.1 = (bf16[512,1600]{1,0:T(8,128)(2,1)}, bf16[512,1600]{1,0:T(8,128)(2,1)}, bf16[512,1600]{1,0:T(8,128)(2,1)}, bf16[512,1600]{1,0:T(8,128)(2,1)}) custom-call(s32[2]{0:T(128)} %pad_add_fusion.1.place_ref.refs_0_, bf16[512,1600]{1,0:T(8,128)(2,1)} %bitcast.14.tokens_ref.refs_1_, f32[1,1600]{1,0:T(1,128)} %get-tuple-element.147.gain_ref.refs_3_, ...), custom_call_target="tpu_custom_call" | custom-call | flops 1 | bytes 1 | tf_op jit(solution)/shard_map/project/pallas_call | solution.py:925
  280.8 36.8 %attend_forward.1 = (bf16[512,1600]{1,0:T(8,128)(2,1)}, f32[13,2,512]{2,1,0:T(2,128)}) custom-call(s32[1]{0:T(128)} %bitcast.2.core_ref.refs_0_, s32[1,512]{1,0:T(1,128)} %max.10.limit_ref.refs_1_, bf16[512,1600]{1,0:T(8,128)(2,1)} %get-tuple-element.156.q_ref.refs_2_, bf16[512,1600]{1,0:T(8,128)(2,1)} %get-tuple-element.157.k_ref.refs_3_, ...), custom_call_target="tpu_custom_call" | custom-call | flops 1 | bytes 1 | tf_op jit(solution)/shard_map/attend_forward/pallas_call | solution.py:514
  317.7 12.8 %attention_out.1 = (f32[512,1600]{1,0:T(8,128)}, bf16[512,1600]{1,0:T(8,128)(2,1)}, bf16[512,1600]{1,0:T(8,128)(2,1)}, bf16[512,1600]{1,0:T(8,128)(2,1)}) custom-call(s32[2]{0:T(128)} %pad_add_fusion.1.place_ref.refs_0_, bf16[512,1600]{1,0:T(8,128)(2,1)} %get-tuple-element.161.attn_ref, bf16[512,1600]{1,0:T(8,128)(2,1)} %get-tuple-element.216.hidden_ref, ...), custom_call_target="tpu_custom_call" | custom-call | flops 1 | bytes 1 | tf_op jit(solution)/shard_map/attention_out/pallas_call | solution.py:925
  337.0 37.9 %feed_forward.2 = (bf16[1024,1600]{1,0:T(8,128)(2,1)}, bf16[1024,1600]{1,0:T(8,128)(2,1)}, bf16[512,1600]{1,0:T(8,128)(2,1)}, bf16[512,1600]{1,0:T(8,128)(2,1)},...) custom-call(s32[2]{0:T(128)} %pad_add_fusion.1.place_ref.refs_0_, ...), custom_call_target="tpu_custom_call" | custom-call | flops 1 | bytes 1 | tf_op jit(solution)/shard_map/feed_forward/pallas_call | solution.py:992
  382.2 38.2 %feed_forward.3 = (bf16[1024,1600]{1,0:T(8,128)(2,1)}, bf16[1024,1600]{1,0:T(8,128)(2,1)}, bf16[512,1600]{1,0:T(8,128)(2,1)}, bf16[512,1600]{1,0:T(8,128)(2,1)},...) custom-call(s32[2]{0:T(128)} %pad_add_fusion.1.place_ref.refs_0_, ...), custom_call_target="tpu_custom_call" | custom-call | flops 1 | bytes 1 | tf_op jit(solution)/shard_map/feed_forward/pallas_call | solution.py:992
  435.4 21.7 %weight_gradient.2 = (bf16[800,1600]{1,0:T(8,128)(2,1)}, bf16[800,1600]{1,0:T(8,128)(2,1)}) custom-call(s32[2]{0:T(128)} %pad_add_fusion.1.place_ref.refs_0_, bf16[1024,1600]{1,0:T(8,128)(2,1)} %get-tuple-element.183.refs_1_, bf16[1024,1600]{1,0:T(8,128)(2,1)} %get-tuple-element.184.refs_2_, bf16[512,1600]{1,0:T(8,128)(2,1)} %bitcast.30.refs_2_.refs_3_.cot_ref, ...), custom_call_target="tpu_custom_call" | custom-call | flops 1 | bytes 1 | tf_op jit(solution)/shard_map/weight_gradient/pallas_call | solution.py:584
  457.2 12.0 %collective-permute-done.24 = bf16[64,8,1600]{2,1,0:T(8,128)(2,1)} collective-permute-done((bf16[64,8,1600]{2,1,0:T(8,128)(2,1)}, bf16[64,8,1600]{2,1,0:T(8,128)(2,1)}, u32[]{:S(2)}, u32[]{:S(2)}) %collective-permute-start.24) | collective-permute-done | bytes 1638432 | tf_op jit(solution)/shard_map/ppermute | solution.py:338
  471.1 12.5 %attention_out_back.1 = (f32[512,1600]{1,0:T(8,128)}, bf16[512,1600]{1,0:T(8,128)(2,1)}, bf16[512,1600]{1,0:T(8,128)(2,1)}, f32[4,1600]{1,0:T(4,128)}) custom-call(s32[2]{0:T(128)} %pad_add_fusion.1.place_ref.refs_0_, bf16[512,1600]{1,0:T(8,128)(2,1)} %get-tuple-element.173.own_ref, bf16[512,1600]{1,0:T(8,128)(2,1)} %bitcast.327, ...), custom_call_target="tpu_custom_call" | custom-call | flops 1 | bytes 1 | tf_op jit(solution)/shard_map/attention_out_back/pallas_call | solution.py:925
  483.6 27.1 %attend_backward.2 = (bf16[512,896]{1,0:T(8,128)(2,1)}, bf16[512,896]{1,0:T(8,128)(2,1)}, bf16[512,896]{1,0:T(8,128)(2,1)}, bf16[512,896]{1,0:T(8,128)(2,1)}, bf...) custom-call(s32[1]{0:T(128)} %bitcast.2.core_ref.refs_0_, ...), custom_call_target="tpu_custom_call" | custom-call | flops 1 | bytes 1 | tf_op jit(solution)/shard_map/attend_backward/pallas_call | solution.py:538
  510.7 21.7 %weight_gradient.3 = (bf16[800,1600]{1,0:T(8,128)(2,1)}, bf16[800,1600]{1,0:T(8,128)(2,1)}) custom-call(s32[2]{0:T(128)} %pad_add_fusion.1.place_ref.refs_0_, bf16[512,1600]{1,0:T(8,128)(2,1)} %get-tuple-element.167.refs_0_.refs_1_, bf16[512,1600]{1,0:T(8,128)(2,1)} %bitcast.303, bf16[512,1600]{1,0:T(8,128)(2,1)} %bitcast.305, bf16[512,1600]{1,0:T(8,128)(2,1)} %bitcast.309, ...), custom_call_target="tpu_custom_call" | custom-call | flops 1 | bytes 1 | tf_op jit(solution)/shard_map/weight_gradient/pallas_call | solution.py:584
  543.3 4.7 collective-permute-done.29
  551.0 16.6 %attention_weights.2 = (bf16[2,400,896]{2,1,0:T(8,128)(2,1)}, bf16[2,400,896]{2,1,0:T(8,128)(2,1)}, bf16[2,400,896]{2,1,0:T(8,128)(2,1)}, bf16[2,400,896]{2,1,0:T(8,128)(2,1)}) custom-call(s32[2]{0:T(128)} %pad_add_fusion.1.place_ref.refs_0_, bf16[512,1600]{1,0:T(8,128)(2,1)} %get-tuple-element.216.hidden_ref, bf16[512,1600]{1,0:T(8,128)(2,1)} %bitcast.286, ...), custom_call_target="tpu_custom_call" | custom-call | flops 1 | bytes 1 | tf_op jit(solution)/shard_map/attention_weights/pallas_call | solution.py:752
  567.6 23.6 %attend_backward.3 = (bf16[512,704]{1,0:T(8,128)(2,1)}, bf16[512,704]{1,0:T(8,128)(2,1)}, bf16[512,704]{1,0:T(8,128)(2,1)}, bf16[512,704]{1,0:T(8,128)(2,1)}, bf...) custom-call(s32[1]{0:T(128)} %bitcast.2.core_ref.refs_0_, ...), custom_call_target="tpu_custom_call" | custom-call | flops 1 | bytes 1 | tf_op jit(solution)/shard_map/attend_backward/pallas_call | solution.py:538
  591.2 6.2 collective-permute-done.34
  607.3 5.3 block_value.1
  624.6 13.8 %attention_weights.3 = (bf16[2,400,704]{2,1,0:T(8,128)(2,1)}, bf16[2,400,704]{2,1,0:T(8,128)(2,1)}, bf16[2,400,704]{2,1,0:T(8,128)(2,1)}, bf16[2,400,704]{2,1,0:T(8,128)(2,1)}) custom-call(s32[2]{0:T(128)} %pad_add_fusion.1.place_ref.refs_0_, bf16[512,1600]{1,0:T(8,128)(2,1)} %get-tuple-element.216.hidden_ref, bf16[512,1600]{1,0:T(8,128)(2,1)} %bitcast.287, ...), custom_call_target="tpu_custom_call" | custom-call | flops 1 | bytes 1 | tf_op jit(solution)/shard_map/attention_weights/pallas_call | solution.py:752
  638.3 12.2 %collective-permute-done.39 = bf16[100,8,896]{2,1,0:T(8,128)(2,1)S(1)} collective-permute-done((bf16[100,8,896]{2,1,0:T(8,128)(2,1)}, bf16[100,8,896]{2,1,0:T(8,128)(2,1)S(1)}, u32[]{:S(2)}, u32[]{:S(2)}) %collective-permute-start.39) | collective-permute-done | bytes 1433632 | tf_op jit(solution)/shard_map/ppermute | solution.py:338
  658.3 21.4 %project_back.1 = (bf16[512,1600]{1,0:T(8,128)(2,1)}, f32[4,1600]{1,0:T(4,128)}) custom-call(s32[2]{0:T(128)} %pad_add_fusion.1.place_ref.refs_0_, bf16[512,1600]{1,0:T(8,128)(2,1)} %bitcast.14.tokens_ref.refs_1_, f32[512,1600]{1,0:T(8,128)} %get-tuple-element.233.refs_2_, f32[1,1600]{1,0:T(1,128)} %get-tuple-element.147.gain_ref.refs_3_, ...), custom_call_target="tpu_custom_call" | custom-call | flops 1 | bytes 1 | tf_op jit(solution)/shard_map/project_back/pallas_call | solution.py:925
  679.8 9.1 %all-to-all-done.3 = bf16[4,16,8,1600]{3,2,1,0:T(8,128)(2,1)S(1)} async-done(((bf16[4,16,8,1600]{3,2,1,0:T(8,128)(2,1)}), bf16[4,16,8,1600]{3,2,1,0:T(8,128)(2,1)S(1)}, u32[]{:S(2)}, u32[]{:S(2)}) %all-to-all-start.3) | async-done | bytes 1638432 | tf_op jit(solution)/shard_map/all_to_all | solution.py:1124
  699.7 26.2 %collective-permute-done.43 = bf16[100,8,704]{2,1,0:T(8,128)(2,1)} collective-permute-done((bf16[100,8,704]{2,1,0:T(8,128)(2,1)}, bf16[100,8,704]{2,1,0:T(8,128)(2,1)}, u32[]{:S(2)}, u32[]{:S(2)}) %collective-permute-start.43) | collective-permute-done | bytes 1126432 | tf_op jit(solution)/shard_map/ppermute | solution.py:338
  734.3 20.9 %reduce-scatter.17.cloned.1.call-done = bf16[200,896]{1,0:T(8,128)(2,1)} async-done(((bf16[800,896]{1,0:T(8,128)(2,1)}), bf16[200,896]{1,0:T(8,128)(2,1)}) %reduce-scatter.17.cloned.1.call-update) | async-done | bytes 358416 | tf_op jit(solution)/shard_map/optimization_barrier | solution.py:364
  767.8 10.2 %collective-permute-done.56 = bf16[25,8,1600]{2,1,0:T(8,128)(2,1)S(1)} collective-permute-done((bf16[25,8,1600]{2,1,0:T(8,128)(2,1)S(1)}, bf16[25,8,1600]{2,1,0:T(8,128)(2,1)S(1)}, u32[]{:S(2)}, u32[]{:S(2)}) %collective-permute-start.56) | collective-permute-done | bytes 640032 | tf_op jit(solution)/shard_map/ppermute | solution.py:338
  780.2 13.1 %collective-permute-done.52 = bf16[25,8,1600]{2,1,0:T(8,128)(2,1)S(1)} collective-permute-done((bf16[25,8,1600]{2,1,0:T(8,128)(2,1)S(1)}, bf16[25,8,1600]{2,1,0:T(8,128)(2,1)S(1)}, u32[]{:S(2)}, u32[]{:S(2)}) %collective-permute-start.52) | collective-permute-done | bytes 640032 | tf_op jit(solution)/shard_map/ppermute | solution.py:338
  808.9 5.9 merge_units.1
  816.3 11.4 %all_to_all.30 = f32[4,1,2400]{2,1,0:T(1,128)S(1)} all-to-all(f32[4,1,2400]{2,1,0:T(1,128)S(1)} %broadcast_in_dim.75), channel_id=1, replica_groups=mesh['rep'=4,'dp'=2,'ctx'=4] {'ctx'}, dimensions={0} | all-to-all | bytes 76800 | tf_op jit(solution)/shard_map/all_to_all | solution.py:1378
  845.9 5.9 concatenate.70
  (334 shorter events, 202.9 us)
Async XLA Ops:
  7.2 98.0 %all-gather.5.cloned.1.call-start = ((), (), s32[]{:S(2)}) async-start(), calls=%async_computation.10 | async-start | bytes 3328000 | tf_op jit(solution)/shard_map/all_gather | solution.py:1144
  30.4 74.9 %all-to-all-start = ((bf16[4,16,8,1600]{3,2,1,0:T(8,128)(2,1)}), bf16[4,16,8,1600]{3,2,1,0:T(8,128)(2,1)}, u32[]{:S(2)}, u32[]{:S(2)}) async-start(bf16[4,16,8,1600]{3,2,1,0:T(8,128)(2,1)} %bitcast.298), calls=%async_computation | async-start | bytes 3407872 | tf_op jit(solution)/shard_map/all_to_all | solution.py:1124
  34.8 124.7 %all-gather.7.cloned.1.call-start = ((), (), s32[]{:S(2)}) async-start(), calls=%async_computation.11 | async-start | bytes 3328000 | tf_op jit(solution)/shard_map/all_gather | solution.py:1144
  105.2 60.9 %collective-permute-start.4 = (bf16[100,8,1600]{2,1,0:T(8,128)(2,1)}, bf16[100,8,1600]{2,1,0:T(8,128)(2,1)}, u32[]{:S(2)}, u32[]{:S(2)}) collective-permute-start(bf16[100,8,1600]{2,1,0:T(8,128)(2,1)} %bitcast.264), channel_id=1, source_target_pairs={{0,4},{4,0},{1,5},{5,1},{2,6},{6,2},{3,7},{7,3},{8,12},{12,8},{9,1... | collective-permute-start | bytes 7680008 | tf_op jit(solution)/shard_map/ppermute | solution.py:338
  106.7 59.7 %collective-permute-start.5 = (bf16[100,8,1600]{2,1,0:T(8,128)(2,1)}, bf16[100,8,1600]{2,1,0:T(8,128)(2,1)}, u32[]{:S(2)}, u32[]{:S(2)}) collective-permute-start(bf16[100,8,1600]{2,1,0:T(8,128)(2,1)} %bitcast.265), channel_id=1, source_target_pairs={{0,16},{16,0},{8,24},{24,8},{1,17},{17,1},{9,25},{25,9},{2,18},{18... | collective-permute-start | bytes 7680008 | tf_op jit(solution)/shard_map/ppermute | solution.py:338
  159.5 85.2 %collective-permute-start.9 = (bf16[100,8,1600]{2,1,0:T(8,128)(2,1)}, bf16[100,8,1600]{2,1,0:T(8,128)(2,1)}, u32[]{:S(2)}, u32[]{:S(2)}) collective-permute-start(bf16[100,8,1600]{2,1,0:T(8,128)(2,1)} %bitcast.282), channel_id=1, source_target_pairs={{0,4},{4,0},{1,5},{5,1},{2,6},{6,2},{3,7},{7,3},{8,12},{12,8},{9,1... | collective-permute-start | bytes 7680008 | tf_op jit(solution)/shard_map/ppermute | solution.py:338
  166.5 78.2 %collective-permute-start.8 = (bf16[100,8,1600]{2,1,0:T(8,128)(2,1)}, bf16[100,8,1600]{2,1,0:T(8,128)(2,1)}, u32[]{:S(2)}, u32[]{:S(2)}) collective-permute-start(bf16[100,8,1600]{2,1,0:T(8,128)(2,1)} %bitcast.27), channel_id=1, source_target_pairs={{0,16},{16,0},{8,24},{24,8},{1,17},{17,1},{9,25},{25,9},{2,18},{18... | collective-permute-start | bytes 7680008 | tf_op jit(solution)/shard_map/ppermute | solution.py:338
  167.9 76.7 %all-to-all-start.2 = ((bf16[4,16,8,1600]{3,2,1,0:T(8,128)(2,1)}), bf16[4,16,8,1600]{3,2,1,0:T(8,128)(2,1)}, u32[]{:S(2)}, u32[]{:S(2)}) async-start(bf16[4,16,8,1600]{3,2,1,0:T(8,128)(2,1)} %bitcast.299), calls=%async_computation.2 | async-start | bytes 3407872 | tf_op jit(solution)/shard_map/all_to_all | solution.py:1124
  172.3 81.9 %all-gather.9.cloned.1.call-start = ((), (), s32[]{:S(2)}) async-start(), calls=%async_computation.13 | async-start | bytes 3328000 | tf_op jit(solution)/shard_map/all_gather | solution.py:1144
  173.3 553.8 %reduce-scatter.13.cloned.1.call-start = ((), (), s32[]{:S(2)}) async-start(), calls=%async_computation.14 | async-start | bytes 3328000
  173.5 81.9 %collective-permute-start.6 = (bf16[100,8,1600]{2,1,0:T(8,128)(2,1)}, bf16[100,8,1600]{2,1,0:T(8,128)(2,1)S(1)}, u32[]{:S(2)}, u32[]{:S(2)}) collective-permute-start(bf16[100,8,1600]{2,1,0:T(8,128)(2,1)} %bitcast.266), channel_id=1, source_target_pairs={{0,8},{8,0},{16,24},{24,16},{1,9},{9,1},{17,25},{25,17},{2,10},{10... | collective-permute-start | bytes 7680008 | tf_op jit(solution)/shard_map/ppermute | solution.py:338
  173.6 81.8 %collective-permute-start.7 = (bf16[100,8,1600]{2,1,0:T(8,128)(2,1)}, bf16[100,8,1600]{2,1,0:T(8,128)(2,1)}, u32[]{:S(2)}, u32[]{:S(2)}) collective-permute-start(bf16[100,8,1600]{2,1,0:T(8,128)(2,1)} %bitcast.27), channel_id=1, source_target_pairs={{0,8},{8,0},{16,24},{24,16},{1,9},{9,1},{17,25},{25,17},{2,10},{10... | collective-permute-start | bytes 7680008 | tf_op jit(solution)/shard_map/ppermute | solution.py:338
  174.1 81.4 %collective-permute-start.10 = (bf16[100,8,1600]{2,1,0:T(8,128)(2,1)}, bf16[100,8,1600]{2,1,0:T(8,128)(2,1)}, u32[]{:S(2)}, u32[]{:S(2)}) collective-permute-start(bf16[100,8,1600]{2,1,0:T(8,128)(2,1)} %bitcast.33), channel_id=1, source_target_pairs={{0,8},{8,0},{16,24},{24,16},{1,9},{9,1},{17,25},{25,17},{2,10},{10... | collective-permute-start | bytes 7680008 | tf_op jit(solution)/shard_map/ppermute | solution.py:338
  254.3 63.4 %collective-permute-start.15 = (bf16[100,8,1600]{2,1,0:T(8,128)(2,1)}, bf16[100,8,1600]{2,1,0:T(8,128)(2,1)}, u32[]{:S(2)}, u32[]{:S(2)}) collective-permute-start(bf16[100,8,1600]{2,1,0:T(8,128)(2,1)} %bitcast.283), channel_id=1, source_target_pairs={{0,4},{4,0},{1,5},{5,1},{2,6},{6,2},{3,7},{7,3},{8,12},{12,8},{9,1... | collective-permute-start | bytes 7680008 | tf_op jit(solution)/shard_map/ppermute | solution.py:338
  273.9 43.7 %collective-permute-start.14 = (bf16[64,8,1600]{2,1,0:T(8,128)(2,1)}, bf16[64,8,1600]{2,1,0:T(8,128)(2,1)S(1)}, u32[]{:S(2)}, u32[]{:S(2)}) collective-permute-start(bf16[64,8,1600]{2,1,0:T(8,128)(2,1)} %bitcast.43), channel_id=1, source_target_pairs={{0,16},{16,0},{8,24},{24,8},{1,17},{17,1},{9,25},{25,9},{2,18},{18... | collective-permute-start | bytes 4915208 | tf_op jit(solution)/shard_map/ppermute | solution.py:338
  331.1 43.7 %collective-permute-start.19 = (bf16[64,8,1600]{2,1,0:T(8,128)(2,1)}, bf16[64,8,1600]{2,1,0:T(8,128)(2,1)S(1)}, u32[]{:S(2)}, u32[]{:S(2)}) collective-permute-start(bf16[64,8,1600]{2,1,0:T(8,128)(2,1)} %bitcast.301), channel_id=1, source_target_pairs={{0,16},{16,0},{8,24},{24,8},{1,17},{17,1},{9,25},{25,9},{2,18},{18... | collective-permute-start | bytes 4915208 | tf_op jit(solution)/shard_map/ppermute | solution.py:338
  429.6 39.6 %collective-permute-start.24 = (bf16[64,8,1600]{2,1,0:T(8,128)(2,1)}, bf16[64,8,1600]{2,1,0:T(8,128)(2,1)}, u32[]{:S(2)}, u32[]{:S(2)}) collective-permute-start(bf16[64,8,1600]{2,1,0:T(8,128)(2,1)} %bitcast.321), channel_id=1, source_target_pairs={{0,16},{16,0},{8,24},{24,8},{1,17},{17,1},{9,25},{25,9},{2,18},{18... | collective-permute-start | bytes 4915208 | tf_op jit(solution)/shard_map/ppermute | solution.py:338
  469.1 63.3 %collective-permute-start.27 = (bf16[100,8,1600]{2,1,0:T(8,128)(2,1)}, bf16[100,8,1600]{2,1,0:T(8,128)(2,1)S(1)}, u32[]{:S(2)}, u32[]{:S(2)}) collective-permute-start(bf16[100,8,1600]{2,1,0:T(8,128)(2,1)} %bitcast.355), channel_id=1, source_target_pairs={{0,4},{4,0},{1,5},{5,1},{2,6},{6,2},{3,7},{7,3},{8,12},{12,8},{9,1... | collective-permute-start | bytes 7680008 | tf_op jit(solution)/shard_map/ppermute | solution.py:338
  470.6 40.1 %collective-permute-start.26 = (bf16[64,8,1600]{2,1,0:T(8,128)(2,1)S(1)}, bf16[64,8,1600]{2,1,0:T(8,128)(2,1)S(1)}, u32[]{:S(2)}, u32[]{:S(2)}) collective-permute-start(bf16[64,8,1600]{2,1,0:T(8,128)(2,1)S(1)} %bitcast.320), channel_id=1, source_target_pairs={{0,16},{16,0},{8,24},{24,8},{1,17},{17,1},{9,25},{25,9},{2,18},{18... | collective-permute-start | bytes 4915208 | tf_op jit(solution)/shard_map/ppermute | solution.py:338
  538.7 188.4 %reduce-scatter.15.cloned.1.call-start = ((), (), s32[]{:S(2)}) async-start(), calls=%async_computation.15 | async-start | bytes 3328000
  538.7 58.7 %collective-permute-start.34 = (bf16[100,8,1600]{2,1,0:T(8,128)(2,1)}, bf16[100,8,1600]{2,1,0:T(8,128)(2,1)}, u32[]{:S(2)}, u32[]{:S(2)}) collective-permute-start(bf16[100,8,1600]{2,1,0:T(8,128)(2,1)} %bitcast.354), channel_id=1, source_target_pairs={{0,4},{4,0},{1,5},{5,1},{2,6},{6,2},{3,7},{7,3},{8,12},{12,8},{9,1... | collective-permute-start | bytes 7680008 | tf_op jit(solution)/shard_map/ppermute | solution.py:338
  612.6 76.2 %all-to-all-start.3 = ((bf16[4,16,8,1600]{3,2,1,0:T(8,128)(2,1)}), bf16[4,16,8,1600]{3,2,1,0:T(8,128)(2,1)S(1)}, u32[]{:S(2)}, u32[]{:S(2)}) async-start(bf16[4,16,8,1600]{3,2,1,0:T(8,128)(2,1)} %bitcast.297), calls=%async_computation.3 | async-start | bytes 3407872 | tf_op jit(solution)/shard_map/all_to_all | solution.py:1124
  616.4 138.8 %reduce-scatter.17.cloned.1.call-start = ((), (), s32[]{:S(2)}) async-start(), calls=%async_computation.16 | async-start | bytes 1792000
  616.7 33.9 %collective-permute-start.39 = (bf16[100,8,896]{2,1,0:T(8,128)(2,1)}, bf16[100,8,896]{2,1,0:T(8,128)(2,1)S(1)}, u32[]{:S(2)}, u32[]{:S(2)}) collective-permute-start(bf16[100,8,896]{2,1,0:T(8,128)(2,1)} %bitcast.362), channel_id=1, source_target_pairs={{0,16},{16,0},{8,24},{24,8},{1,17},{17,1},{9,25},{25,9},{2,18},{18... | collective-permute-start | bytes 4300808 | tf_op jit(solution)/shard_map/ppermute | solution.py:338
  618.2 33.7 %collective-permute-start.40 = (bf16[100,8,896]{2,1,0:T(8,128)(2,1)}, bf16[100,8,896]{2,1,0:T(8,128)(2,1)}, u32[]{:S(2)}, u32[]{:S(2)}) collective-permute-start(bf16[100,8,896]{2,1,0:T(8,128)(2,1)} %bitcast.361), channel_id=1, source_target_pairs={{0,4},{4,0},{1,5},{5,1},{2,6},{6,2},{3,7},{7,3},{8,12},{12,8},{9,1... | collective-permute-start | bytes 4300808 | tf_op jit(solution)/shard_map/ppermute | solution.py:338
  692.0 67.9 %all-to-all-start.4 = ((bf16[4,16,8,1600]{3,2,1,0:T(8,128)(2,1)}), bf16[4,16,8,1600]{3,2,1,0:T(8,128)(2,1)}, u32[]{:S(2)}, u32[]{:S(2)}) async-start(bf16[4,16,8,1600]{3,2,1,0:T(8,128)(2,1)} %bitcast.324), calls=%async_computation.4 | async-start | bytes 3407872 | tf_op jit(solution)/shard_map/all_to_all | solution.py:1124
  696.4 118.4 %reduce-scatter.11.cloned.1.call-start = ((), (), s32[]{:S(2)}) async-start(), calls=%async_computation.12 | async-start | bytes 1536000 | tf_op jit(solution)/shard_map/reduce_scatter | solution.py:1258
  696.5 29.4 %collective-permute-start.43 = (bf16[100,8,704]{2,1,0:T(8,128)(2,1)}, bf16[100,8,704]{2,1,0:T(8,128)(2,1)}, u32[]{:S(2)}, u32[]{:S(2)}) collective-permute-start(bf16[100,8,704]{2,1,0:T(8,128)(2,1)} %bitcast.364), channel_id=1, source_target_pairs={{0,16},{16,0},{8,24},{24,8},{1,17},{17,1},{9,25},{25,9},{2,18},{18... | collective-permute-start | bytes 3379208 | tf_op jit(solution)/shard_map/ppermute | solution.py:338
  698.0 29.1 %collective-permute-start.44 = (bf16[100,8,704]{2,1,0:T(8,128)(2,1)}, bf16[100,8,704]{2,1,0:T(8,128)(2,1)}, u32[]{:S(2)}, u32[]{:S(2)}) collective-permute-start(bf16[100,8,704]{2,1,0:T(8,128)(2,1)} %bitcast.363), channel_id=1, source_target_pairs={{0,4},{4,0},{1,5},{5,1},{2,6},{6,2},{3,7},{7,3},{8,12},{12,8},{9,1... | collective-permute-start | bytes 3379208 | tf_op jit(solution)/shard_map/ppermute | solution.py:338
  763.9 33.7 %collective-permute-start.48 = (bf16[32,8,1600]{2,1,0:T(8,128)(2,1)}, bf16[32,8,1600]{2,1,0:T(8,128)(2,1)}, u32[]{:S(2)}, u32[]{:S(2)}) collective-permute-start(bf16[32,8,1600]{2,1,0:T(8,128)(2,1)} %bitcast.116), channel_id=1, source_target_pairs={{0,8},{8,0},{16,24},{24,16},{1,9},{9,1},{17,25},{25,17},{2,10},{10... | collective-permute-start | bytes 2457608 | tf_op jit(solution)/shard_map/ppermute | solution.py:338
  764.2 31.7 %collective-permute-start.50 = (f32[1,8,2400]{2,1,0:T(8,128)S(1)}, f32[1,8,2400]{2,1,0:T(8,128)S(1)}, u32[]{:S(2)}, u32[]{:S(2)}) collective-permute-start(f32[1,8,2400]{2,1,0:T(8,128)S(1)} %fusion.16), channel_id=1, source_target_pairs={{0,16},{16,0},{8,24},{24,8},{1,17},{17,1},{9,25},{25,9},{2,18},{18... | collective-permute-start | bytes 230408 | tf_op jit(solution)/shard_map/ppermute | solution.py:338
  766.4 26.9 %collective-permute-start.52 = (bf16[25,8,1600]{2,1,0:T(8,128)(2,1)S(1)}, bf16[25,8,1600]{2,1,0:T(8,128)(2,1)S(1)}, u32[]{:S(2)}, u32[]{:S(2)}) collective-permute-start(bf16[25,8,1600]{2,1,0:T(8,128)(2,1)S(1)} %bitcast.344), channel_id=1, source_target_pairs={{0,16},{16,0},{8,24},{24,8},{1,17},{17,1},{9,25},{25,9},{2,18},{18... | collective-permute-start | bytes 1920008 | tf_op jit(solution)/shard_map/ppermute | solution.py:338
  (90 other events, 842.7 us)
Sparse Core Ops, SparseCore 0:
  10.3 92.6 all-gather.4
  105.1 54.3 all-gather.6
  175.3 78.9 all-gather.8
  538.8 50.5 reduce-scatter.12
  602.3 76.5 reduce-scatter.14
  692.2 62.9 reduce-scatter.16
  759.3 33.0 reduce-scatter.10
